TPU v7x, 128 devices: a whole 4x4x4 slice. The times are simulated.
128 devices in a mesh: row: 16 (over z_hi, x, core), col: 8 (over y, z_lo).
Axes of the slice: x: 4, y: 4, z: 4 (z_hi: 2, z_lo: 2; z = z_hi * 2 + z_lo), core: 2. Of those that a mesh axis runs over, the one named last changes fastest.
Arguments:
- before_scan: float32 [4, 4096, 8192], P(None, 'row', 'col'), may hold values from -40 to 40
- after_scan: float32 [4, 4096, 8192], P(None, 'row', 'col'), may hold values from -40 to 40
- drift_offsets: int32 [2, 4, 16, 8], P(None, None, 'row', 'col'), may hold values from -128 to 128, as said below
- drift_fractions: int32 [2, 4, 16, 8], P(None, None, 'row', 'col'), may hold values from 0 to 255
Outputs:
- band_field: float32 [4, 4096, 8192], P(None, 'row', 'col')
- slope_field: float32 [4, 4096, 8192], P(None, 'row', 'col')
- surface_params: float32 [2, 4], replicated
Inputs may be any that keep to these rules, and one draw needn't show every extreme that they name: `drift_offsets`: for every scan and tile, the cells a tile reads (its own cells shifted by its offsets, widened by one row and column before and two after) lie inside the window. In every scan the first tile has offsets 128, 128 and the last tile minus 128, minus 128.
All inputs are finite; a program needn't handle non-finite values.
Results may differ from a plain program's by a relative error of at most 0.00014.
Values sent between devices are 32-bit elements; how exact they have to be, the bound alone decides.
No kernel may reach another device: no remote copies, remote signals or barrier semaphores. Data moves between devices by JAX's collectives and lax.ppermute only.
A program may use at most 128 MiB of HBM per device.

v0:
```python
import math

import jax
import jax.numpy as jnp
from jax import lax
from jax.sharding import PartitionSpec as P

LS = 5
SR = 4
LCUT = 1600
BLOCK = 16
DRIFT = 128


ALPHA = math.sqrt(math.log(2.0) / math.pi)
SPACING = 0.5
EPSILON = 1e-06
HIGHEST = lax.Precision.HIGHEST


def with_halo(value, sides, width):
    for axis, dim in sides:
        count, length = (lax.axis_size(axis), value.shape[dim])
        up = [(i, (i + 1) % count) for i in range(count - 1)]
        down = [(j, i) for i, j in up]
        last = lax.slice_in_dim(value, length - width, length, axis=dim)
        leading = lax.slice_in_dim(value, 0, width, axis=dim)
        before = lax.ppermute(last, axis, up)
        after = lax.ppermute(leading, axis, down)
        value = jnp.concatenate([before, value, after], axis=dim)
    return value


def cubic_weights(fraction):
    position = fraction.astype(jnp.float32) / 256.0
    square = position * position
    cube_term = square * position
    return (
        0.5 * (2.0 * square - cube_term - position),
        0.5 * (3.0 * cube_term - 5.0 * square + 2.0),
        0.5 * (4.0 * square - 3.0 * cube_term + position),
        0.5 * (cube_term - square),
    )


def interpolate(window, row_taps, col_taps):
    height = window.shape[0] - 3
    length = window.shape[1] - 3
    across = (
        row_taps[0] * window[0:height]
        + row_taps[1] * window[1 : height + 1]
        + row_taps[2] * window[2 : height + 2]
        + row_taps[3] * window[3 : height + 3]
    )
    return (
        col_taps[0] * across[:, 0:length]
        + col_taps[1] * across[:, 1 : length + 1]
        + col_taps[2] * across[:, 2 : length + 2]
        + col_taps[3] * across[:, 3 : length + 3]
    )


def resample(after_scan, drift_offsets, drift_fractions):
    height, length = (after_scan.shape[1], after_scan.shape[2])
    margin = DRIFT + 2
    widened = with_halo(after_scan, (("row", 1), ("col", 2)), margin)
    row_taps = jnp.stack(cubic_weights(drift_fractions[0, :, 0, 0]), axis=-1)
    col_taps = jnp.stack(cubic_weights(drift_fractions[1, :, 0, 0]), axis=-1)

    def one_scan(window, row_shift, col_shift, row_weights, col_weights):
        source = lax.dynamic_slice(
            window, (margin - 1 + row_shift, margin - 1 + col_shift), (height + 3, length + 3)
        )
        return interpolate(source, row_weights, col_weights)

    return jax.vmap(one_scan)(
        widened, drift_offsets[0, :, 0, 0], drift_offsets[1, :, 0, 0], row_taps, col_taps
    )


def short_taps():
    return [math.exp(-math.pi * (offset / (ALPHA * LS)) ** 2) for offset in range(-SR, SR + 1)]


def short_filter(widened, height, length):
    kernel_taps = short_taps()
    column_index = (
        lax.axis_index("col") * length - SR + jnp.arange(length + 2 * SR, dtype=jnp.int32)
    )
    column_inside = ((column_index >= 0) & (column_index < length * lax.axis_size("col"))).astype(
        jnp.float32
    )
    summed = kernel_taps[0] * widened[:, :, 0:length]
    weight = kernel_taps[0] * column_inside[0:length]
    for offset in range(1, 2 * SR + 1):
        summed = summed + kernel_taps[offset] * widened[:, :, offset : offset + length]
        weight = weight + kernel_taps[offset] * column_inside[offset : offset + length]
    across = summed / weight
    row_index = lax.axis_index("row") * height - SR + jnp.arange(height + 2 * SR, dtype=jnp.int32)
    row_inside = ((row_index >= 0) & (row_index < height * lax.axis_size("row"))).astype(
        jnp.float32
    )
    summed = kernel_taps[0] * across[:, 0:height, :]
    weight = kernel_taps[0] * row_inside[0:height]
    for offset in range(1, 2 * SR + 1):
        summed = summed + kernel_taps[offset] * across[:, offset : offset + height, :]
        weight = weight + kernel_taps[offset] * row_inside[offset : offset + height]
    return summed / weight[:, None]


def coarse_means(surface):
    scans, height, length = surface.shape
    return surface.reshape(scans, height // BLOCK, BLOCK, length // BLOCK, BLOCK).mean(axis=(2, 4))


def gauss_block(source, target):
    distance = ((source[:, None] - target[None, :]) * BLOCK).astype(jnp.float32) / (ALPHA * LCUT)
    return jnp.exp(-math.pi * distance * distance)


def long_cols(coarse):
    width = coarse.shape[2]
    target = lax.axis_index("col") * width + jnp.arange(width, dtype=jnp.int32)
    portion = lax.all_gather(coarse, "col", axis=2, tiled=True)
    source = jnp.arange(portion.shape[2], dtype=jnp.int32)
    matrix = gauss_block(source, target)
    summed = jnp.einsum("frk,kc->frc", portion, matrix, precision=HIGHEST)
    weight = jnp.sum(matrix, axis=0)
    return summed / weight


def long_rows(surface):
    rows_here = surface.shape[1]
    target = lax.axis_index("row") * rows_here + jnp.arange(rows_here, dtype=jnp.int32)
    portion = lax.all_gather(surface, "row", axis=1, tiled=True)
    source = jnp.arange(portion.shape[1], dtype=jnp.int32)
    matrix = gauss_block(target, source)
    summed = jnp.einsum("rk,fkc->frc", matrix, portion, precision=HIGHEST)
    weight = jnp.sum(matrix, axis=1)
    return summed / weight[:, None]


def upsample_matrix(fine_index, coarse_index, coarse_count):
    numerator = 2 * fine_index + 1 - BLOCK
    lower_index = numerator // (2 * BLOCK)
    fraction = (numerator - lower_index * (2 * BLOCK)).astype(jnp.float32) / (2.0 * BLOCK)
    outside = (lower_index < 0) | (lower_index >= coarse_count - 1)
    fraction = jnp.where(outside, jnp.zeros_like(fraction), fraction)
    lower_index = jnp.clip(lower_index, 0, coarse_count - 1)
    first_part = (coarse_index[None, :] == lower_index[:, None]).astype(jnp.float32) * (
        1.0 - fraction
    )[:, None]
    second_part = (coarse_index[None, :] == (lower_index + 1)[:, None]).astype(
        jnp.float32
    ) * fraction[:, None]
    return first_part + second_part


def upsample(wavy_coarse, height, length):
    coarse_rows, coarse_cols = (wavy_coarse.shape[1], wavy_coarse.shape[2])
    widened_coarse = with_halo(wavy_coarse, (("row", 1), ("col", 2)), 1)
    row_fine = lax.axis_index("row") * height + jnp.arange(height, dtype=jnp.int32)
    row_blocks = (
        lax.axis_index("row") * coarse_rows - 1 + jnp.arange(coarse_rows + 2, dtype=jnp.int32)
    )
    col_fine = lax.axis_index("col") * length + jnp.arange(length, dtype=jnp.int32)
    col_blocks = (
        lax.axis_index("col") * coarse_cols - 1 + jnp.arange(coarse_cols + 2, dtype=jnp.int32)
    )
    row_up = upsample_matrix(row_fine, row_blocks, coarse_rows * lax.axis_size("row"))
    col_up = upsample_matrix(col_fine, col_blocks, coarse_cols * lax.axis_size("col"))
    row_mixed = jnp.einsum("pa,sab->spb", row_up, widened_coarse, precision=HIGHEST)
    return jnp.einsum("spb,qb->spq", row_mixed, col_up, precision=HIGHEST)


def slopes(surface):
    height, length = (surface.shape[1], surface.shape[2])
    bordered = with_halo(surface, (("row", 1), ("col", 2)), 1)
    column_index = lax.axis_index("col") * length + jnp.arange(length, dtype=jnp.int32)
    row_index = lax.axis_index("row") * height + jnp.arange(height, dtype=jnp.int32)
    column_mask = (
        (column_index >= 1) & (column_index <= length * lax.axis_size("col") - 2)
    ).astype(jnp.float32)
    row_mask = ((row_index >= 1) & (row_index <= height * lax.axis_size("row") - 2)).astype(
        jnp.float32
    )
    along_cols = (bordered[:, 1:-1, 2:] - bordered[:, 1:-1, :-2]) / (2.0 * SPACING) * column_mask
    along_rows = (
        (bordered[:, 2:, 1:-1] - bordered[:, :-2, 1:-1]) / (2.0 * SPACING) * row_mask[:, None]
    )
    return along_cols * along_cols + along_rows * along_rows


def body(before_scan, after_scan, drift_offsets, drift_fractions):
    height, length = (before_scan.shape[1], before_scan.shape[2])
    shifted = resample(after_scan, drift_offsets, drift_fractions)
    difference = before_scan - shifted
    widened = with_halo(difference, (("row", 1), ("col", 2)), SR)
    smooth = short_filter(widened, height, length)
    coarse = coarse_means(smooth)
    wavy_coarse = long_rows(long_cols(coarse))
    waviness = upsample(wavy_coarse, height, length)
    band_field = smooth - waviness
    slope_field = slopes(band_field)
    height_sq = jnp.sum(band_field * band_field, axis=(1, 2))
    slope_sum = jnp.sum(slope_field, axis=(1, 2))
    height_all, slope_all = lax.psum((height_sq, slope_sum), ("row", "col"))
    total_cells = height * lax.axis_size("row") * length * lax.axis_size("col")
    surface_params = jnp.sqrt(jnp.stack([height_all, slope_all]) / total_cells + EPSILON)
    return (band_field, slope_field, surface_params)


def solution(mesh):
    in_specs = (
        P(None, "row", "col"),
        P(None, "row", "col"),
        P(None, None, "row", "col"),
        P(None, None, "row", "col"),
    )
    out_specs = (P(None, "row", "col"), P(None, "row", "col"), P())
    return jax.shard_map(body, mesh=mesh, in_specs=in_specs, out_specs=out_specs, check_vma=False)
```

profile of v0, /device:TPU:1, one launch (start us, length us, event | category | flops | bytes accessed | tf_op | source)
XLA Modules:
  0.0 455.7 jit_solution(10664465496469987918)
XLA Ops:
  0.6 3.2 fusion.118
  5.3 4.5 collective-permute-start
  9.8 2.7 copy.43
  12.5 2.0 collective-permute-start.1
  14.5 5.2 %copy.28 = f32[4,256,1024]{1,0,2:T(4,128)} copy(f32[4,256,1024]{2,1,0:T(8,128)} %param.5) | data formatting | bytes 8388608 | tf_op args[1]
  19.9 13.1 %collective-permute-done = f32[4,130,1024]{2,0,1:T(4,128)} collective-permute-done((f32[4,130,1024]{2,0,1:T(4,128)S(1)}, f32[4,130,1024]{2,0,1:T(4,128)}, u32[]{:S(2)}, u32[]{:S(2)}) %collective-permute-start) | collective-permute-done | bytes 2129952 | tf_op jit(solution)/shard_map/ppermute | solution.py:28
  33.1 6.2 %copy.27 = f32[4,130,1024]{1,0,2:T(4,128)} copy(f32[4,130,1024]{2,0,1:T(4,128)} %collective-permute-done) | data formatting | bytes 4259840 | tf_op jit(solution)/shard_map/ppermute | solution.py:28
  40.6 6.2 %copy.29 = f32[4,130,1024]{1,0,2:T(4,128)} copy(f32[4,130,1024]{2,0,1:T(4,128)} %collective-permute-done.1) | data formatting | bytes 4259840 | tf_op jit(solution)/shard_map/ppermute | solution.py:29
  46.8 3.5 pad_maximum_fusion.13
  50.3 3.8 collective-permute-start.2
  54.1 1.5 collective-permute-start.3
  56.2 40.7 %collective-permute-done.2 = f32[4,516,130]{1,0,2:T(4,128)S(1)} collective-permute-done((f32[4,516,130]{1,0,2:T(4,128)S(1)}, f32[4,516,130]{1,0,2:T(4,128)S(1)}, u32[]{:S(2)}, u32[]{:S(2)}) %collective-permute-start.2) | collective-permute-done | bytes 1073312 | tf_op jit(solution)/shard_map/ppermute | solution.py:28
  97.0 29.5 %pad_maximum_fusion = f32[4,516,1284]{1,0,2:T(4,128)} fusion(f32[4,516,130]{1,0,2:T(4,128)S(1)} %collective-permute-done.3, f32[4,130,1024]{1,0,2:T(4,128)} %copy.29, f32[4,256,1024]{1,0,2:T(4,128)S(1)} %copy-done.2, f32[4,130,1024]{1,0,2:T(4,128)} %copy.27, f32[4,516,130]{1,0,2:T(4,128)S(1)} %collective-permute-done.2), kind=kLoop, calls=%fused_computation.2 | loop fusion | flops 10600704 | bytes 21201408 | tf_op jit(solution)/shard_map/concatenate | solution.py:30
  126.4 15.3 %copy.30 = f32[4,516,1284]{2,1,0:T(8,128)} copy(f32[4,516,1284]{1,0,2:T(4,128)} %pad_maximum_fusion) | data formatting | bytes 21201408
  141.7 21.6 %while.1 = (s32[]{:T(128)}, f32[4,516,1284]{2,1,0:T(8,128)}, s32[4,3]{1,0:T(4,128)S(1)}, f32[4,259,1027]{2,1,0:T(8,128)}, s32[]{:T(128)}) while((s32[]{:T(128)}, f32[4,516,1284]{2,1,0:T(8,128)}, s32[4,3]{1,0:T(4,128)S(1)}, f32[4,259,1027]{2,1,0:T(8,128)}, s32[]{:T(128)}) %tuple.51), condition=%wide.while_cond, body=%wide.while_body.sunk | while | flops 2 | bytes 2435185 | solution.py:71
  142.3 4.8 %dynamic-slice_dynamic-update-slice_fusion.2 = f32[4,259,1027]{2,1,0:T(8,128)} fusion(f32[4,259,1027]{2,1,0:T(8,128)} %get-tuple-element.118, s32[]{:T(128)} %get-tuple-element.115, f32[4,516,1284]{2,1,0:T(8,128)} %get-tuple-element.121, s32[]{:T(128)} %bitcast.84, s32[]{:T(128)} %bitcast.85, s32[]{:T(128)} %bitcast.86), kind=kLoop, calls=%fused_computation.clone.1 | loop fusion | bytes 2435072 | tf_op jit(solution)/shard_map/vmap()/gather
  147.8 4.7 %dynamic-slice_dynamic-update-slice_fusion.2 = f32[4,259,1027]{2,1,0:T(8,128)} fusion(f32[4,259,1027]{2,1,0:T(8,128)} %get-tuple-element.118, s32[]{:T(128)} %get-tuple-element.115, f32[4,516,1284]{2,1,0:T(8,128)} %get-tuple-element.121, s32[]{:T(128)} %bitcast.84, s32[]{:T(128)} %bitcast.85, s32[]{:T(128)} %bitcast.86), kind=kLoop, calls=%fused_computation.clone.1 | loop fusion | bytes 2435072 | tf_op jit(solution)/shard_map/vmap()/gather
  153.1 4.7 %dynamic-slice_dynamic-update-slice_fusion.2 = f32[4,259,1027]{2,1,0:T(8,128)} fusion(f32[4,259,1027]{2,1,0:T(8,128)} %get-tuple-element.118, s32[]{:T(128)} %get-tuple-element.115, f32[4,516,1284]{2,1,0:T(8,128)} %get-tuple-element.121, s32[]{:T(128)} %bitcast.84, s32[]{:T(128)} %bitcast.85, s32[]{:T(128)} %bitcast.86), kind=kLoop, calls=%fused_computation.clone.1 | loop fusion | bytes 2435072 | tf_op jit(solution)/shard_map/vmap()/gather
  158.5 4.7 %dynamic-slice_dynamic-update-slice_fusion.2 = f32[4,259,1027]{2,1,0:T(8,128)} fusion(f32[4,259,1027]{2,1,0:T(8,128)} %get-tuple-element.118, s32[]{:T(128)} %get-tuple-element.115, f32[4,516,1284]{2,1,0:T(8,128)} %get-tuple-element.121, s32[]{:T(128)} %bitcast.84, s32[]{:T(128)} %bitcast.85, s32[]{:T(128)} %bitcast.86), kind=kLoop, calls=%fused_computation.clone.1 | loop fusion | bytes 2435072 | tf_op jit(solution)/shard_map/vmap()/gather
  163.2 9.2 %multiply_add_fusion = f32[4,256,1027]{2,1,0:T(8,128)S(1)} fusion(f32[4,259,1027]{2,1,0:T(8,128)} %get-tuple-element.10, f32[4]{0:T(128)S(1)} %get-tuple-element.67, f32[4]{0:T(128)S(1)} %get-tuple-element.62, f32[4]{0:T(128)S(1)} %get-tuple-element.64, f32[4]{0:T(128)S(1)} %get-tuple-element.63), kind=kLoop, calls=%fused_computation.5 | loop fusion | flops 7361536 | bytes 21033024 | tf_op jit(solution)/shard_map/vmap()/add | solution.py:50
  172.5 3.4 fusion.25
  176.0 17.8 %collective-permute-start.4 = (f32[4,4,1024]{2,1,0:T(4,128)S(1)}, f32[4,4,1024]{2,1,0:T(4,128)S(1)}, u32[]{:S(2)}, u32[]{:S(2)}) collective-permute-start(f32[4,4,1024]{2,1,0:T(4,128)S(1)} %get-tuple-element.53), channel_id=1, source_target_pairs={{0,8},{8,16},{16,24},{24,32},{32,40},{40,48},{48,56},{56,64},{64,7... | collective-permute-start | bytes 196616 | tf_op jit(solution)/shard_map/ppermute | solution.py:28
  193.8 1.9 collective-permute-start.5
  195.8 3.6 collective-permute-done.5
  200.4 4.1 collective-permute-start.6
  204.8 1.5 collective-permute-start.7
  206.6 3.0 collective-permute-done.7
  209.9 7.4 %maximum_maximum_fusion = (f32[4,264,1028]{2,1,0:T(8,128)S(1)}, f32[4,264,1028]{2,1,0:T(8,128)}) fusion(f32[4,4,1024]{2,1,0:T(4,128)S(1)} %collective-permute-done.5, f32[4,256,1024]{2,1,0:T(8,128)} %copy-done, f32[4,4,1024]{2,1,0:T(4,128)S(1)} %collective-permute-done.4, f32[4,264,4]{2,1,0:T(8,128)S(1)} %copy.33, f32[4,264,4]{2,1,0:T(8,128)S(1)} %copy.35), kind=kLoop, calls=%fused_computation.3 | loop fusion | flops 6513408 | bytes 13043712 | tf_op jit(solution)/shard_map/concatenate | solution.py:30
  217.3 15.3 %fusion.1 = f32[4,264,1024]{2,1,0:T(8,128)S(1)} fusion(f32[4,264,1028]{2,1,0:T(8,128)} %get-tuple-element.45, f32[4,264,1028]{2,1,0:T(8,128)S(1)} %get-tuple-element.44, f32[1024]{0:T(1024)S(1)} %fusion.80, f32[4,4,1024]{2,1,0:T(4,128)S(1)} %collective-permute-done.5, f32[4,256,1024]{2,1,0:T(8,128)} %copy-done, f32[4,4,1024]{2,1,0:T(4,128)S(1)} %collective-permute-done.4), kind=kLoop, calls=%fused_computation.8 | loop fusion | flops 20545536 | bytes 43257856 | tf_op jit(solution)/shard_map/div | solution.py:98
  232.7 5.7 %fusion.17 = f32[4,256,1024]{2,1,0:T(8,128)} fusion(f32[4,264,1024]{2,1,0:T(8,128)S(1)} %fusion.1, f32[256]{0:T(256)S(1)} %multiply_add_fusion.3), kind=kLoop, calls=%fused_computation.41 | loop fusion | flops 17825792 | bytes 41944064 | tf_op jit(solution)/shard_map/div | solution.py:108
  238.3 19.0 %reshape.249 = f32[4,16,16,64,16]{4,3,2,1,0:T(8,128)} reshape(f32[4,256,1024]{2,1,0:T(8,128)} %fusion.17) | data formatting | bytes 8388608 | tf_op jit(solution)/shard_map/reshape | solution.py:113
  257.3 12.2 %reduce_sum.45 = f32[4,16,64]{2,1,0:T(8,128)S(1)} reduce(f32[4,16,16,64,16]{4,3,2,1,0:T(8,128)} %reshape.249, f32[]{:T(128)} %constant.64.clone.1), dimensions={2,4}, to_apply=%region_0.0 | reduce | flops 1044480 | bytes 4210692 | tf_op jit(solution)/shard_map/reduce_sum | solution.py:113
  269.6 27.9 %all_gather.6 = f32[4,16,512]{1,0,2:T(4,128)S(1)} all-gather(f32[4,16,64]{1,0,2:T(4,128)S(1)} %copy.36), channel_id=1, replica_groups=mesh['row'=16,'col'=8] {'col'}, dimensions={2}, use_global_device_ids=true | all-gather | bytes 147456 | tf_op jit(solution)/shard_map/all_gather | solution.py:124
  297.6 1.8 convolution_divide_fusion
  299.4 27.5 %all_gather.7 = f32[4,256,64]{2,1,0:T(8,128)S(1)} all-gather(f32[4,16,64]{2,1,0:T(8,128)S(1)} %convolution_divide_fusion), channel_id=1, replica_groups=mesh['row'=16,'col'=8] {'row'}, dimensions={1}, use_global_device_ids=true | all-gather | bytes 278528 | tf_op jit(solution)/shard_map/all_gather | solution.py:135
  327.3 1.9 collective-permute-start.8
  329.3 2.4 collective-permute-start.9
  331.7 2.5 collective-permute-done.9
  334.3 1.8 collective-permute-start.10
  336.1 1.6 collective-permute-start.11
  337.7 3.2 collective-permute-done.11
  341.5 6.0 %convolution_subtract_fusion = f32[4,256,1024]{2,1,0:T(8,128)S(1)} fusion(f32[4,256,1024]{2,1,0:T(8,128)} %fusion.17, f32[4,256,66]{1,2,0:T(8,128)S(1)} %convolution_bitcast_fusion, f32[1024]{0:T(1024)S(1)} %get-tuple-element.71, s32[1024]{0:T(1024)S(1)} %get-tuple-element.74, f32[1024]{0:T(1024)S(1)} %get-tuple-element.72, ...), kind=kOutput, calls=%fused_computation.65 | convolution fusion | flops 831858688 | bytes 8675592 | tf_op jit(solution)/shard_map/spb,qb->spq/dot_general | solution.py:173
  347.5 3.4 collective-permute-start.12
  350.9 1.9 collective-permute-start.13
  352.9 3.1 collective-permute-done.13
  358.1 4.0 collective-permute-start.15
  363.0 13.9 %fusion.112 = (f32[4]{0:T(128)S(1)}, f32[4,256,1024]{2,1,0:T(8,128)}, f32[4]{0:T(128)S(1)}) fusion(f32[256]{0:T(256)S(1)} %and_convert_fusion, f32[4,256,1024]{2,1,0:T(8,128)} %copy-done.1, f32[4,1,1024]{2,1,0:T(1,128)S(1)} %collective-permute-done.12, f32[4,1,1024]{2,1,0:T(1,128)S(1)} %collective-permute-done.13, f32[1024]{0:T(1024)S(1)} %fusion.92, ...), kind=kLoop, calls=%fused_computation.219 | loop fusion | flops 18874360 | bytes 8434784 | tf_op jit(solution)/shard_map/reduce_sum | solution.py:206
  377.0 78.1 %all-reduce = (f32[1,4]{1,0:T(1,128)S(1)}, f32[1,4]{1,0:T(1,128)S(1)}) all-reduce(f32[1,4]{1,0:T(1,128)S(1)} %bitcast.87, f32[1,4]{1,0:T(1,128)S(1)} %bitcast.88), channel_id=1, replica_groups=mesh['row'=16,'col'=8] {'row','col'}, use_global_device_ids=true, to_apply=%region_6.7 | all-reduce | flops 8 | bytes 64 | tf_op jit(solution)/shard_map/psum | solution.py:207
  (74 shorter events, 12.7 us)
Async XLA Ops:
  5.3 27.8 %collective-permute-start = (f32[4,130,1024]{2,0,1:T(4,128)S(1)}, f32[4,130,1024]{2,0,1:T(4,128)}, u32[]{:S(2)}, u32[]{:S(2)}) collective-permute-start(f32[4,130,1024]{2,0,1:T(4,128)S(1)} %copy.42), channel_id=1, source_target_pairs={{0,8},{8,16},{16,24},{24,32},{32,40},{40,48},{48,56},{56,64},{64,7... | collective-permute-start | bytes 6389768 | tf_op jit(solution)/shard_map/ppermute | solution.py:28
  12.5 7.3 %copy-start.5 = (s32[2,4,1,1]{1,3,2,0:T(1,128)S(1)}, s32[2,4,1,1]{1,3,2,0:T(1,128)}, u32[]{:S(2)}) copy-start(s32[2,4,1,1]{1,3,2,0:T(1,128)} %param.6) | copy-start | bytes 100
  12.5 28.1 %collective-permute-start.1 = (f32[4,130,1024]{2,0,1:T(4,128)}, f32[4,130,1024]{2,0,1:T(4,128)}, u32[]{:S(2)}, u32[]{:S(2)}) collective-permute-start(f32[4,130,1024]{2,0,1:T(4,128)} %copy.43), channel_id=1, source_target_pairs={{8,0},{16,8},{24,16},{32,24},{40,32},{48,40},{56,48},{64,56},{72,6... | collective-permute-start | bytes 6389768 | tf_op jit(solution)/shard_map/ppermute | solution.py:29
  46.8 9.3 %copy-start.4 = (s32[2,4,1,1]{1,3,2,0:T(1,128)S(1)}, s32[2,4,1,1]{1,3,2,0:T(1,128)}, u32[]{:S(2)}) copy-start(s32[2,4,1,1]{1,3,2,0:T(1,128)} %param.7) | copy-start | bytes 100
  46.8 50.1 %copy-start.2 = (f32[4,256,1024]{1,0,2:T(4,128)S(1)}, f32[4,256,1024]{1,0,2:T(4,128)}, u32[]{:S(2)}) copy-start(f32[4,256,1024]{1,0,2:T(4,128)} %copy.28) | copy-start | bytes 12582916
  50.3 46.6 %collective-permute-start.2 = (f32[4,516,130]{1,0,2:T(4,128)S(1)}, f32[4,516,130]{1,0,2:T(4,128)S(1)}, u32[]{:S(2)}, u32[]{:S(2)}) collective-permute-start(f32[4,516,130]{1,0,2:T(4,128)S(1)} %get-tuple-element.42), channel_id=1, source_target_pairs={{0,1},{1,2},{2,3},{3,4},{4,5},{5,6},{6,7},{8,9},{9,10},{10,11},{11... | collective-permute-start | bytes 3219848 | tf_op jit(solution)/shard_map/ppermute | solution.py:28
  54.1 42.8 %collective-permute-start.3 = (f32[4,516,130]{1,0,2:T(4,128)S(1)}, f32[4,516,130]{1,0,2:T(4,128)S(1)}, u32[]{:S(2)}, u32[]{:S(2)}) collective-permute-start(f32[4,516,130]{1,0,2:T(4,128)S(1)} %get-tuple-element.43), channel_id=1, source_target_pairs={{1,0},{2,1},{3,2},{4,3},{5,4},{6,5},{7,6},{9,8},{10,9},{11,10},{12... | collective-permute-start | bytes 3219848 | tf_op jit(solution)/shard_map/ppermute | solution.py:29
  163.2 9.2 %copy-start.3 = (f32[4,256,1024]{2,1,0:T(8,128)S(1)}, f32[4,256,1024]{2,1,0:T(8,128)}, u32[]{:S(2)}) copy-start(f32[4,256,1024]{2,1,0:T(8,128)} %param.4) | copy-start | bytes 12582916
  175.9 24.1 %copy-start = (f32[4,256,1024]{2,1,0:T(8,128)}, f32[4,256,1024]{2,1,0:T(8,128)S(1)}, u32[]{:S(2)}) copy-start(f32[4,256,1024]{2,1,0:T(8,128)S(1)} %fusion.25) | copy-start | bytes 12582916
  176.0 19.8 %collective-permute-start.4 = (f32[4,4,1024]{2,1,0:T(4,128)S(1)}, f32[4,4,1024]{2,1,0:T(4,128)S(1)}, u32[]{:S(2)}, u32[]{:S(2)}) collective-permute-start(f32[4,4,1024]{2,1,0:T(4,128)S(1)} %get-tuple-element.53), channel_id=1, source_target_pairs={{0,8},{8,16},{16,24},{24,32},{32,40},{40,48},{48,56},{56,64},{64,7... | collective-permute-start | bytes 196616 | tf_op jit(solution)/shard_map/ppermute | solution.py:28
  193.8 5.6 %collective-permute-start.5 = (f32[4,4,1024]{2,1,0:T(4,128)S(1)}, f32[4,4,1024]{2,1,0:T(4,128)S(1)}, u32[]{:S(2)}, u32[]{:S(2)}) collective-permute-start(f32[4,4,1024]{2,1,0:T(4,128)S(1)} %get-tuple-element.54), channel_id=1, source_target_pairs={{8,0},{16,8},{24,16},{32,24},{40,32},{48,40},{56,48},{64,56},{72,6... | collective-permute-start | bytes 196616 | tf_op jit(solution)/shard_map/ppermute | solution.py:29
  200.4 5.9 %collective-permute-start.6 = (f32[4,264,4]{1,2,0:T(4,128)S(1)}, f32[4,264,4]{1,2,0:T(4,128)S(1)}, u32[]{:S(2)}, u32[]{:S(2)}) collective-permute-start(f32[4,264,4]{1,2,0:T(4,128)S(1)} %copy.32), channel_id=1, source_target_pairs={{0,1},{1,2},{2,3},{3,4},{4,5},{5,6},{6,7},{8,9},{9,10},{10,11},{11... | collective-permute-start | bytes 50696 | tf_op jit(solution)/shard_map/ppermute | solution.py:28
  204.8 4.8 %collective-permute-start.7 = (f32[4,264,4]{1,2,0:T(4,128)S(1)}, f32[4,264,4]{1,2,0:T(4,128)S(1)}, u32[]{:S(2)}, u32[]{:S(2)}) collective-permute-start(f32[4,264,4]{1,2,0:T(4,128)S(1)} %copy.34), channel_id=1, source_target_pairs={{1,0},{2,1},{3,2},{4,3},{5,4},{6,5},{7,6},{9,8},{10,9},{11,10},{12... | collective-permute-start | bytes 50696 | tf_op jit(solution)/shard_map/ppermute | solution.py:29
  327.3 4.4 collective-permute-start.8
  329.3 4.9 %collective-permute-start.9 = (f32[4,1,64]{2,1,0:T(1,128)S(1)}, f32[4,1,64]{2,1,0:T(1,128)S(1)}, u32[]{:S(2)}, u32[]{:S(2)}) collective-permute-start(f32[4,1,64]{2,1,0:T(1,128)S(1)} %get-tuple-element.60), channel_id=1, source_target_pairs={{8,0},{16,8},{24,16},{32,24},{40,32},{48,40},{56,48},{64,56},{72,6... | collective-permute-start | bytes 3080 | tf_op jit(solution)/shard_map/ppermute | solution.py:29
  334.3 3.4 collective-permute-start.10
  336.1 4.8 %collective-permute-start.11 = (f32[4,18,1]{2,1,0:T(8,128)S(1)}, f32[4,18,1]{2,1,0:T(8,128)S(1)}, u32[]{:S(2)}, u32[]{:S(2)}) collective-permute-start(f32[4,18,1]{2,1,0:T(8,128)S(1)} %get-tuple-element.58), channel_id=1, source_target_pairs={{1,0},{2,1},{3,2},{4,3},{5,4},{6,5},{7,6},{9,8},{10,9},{11,10},{12... | collective-permute-start | bytes 872 | tf_op jit(solution)/shard_map/ppermute | solution.py:29
  347.5 8.5 %copy-start.1 = (f32[4,256,1024]{2,1,0:T(8,128)}, f32[4,256,1024]{2,1,0:T(8,128)S(1)}, u32[]{:S(2)}) copy-start(f32[4,256,1024]{2,1,0:T(8,128)S(1)} %convolution_subtract_fusion) | copy-start | bytes 12582916
  347.5 5.3 %collective-permute-start.12 = (f32[4,1,1024]{2,1,0:T(1,128)S(1)}, f32[4,1,1024]{2,1,0:T(1,128)S(1)}, u32[]{:S(2)}, u32[]{:S(2)}) collective-permute-start(f32[4,1,1024]{2,1,0:T(1,128)S(1)} %get-tuple-element.52), channel_id=1, source_target_pairs={{0,8},{8,16},{16,24},{24,32},{32,40},{40,48},{48,56},{56,64},{64,7... | collective-permute-start | bytes 49160 | tf_op jit(solution)/shard_map/ppermute | solution.py:28
  350.9 5.1 %collective-permute-start.13 = (f32[4,1,1024]{2,1,0:T(1,128)S(1)}, f32[4,1,1024]{2,1,0:T(1,128)S(1)}, u32[]{:S(2)}, u32[]{:S(2)}) collective-permute-start(f32[4,1,1024]{2,1,0:T(1,128)S(1)} %get-tuple-element.51), channel_id=1, source_target_pairs={{8,0},{16,8},{24,16},{32,24},{40,32},{48,40},{56,48},{64,56},{72,6... | collective-permute-start | bytes 49160 | tf_op jit(solution)/shard_map/ppermute | solution.py:29
  356.5 5.6 %collective-permute-start.14 = (f32[4,258,1]{1,0,2:T(4,128)S(1)}, f32[4,258,1]{1,0,2:T(4,128)S(1)}, u32[]{:S(2)}, u32[]{:S(2)}) collective-permute-start(f32[4,258,1]{1,0,2:T(4,128)S(1)} %copy.38), channel_id=1, source_target_pairs={{1,0},{2,1},{3,2},{4,3},{5,4},{6,5},{7,6},{9,8},{10,9},{11,10},{12... | collective-permute-start | bytes 12392 | tf_op jit(solution)/shard_map/ppermute | solution.py:29
  358.1 4.8 %collective-permute-start.15 = (f32[4,258,1]{1,0,2:T(4,128)S(1)}, f32[4,258,1]{1,0,2:T(4,128)S(1)}, u32[]{:S(2)}, u32[]{:S(2)}) collective-permute-start(f32[4,258,1]{1,0,2:T(4,128)S(1)} %copy.40), channel_id=1, source_target_pairs={{0,1},{1,2},{2,3},{3,4},{4,5},{5,6},{6,7},{8,9},{9,10},{10,11},{11... | collective-permute-start | bytes 12392 | tf_op jit(solution)/shard_map/ppermute | solution.py:28
where the time goes:
time: 458 us; the launch traced here: 456 us
  blocking collectives  134 us (29%)
  other arithmetic  102 us (22%)
  local copies, waits for them, and re-layouts  83.4 us (18%)
  waiting for transfers between devices  71.2 us (16%)
  starting transfers between devices  55.5 us (12%)
  matrix products  8.74 us (2%)
    psum x1, blocking collectives, body(): height_all, slope_all = lax.psum((height_sq, slope_sum), ('row', 'col'))  78.1 us
    ppermute x8, waiting for transfers between devices, with_halo(): before = lax.ppermute(last, axis, up)  54.4 us
    ppermute x8, starting transfers between devices, with_halo(): before = lax.ppermute(last, axis, up)  41.4 us
    concatenate x4, other arithmetic, with_halo(): value = jnp.concatenate([before, value, after], axis=dim)  37.5 us
    all_gather x1, blocking collectives, long_cols(): portion = lax.all_gather(coarse, 'col', axis=2, tiled=True)  27.9 us
    all_gather x1, blocking collectives, long_rows(): portion = lax.all_gather(surface, 'row', axis=1, tiled=True)  27.5 us
    unnamed x18, local copies, waits for them, and re-layouts  24.7 us
    gather x12, local copies, waits for them, and re-layouts  21.5 us
  transfers between devices with their start and end apart: 16, of which 9 were waited for; matrix products, arithmetic and copies ran while one was open for 4% of the time, Pallas kernels for 0%

commit v1 on v0

v1 whole, which is shorter than its diff:
```python
import math

import jax
import jax.numpy as jnp
from jax import lax
from jax.experimental import pallas as pl
from jax.experimental.pallas import tpu as pltpu
from jax.sharding import PartitionSpec as P

LS = 5
SR = 4
LCUT = 1600
BLOCK = 16
ALPHA = math.sqrt(math.log(2.0) / math.pi)
EPSILON = 1e-06
HIGHEST = lax.Precision.HIGHEST
HALO = 136
EDGE = 8
LANES = 128
TAPS = [math.exp(-math.pi * (k / (ALPHA * LS)) ** 2) for k in range(-SR, SR + 1)]
VMEM_LIMIT = 56 * 1024 * 1024


def lane_iota(rows):
    return lax.broadcasted_iota(jnp.int32, (rows, LANES), 1)


def pack_kernel(offs_ref, x_ref, top_ref, bot_ref, left_ref, right_ref):
    s = pl.program_id(0)
    shift = offs_ref[1, s].astype(jnp.float32)
    rows, cols = x_ref.shape[1], x_ref.shape[2]
    for j in range(cols // LANES):
        sl = slice(j * LANES, (j + 1) * LANES)
        top_ref[0, j] = x_ref[0, 0:HALO, sl]
        bot_ref[0, j] = x_ref[0, rows - HALO : rows, sl]
    top_ref[0, 0, HALO - 1 : HALO, :] = jnp.full((1, LANES), shift, jnp.float32)
    bot_ref[0, 0, 0:1, :] = jnp.full((1, LANES), shift, jnp.float32)
    left_ref[0] = x_ref[0, :, 0:256].T[0:HALO, :]
    right_ref[0] = x_ref[0, :, cols - 256 : cols].T[256 - HALO : 256, :]


def pack(after, offs):
    scans, rows, cols = after.shape
    n_tiles = cols // LANES
    return pl.pallas_call(
        pack_kernel,
        grid=(scans,),
        in_specs=[
            pl.BlockSpec(memory_space=pltpu.SMEM),
            pl.BlockSpec((1, rows, cols), lambda s: (s, 0, 0)),
        ],
        out_specs=[
            pl.BlockSpec((1, n_tiles, HALO, LANES), lambda s: (s, 0, 0, 0)),
            pl.BlockSpec((1, n_tiles, HALO, LANES), lambda s: (s, 0, 0, 0)),
            pl.BlockSpec((1, HALO, rows), lambda s: (s, 0, 0)),
            pl.BlockSpec((1, HALO, rows), lambda s: (s, 0, 0)),
        ],
        out_shape=[
            jax.ShapeDtypeStruct((scans, n_tiles, HALO, LANES), jnp.float32),
            jax.ShapeDtypeStruct((scans, n_tiles, HALO, LANES), jnp.float32),
            jax.ShapeDtypeStruct((scans, HALO, rows), jnp.float32),
            jax.ShapeDtypeStruct((scans, HALO, rows), jnp.float32),
        ],
        name="pack",
    )(offs, after)


def scalar_taps(fraction):
    t = fraction.astype(jnp.float32) * (1.0 / 256.0)
    t2 = t * t
    t3 = t2 * t
    return (
        0.5 * (2.0 * t2 - t3 - t),
        0.5 * (3.0 * t3 - 5.0 * t2 + 2.0),
        0.5 * (4.0 * t2 - 3.0 * t3 + t),
        0.5 * (t3 - t2),
    )


RB = 16


def resample_kernel(
    offs_ref, fracs_ref, cm_ref, rm_ref, hc_ref,
    after, before, up, dn, lcols, rcols, cup, cdn,
    diff_out, edge_l, edge_r, y_ref,
    win, stage, bef, dif, sem, bsem, osem,
):
    scans = win.shape[0]
    rows, cols = bef.shape[1], bef.shape[2]
    n_out = cols // LANES
    left = 2 * LANES

    def copies(s):
        return [
            (after.at[s, :, pl.ds(j * LANES, LANES)], win.at[s, 2 + j, pl.ds(HALO, rows), :])
            for j in range(n_out)
        ] + [
            (up.at[s], win.at[s, pl.ds(2, n_out), pl.ds(0, HALO), :]),
            (dn.at[s], win.at[s, pl.ds(2, n_out), pl.ds(HALO + rows, HALO), :]),
            (lcols.at[s], stage.at[s, 0, pl.ds(256 - HALO, HALO), :]),
            (rcols.at[s], stage.at[s, 1, pl.ds(0, HALO), :]),
            (cup.at[s], stage.at[s, 2, pl.ds(256 - HALO, HALO), :]),
            (cup.at[s], stage.at[s, 3, pl.ds(0, HALO), :]),
            (cdn.at[s], stage.at[s, 4, pl.ds(256 - HALO, HALO), :]),
            (cdn.at[s], stage.at[s, 5, pl.ds(0, HALO), :]),
        ]

    for s in range(scans):
        for n, (a, b) in enumerate(copies(s)):
            pltpu.make_async_copy(a, b, sem.at[s, n]).start()
        pltpu.make_async_copy(before.at[s], bef.at[s], bsem.at[s]).start()

    def one_scan(s, carry):
        for n, (a, b) in enumerate(copies(s)):
            pltpu.make_async_copy(a, b, sem.at[s, n]).wait()
        pltpu.make_async_copy(before.at[s], bef.at[s], bsem.at[s]).wait()
        dr = offs_ref[0, s]
        dc = offs_ref[1, s]

        def put(slot, first_tile, row0, part):
            flipped = stage[s, slot].T
            for h in range(2):
                win[s, first_tile + h, row0 : row0 + part.stop - part.start, :] = flipped[
                    part, h * LANES : (h + 1) * LANES
                ]

        def put_side(first_tile, slots):
            put(slots[0], first_tile, HALO, slice(0, rows))

            @pl.when(dr <= 0)
            def _():
                put(slots[1], first_tile, 0, slice(rows - HALO, rows))

            @pl.when(dr >= -1)
            def _():
                put(slots[2], first_tile, HALO + rows, slice(0, HALO))

        @pl.when(dc <= 0)
        def _():
            put_side(0, (0, 2, 4))

        @pl.when(dc >= -1)
        def _():
            put_side(2 + n_out, (1, 3, 5))

        rt = scalar_taps(fracs_ref[0, s])
        ct = scalar_taps(fracs_ref[1, s])
        r0 = HALO + dr - 1
        c0 = left + dc - 1
        k = lax.div(c0, LANES)
        r = c0 - k * LANES
        back = lax.rem(LANES - r, LANES)
        lane = lane_iota(RB)
        keep = lane < LANES - r

        def block(i, carry):
            p0 = i * RB
            first = r0 + p0
            tiles = []
            for j in range(n_out + 2):
                acc = rt[0] * win[s, k + j, pl.ds(first, RB), :]
                for a in range(1, 4):
                    acc = acc + rt[a] * win[s, k + j, pl.ds(first + a, RB), :]
                tiles.append(pltpu.roll(acc, back, 1))
            al = [jnp.where(keep, tiles[j], tiles[j + 1]) for j in range(n_out + 1)]
            outs = [ct[0] * al[j] for j in range(n_out)]
            for b in range(1, 4):
                rolled = [pltpu.roll(t, LANES - b, 1) for t in al]
                m = lane < LANES - b
                for j in range(n_out):
                    outs[j] = outs[j] + ct[b] * jnp.where(m, rolled[j], rolled[j + 1])
            po = pl.multiple_of(p0, RB)
            for j in range(n_out):
                sl = slice(j * LANES, (j + 1) * LANES)
                dif[s, pl.ds(po, RB), sl] = bef[s, pl.ds(po, RB), sl] - outs[j]
            return carry

        lax.fori_loop(0, rows // RB, block, 0)
        pltpu.make_async_copy(dif.at[s], diff_out.at[s], osem.at[s]).start()
        d = dif[s]
        edge_l[s] = d[:, 0:LANES].T[0:EDGE]
        edge_r[s] = d[:, cols - LANES : cols].T[LANES - EDGE : LANES]
        t1 = jnp.dot(d, cm_ref[...], precision=HIGHEST, preferred_element_type=jnp.float32)
        c1 = jnp.dot(rm_ref[...], t1, precision=HIGHEST, preferred_element_type=jnp.float32)
        for t in range(y_ref.shape[0]):
            y_ref[t, s] = jnp.dot(
                c1, hc_ref[:, t * LANES : (t + 1) * LANES],
                precision=HIGHEST, preferred_element_type=jnp.float32,
            )
        return carry

    lax.fori_loop(0, scans, one_scan, 0)
    for s in range(scans):
        pltpu.make_async_copy(dif.at[s], diff_out.at[s], osem.at[s]).wait()


def resample(offs, fracs, cm, rm, hc, after, before, up, dn, lcols, rcols, cup, cdn):
    scans, rows, cols = after.shape
    n_col = hc.shape[1] // LANES
    ext = rm.shape[0]
    anywhere = pl.BlockSpec(memory_space=pl.ANY)
    vmem = pl.BlockSpec(memory_space=pltpu.VMEM)
    smem = pl.BlockSpec(memory_space=pltpu.SMEM)
    return pl.pallas_call(
        resample_kernel,
        in_specs=[smem, smem, vmem, vmem, vmem] + [anywhere] * 8,
        out_specs=[anywhere, vmem, vmem, vmem],
        out_shape=[
            jax.ShapeDtypeStruct((scans, rows, cols), jnp.float32),
            jax.ShapeDtypeStruct((scans, EDGE, rows), jnp.float32),
            jax.ShapeDtypeStruct((scans, EDGE, rows), jnp.float32),
            jax.ShapeDtypeStruct((n_col, scans, ext, LANES), jnp.float32),
        ],
        scratch_shapes=[
            pltpu.VMEM((scans, cols // LANES + 4, 2 * HALO + rows, LANES), jnp.float32),
            pltpu.VMEM((scans, 6, 256, rows), jnp.float32),
            pltpu.VMEM((scans, rows, cols), jnp.float32),
            pltpu.VMEM((scans, rows, cols), jnp.float32),
            pltpu.SemaphoreType.DMA((scans, cols // LANES + 8)),
            pltpu.SemaphoreType.DMA((scans,)),
            pltpu.SemaphoreType.DMA((scans,)),
        ],
        compiler_params=pltpu.CompilerParams(vmem_limit_bytes=VMEM_LIMIT),
        name="resample",
    )(offs, fracs, cm, rm, hc, after, before, up, dn, lcols, rcols, cup, cdn)


def filter_lanes(tiles, inv, lane):
    n = len(tiles) - 2
    outs = [TAPS[SR] * tiles[j + 1] for j in range(n)]
    for k in range(1, SR + 1):
        fwd = [pltpu.roll(t, LANES - k, 1) for t in tiles[1:]]
        bwd = [pltpu.roll(t, k, 1) for t in tiles[:-1]]
        mf = lane < LANES - k
        mb = lane >= k
        for j in range(n):
            ahead = jnp.where(mf, fwd[j], fwd[j + 1])
            behind = jnp.where(mb, bwd[j + 1], bwd[j])
            outs[j] = outs[j] + TAPS[SR + k] * (ahead + behind)
    return [outs[j] * inv[j] for j in range(n)]


def side_tiles(strip_l, strip_r):
    rows = strip_l.shape[1]
    zero = jnp.zeros((LANES - EDGE, rows), jnp.float32)
    return (
        jnp.concatenate([zero, strip_l], axis=0).T,
        jnp.concatenate([strip_r, zero], axis=0).T,
    )


def fill_sides(scr, s, strip_l, strip_r):
    a, b = side_tiles(strip_l, strip_r)
    scr[0] = a
    scr[1] = b


def across_rows(load, sides, p0, n, inv_ref):
    width = inv_ref.shape[1] // LANES - 2
    lane = lane_iota(n)
    zero = jnp.zeros((n, LANES), jnp.float32)
    tiles = [zero, sides[0, pl.ds(p0, n), :]]
    tiles += [load(p0, n, j) for j in range(width)]
    tiles += [sides[1, pl.ds(p0, n), :], zero]
    inv = [inv_ref[0:1, j * LANES : (j + 1) * LANES] for j in range(width + 2)]
    return filter_lanes(tiles, inv, lane)


def strips_kernel(y_ref, hr_ref, top_ref, bot_ref, lref, rref, inv_ref, z_ref, ftop, fbot, sides):
    scans = top_ref.shape[0]
    rows = lref.shape[2]
    for s in range(scans):
        p = y_ref[0, s]
        for t in range(1, y_ref.shape[0]):
            p = p + y_ref[t, s]
        for t in range(z_ref.shape[0]):
            ext = p.shape[0]
            z_ref[t, s] = jnp.dot(
                hr_ref[t * ext : (t + 1) * ext, :], p,
                precision=HIGHEST, preferred_element_type=jnp.float32,
            )
        fill_sides(sides, s, lref[s], rref[s])

        def load_top(p0, n, j):
            return top_ref[s, :, j * LANES : (j + 1) * LANES]

        def load_bot(p0, n, j):
            return bot_ref[s, :, j * LANES : (j + 1) * LANES]

        for j, v in enumerate(across_rows(load_top, sides, 0, EDGE, inv_ref)):
            ftop[s, j] = v
        for j, v in enumerate(across_rows(load_bot, sides, rows - EDGE, EDGE, inv_ref)):
            fbot[s, j] = v


def strips(y, hr, diff, lstrip, rstrip, inv):
    scans, rows, cols = diff.shape
    ext = y.shape[2]
    n_row = hr.shape[0] // ext
    wide = inv.shape[1]
    return pl.pallas_call(
        strips_kernel,
        grid=(1,),
        in_specs=[
            pl.BlockSpec(y.shape, lambda i: (0, 0, 0, 0)),
            pl.BlockSpec(hr.shape, lambda i: (0, 0)),
            pl.BlockSpec((scans, EDGE, cols), lambda i: (0, 0, 0)),
            pl.BlockSpec((scans, EDGE, cols), lambda i: (0, rows // EDGE - 1, 0)),
            pl.BlockSpec(lstrip.shape, lambda i: (0, 0, 0)),
            pl.BlockSpec(rstrip.shape, lambda i: (0, 0, 0)),
            pl.BlockSpec(inv.shape, lambda i: (0, 0)),
        ],
        out_specs=[
            pl.BlockSpec((n_row, scans, ext, LANES), lambda i: (0, 0, 0, 0)),
            pl.BlockSpec((scans, wide // LANES, EDGE, LANES), lambda i: (0, 0, 0, 0)),
            pl.BlockSpec((scans, wide // LANES, EDGE, LANES), lambda i: (0, 0, 0, 0)),
        ],
        out_shape=[
            jax.ShapeDtypeStruct((n_row, scans, ext, LANES), jnp.float32),
            jax.ShapeDtypeStruct((scans, wide // LANES, EDGE, LANES), jnp.float32),
            jax.ShapeDtypeStruct((scans, wide // LANES, EDGE, LANES), jnp.float32),
        ],
        scratch_shapes=[pltpu.VMEM((2, rows, LANES), jnp.float32)],
        compiler_params=pltpu.CompilerParams(vmem_limit_bytes=VMEM_LIMIT),
        name="strips",
    )(y, hr, diff, diff, lstrip, rstrip, inv)


def final_kernel(
    diff_ref, lref, rref, upr, dnr, z_ref, uc_ref, inv_ref, invr_ref, mc_ref, mr_ref,
    band_ref, slope_ref, sum_ref,
    sides, ac, cu, bd,
):
    rows, cols = diff_ref.shape[1], diff_ref.shape[2]
    wide = inv_ref.shape[1]
    n_out = cols // LANES
    w = z_ref[0, 0]
    for t in range(1, z_ref.shape[0]):
        w = w + z_ref[t, 0]
    n_wide = wide // LANES
    for j in range(n_wide):
        cu[j] = jnp.dot(
            w, uc_ref[:, j * LANES : (j + 1) * LANES],
            precision=HIGHEST, preferred_element_type=jnp.float32,
        )
    fill_sides(sides, 0, lref[0], rref[0])
    for j in range(n_wide):
        ac[j, EDGE : 2 * EDGE, :] = upr[0, j]
        ac[j, 2 * EDGE + rows : 3 * EDGE + rows, :] = dnr[0, j]

    def load(p0, n, j):
        return diff_ref[0, pl.ds(p0, n), j * LANES : (j + 1) * LANES]

    def along_lanes(i, carry):
        p0 = pl.multiple_of(i * 16, 16)
        for j, v in enumerate(across_rows(load, sides, p0, 16, inv_ref)):
            ac[j, pl.ds(p0 + 2 * EDGE, 16), :] = v
        return carry

    lax.fori_loop(0, rows // 16, along_lanes, 0)

    sub = lax.broadcasted_iota(jnp.int32, (8, LANES), 0).astype(jnp.float32)
    f_even = (2.0 * sub + 17.0) * (1.0 / 32.0)
    f_odd = (2.0 * sub + 1.0) * (1.0 / 32.0)

    def band_chunk(c, carry):
        base = pl.multiple_of(c * 8, 8)
        e = lax.div(c, 2)
        f = jnp.where(lax.rem(c, 2) == 1, f_even, f_odd)
        inv = invr_ref[pl.ds(base, 8), :]
        for j in range(n_wide):
            acc = TAPS[SR] * ac[j, pl.ds(base + EDGE, 8), :]
            for k in range(1, SR + 1):
                acc = acc + TAPS[SR + k] * (
                    ac[j, pl.ds(base + EDGE - k, 8), :] + ac[j, pl.ds(base + EDGE + k, 8), :]
                )
            a = cu[j, pl.ds(e, 1), :]
            b = cu[j, pl.ds(e + 1, 1), :]
            bd[j, pl.ds(base, 8), :] = acc * inv - (a + f * (b - a))
        return carry

    lax.fori_loop(0, rows // 8 + 2, band_chunk, 0)

    lane = lane_iota(8)
    first = lane >= 1
    last = lane < LANES - 1

    def slope_chunk(c, carry):
        s1, s2 = carry
        base = pl.multiple_of(c * 8, 8)
        here = [bd[j, pl.ds(base + 8, 8), :] for j in range(n_out + 2)]
        fwd = [pltpu.roll(t, LANES - 1, 1) for t in here[1:]]
        bwd = [pltpu.roll(t, 1, 1) for t in here[:-1]]
        mr = mr_ref[pl.ds(base, 8), :]
        for j in range(n_out):
            so = slice(j * LANES, (j + 1) * LANES)
            gc = jnp.where(last, fwd[j], fwd[j + 1]) - jnp.where(first, bwd[j + 1], bwd[j])
            gc = gc * mc_ref[0:1, so]
            gr = (bd[j + 1, pl.ds(base + 9, 8), :] - bd[j + 1, pl.ds(base + 7, 8), :]) * mr
            sq = gc * gc + gr * gr
            v = here[j + 1]
            band_ref[0, pl.ds(base, 8), so] = v
            slope_ref[0, pl.ds(base, 8), so] = sq
            s1 = s1 + v * v
            s2 = s2 + sq
        return s1, s2

    zero = jnp.zeros((8, LANES), jnp.float32)
    s1, s2 = lax.fori_loop(0, rows // 8, slope_chunk, (zero, zero))
    sum_ref[0, 0:1, :] = jnp.sum(s1, axis=0, keepdims=True)
    sum_ref[0, 1:2, :] = jnp.sum(s2, axis=0, keepdims=True)


def final(diff, lstrip, rstrip, upr, dnr, z, uc, inv, invr, mc, mr):
    scans, rows, cols = diff.shape
    wide = inv.shape[1]
    n_row, _, ext, _ = z.shape
    const2 = lambda s: (0, 0)
    one = lambda s: (s, 0, 0)
    return pl.pallas_call(
        final_kernel,
        grid=(scans,),
        in_specs=[
            pl.BlockSpec((1, rows, cols), one),
            pl.BlockSpec((1, EDGE, rows), one),
            pl.BlockSpec((1, EDGE, rows), one),
            pl.BlockSpec((1, wide // LANES, EDGE, LANES), lambda s: (s, 0, 0, 0)),
            pl.BlockSpec((1, wide // LANES, EDGE, LANES), lambda s: (s, 0, 0, 0)),
            pl.BlockSpec((n_row, 1, ext, LANES), lambda s: (0, s, 0, 0)),
            pl.BlockSpec(uc.shape, const2),
            pl.BlockSpec(inv.shape, const2),
            pl.BlockSpec(invr.shape, const2),
            pl.BlockSpec(mc.shape, const2),
            pl.BlockSpec(mr.shape, const2),
        ],
        out_specs=[
            pl.BlockSpec((1, rows, cols), one),
            pl.BlockSpec((1, rows, cols), one),
            pl.BlockSpec((1, 2, LANES), one),
        ],
        out_shape=[
            jax.ShapeDtypeStruct((scans, rows, cols), jnp.float32),
            jax.ShapeDtypeStruct((scans, rows, cols), jnp.float32),
            jax.ShapeDtypeStruct((scans, 2, LANES), jnp.float32),
        ],
        scratch_shapes=[
            pltpu.VMEM((2, rows, LANES), jnp.float32),
            pltpu.VMEM((wide // LANES, rows + 4 * EDGE, LANES), jnp.float32),
            pltpu.VMEM((wide // LANES, ext, LANES), jnp.float32),
            pltpu.VMEM((wide // LANES, rows + 2 * EDGE, LANES), jnp.float32),
        ],
        compiler_params=pltpu.CompilerParams(vmem_limit_bytes=VMEM_LIMIT),
        name="final",
    )(diff, lstrip, rstrip, upr, dnr, z, uc, inv, invr, mc, mr)


def window_weight(index, count):
    total = jnp.zeros(index.shape, jnp.float32)
    for k in range(-SR, SR + 1):
        inside = (index + k >= 0) & (index + k < count)
        total = total + jnp.where(inside, TAPS[k + SR], 0.0)
    return total


def mean_matrix(start, length, count, width):
    fine = start + lax.broadcasted_iota(jnp.int32, (length, 1), 0)
    blocks = start // BLOCK - 1 + lax.broadcasted_iota(jnp.int32, (1, width), 1)
    valid = lax.broadcasted_iota(jnp.int32, (1, width), 1) < length // BLOCK + 2
    total = jnp.zeros((length, width), jnp.float32)
    for k in range(-SR, SR + 1):
        other = fine + k
        inside = (other >= 0) & (other < count)
        coef = jnp.where(inside, TAPS[k + SR] / (BLOCK * window_weight(other, count)), 0.0)
        total = total + jnp.where((other // BLOCK == blocks) & valid, coef, 0.0)
    return total


def gauss(distance):
    scaled = (distance * BLOCK).astype(jnp.float32) / (ALPHA * LCUT)
    return jnp.exp(-math.pi * scaled * scaled)


def long_matrix(start_block, per_tile, tiles, ext, axis_first):
    count = per_tile * tiles
    src = start_block - 1 + jnp.arange(ext, dtype=jnp.int32)
    src_ok = jnp.arange(ext) < per_tile + 2
    e = jnp.arange(ext, dtype=jnp.int32)
    tgt = (jnp.arange(tiles, dtype=jnp.int32)[:, None] * per_tile - 1 + e[None, :]).reshape(-1)
    tgt = jnp.clip(tgt, 0, count - 1)
    norm = jnp.sum(gauss(jnp.arange(count, dtype=jnp.int32)[:, None] - tgt[None, :]), axis=0)
    m = gauss(src[:, None] - tgt[None, :]) / norm[None, :]
    m = jnp.where(src_ok[:, None], m, 0.0)
    return m if axis_first else m.T


def upsample_cols(per_tile, wide):
    q = lax.broadcasted_iota(jnp.int32, (LANES, wide), 1) - LANES
    num = 2 * q + 1 - BLOCK
    low = num // (2 * BLOCK)
    frac = (num - low * (2 * BLOCK)).astype(jnp.float32) / (2.0 * BLOCK)
    e = lax.broadcasted_iota(jnp.int32, (LANES, wide), 0)
    near = (q >= -1) & (q <= per_tile * BLOCK)
    m = jnp.where(e == low + 1, 1.0 - frac, 0.0) + jnp.where(e == low + 2, frac, 0.0)
    return jnp.where(near, m, 0.0)


def gather_sum_ready(y, axis):
    return lax.all_to_all(y, axis, 0, 0, tiled=True)


def body(before_scan, after_scan, drift_offsets, drift_fractions):
    scans, rows, cols = before_scan.shape
    n_row, n_col = lax.axis_size("row"), lax.axis_size("col")
    row, col = lax.axis_index("row"), lax.axis_index("col")
    offs = drift_offsets.reshape(2, scans)
    fracs = drift_fractions.reshape(2, scans)
    row_down = [(i, i + 1) for i in range(n_row - 1)]
    row_up = [(j, i) for i, j in row_down]
    col_down = [(i, i + 1) for i in range(n_col - 1)]
    col_up = [(j, i) for i, j in col_down]

    top, bot, left, right = pack(after_scan, offs)
    up = lax.ppermute(bot, "row", row_down)
    dn = lax.ppermute(top, "row", row_up)
    lcols = lax.ppermute(right, "col", col_down)
    rcols = lax.ppermute(left, "col", col_up)

    slot = lax.broadcasted_iota(jnp.int32, lcols.shape, 1).astype(jnp.float32)
    for_up = jnp.where(slot < up[:, 0, 0:1, 0:1] + 2.0, rcols, lcols)
    for_dn = jnp.where(slot < dn[:, 0, HALO - 1 : HALO, 0:1] + 2.0, rcols, lcols)
    cup = lax.ppermute(for_dn, "row", row_down)
    cdn = lax.ppermute(for_up, "row", row_up)

    wide = cols + 2 * LANES
    ext = 24
    cm = mean_matrix(col * cols, cols, n_col * cols, LANES)
    rm = mean_matrix(row * rows, rows, n_row * rows, ext).T
    hc = long_matrix(col * (cols // BLOCK), cols // BLOCK, n_col, LANES, True)
    hr = long_matrix(row * (rows // BLOCK), rows // BLOCK, n_row, ext, False)
    uc = upsample_cols(cols // BLOCK, wide)
    qg = col * cols - LANES + jnp.arange(wide, dtype=jnp.int32)
    near = (qg >= col * cols - 1) & (qg <= (col + 1) * cols)
    inv = jnp.where(near, 1.0 / jnp.where(near, window_weight(qg, n_col * cols), 1.0), 0.0)[None, :]
    pg = row * rows - EDGE + jnp.arange(rows + 2 * EDGE, dtype=jnp.int32)
    nearr = (pg >= row * rows - 1) & (pg <= (row + 1) * rows)
    invr = jnp.where(nearr, 1.0 / jnp.where(nearr, window_weight(pg, n_row * rows), 1.0), 0.0)
    invr = jnp.broadcast_to(invr[:, None], (rows + 2 * EDGE, LANES))
    qi = col * cols + jnp.arange(cols, dtype=jnp.int32)
    mc = ((qi >= 1) & (qi <= n_col * cols - 2)).astype(jnp.float32)[None, :]
    pi = row * rows + jnp.arange(rows, dtype=jnp.int32)
    mr = ((pi >= 1) & (pi <= n_row * rows - 2)).astype(jnp.float32)
    mr = jnp.broadcast_to(mr[:, None], (rows, LANES))

    diff, edge_l, edge_r, y = resample(
        offs, fracs, cm, rm, hc, after_scan, before_scan, up, dn, lcols, rcols, cup, cdn
    )
    lstrip = lax.ppermute(edge_r, "col", col_down)
    rstrip = lax.ppermute(edge_l, "col", col_up)
    y = lax.all_to_all(y, "col", 0, 0, tiled=True)
    z, ftop, fbot = strips(y, hr, diff, lstrip, rstrip, inv)
    upr = lax.ppermute(fbot, "row", row_down)
    dnr = lax.ppermute(ftop, "row", row_up)
    z = lax.all_to_all(z, "row", 0, 0, tiled=True)
    band, slope, sums = final(diff, lstrip, rstrip, upr, dnr, z, uc, inv, invr, mc, mr)

    mine = jnp.sum(sums, axis=2).T.reshape(1, 2 * scans)
    mine = jnp.broadcast_to(mine[:, None, :], (n_row * n_col, 1, 2 * scans))
    every = lax.all_to_all(mine, ("row", "col"), 0, 0, tiled=True)
    total = jnp.sum(every, axis=(0, 1)).reshape(2, scans)
    cells = n_row * rows * n_col * cols
    return band, slope, jnp.sqrt(total / cells + EPSILON)


def solution(mesh):
    in_specs = (
        P(None, "row", "col"),
        P(None, "row", "col"),
        P(None, None, "row", "col"),
        P(None, None, "row", "col"),
    )
    out_specs = (P(None, "row", "col"), P(None, "row", "col"), P())
    return jax.shard_map(body, mesh=mesh, in_specs=in_specs, out_specs=out_specs, check_vma=False)
```

time: 458 us -> 216 us (0.47)
  blocking collectives: 134 us -> 18.1 us
  other arithmetic: 102 us -> 11.8 us
  Pallas kernels: 0 us -> 81 us
  local copies, waits for them, and re-layouts: 83.4 us -> 4.13 us
  waiting for transfers between devices: 71.2 us -> 49 us
  matrix products: 8.74 us -> 0 us
  starting transfers between devices: 55.5 us -> 50.5 us
    pallas_call x0 -> x4, Pallas kernels: none -> 81 us  [the longest x1 40.6 us: final(): pl.pallas_call(final_kernel, grid=(scans,), in_specs=[pl.BlockSpec((1, ro...]
    psum x1 -> x0, blocking collectives: 78.1 us -> none  [body(): height_all, slope_all = lax.psum((height_sq, slope_sum), ('row', 'col'))]
    all_gather x2 -> x0, blocking collectives: 55.5 us -> none  [the longest x1 27.9 us: long_cols(): portion = lax.all_gather(coarse, 'col', axis=2, tiled=True)]
    concatenate x4 -> x0, other arithmetic: 37.5 us -> none  [with_halo(): value = jnp.concatenate([before, value, after], axis=dim)]
    ppermute x16 -> x10, starting transfers between devices: 55.5 us -> 27.2 us  [the longest x1 4.39 us: body(): lcols = lax.ppermute(right, 'col', col_down)]
    reduce_sum x4, other arithmetic: 26.5 us -> 1.73 us  [the longest x2 0.81 us: long_matrix(): jnp.sum(gauss(jnp.arange(count, dtype=jnp.int32)[:, None] - tgt[None, :])...]
    ppermute x16 -> x10, waiting for transfers between devices: 71.2 us -> 47.5 us  [the longest x1 19.7 us: body(): up = lax.ppermute(bot, 'row', row_down)]
    all_to_all x0 -> x2, starting transfers between devices: none -> 23.3 us  [the longest x1 16.6 us: body(): z = lax.all_to_all(z, 'row', 0, 0, tiled=True)]
  transfers between devices with their start and end apart: 16 -> 12, of which waited for: 9 -> 9; matrix products, arithmetic and copies ran while one was open for 4% -> 5% of each run, Pallas kernels for 0% -> 0%
where the time goes in v1:
time: 216 us
  Pallas kernels  81 us (38%)
  starting transfers between devices  50.5 us (23%)
  waiting for transfers between devices  49 us (23%)
  blocking collectives  18.1 us (8%)
  other arithmetic  11.8 us (5%)
  local copies, waits for them, and re-layouts  4.13 us (2%)
    pallas_call x1, Pallas kernels, final(): pl.pallas_call(final_kernel, grid=(scans,), in_specs=[pl.BlockSpec((1, ro...  40.6 us
    pallas_call x1, Pallas kernels, resample(): pl.pallas_call(resample_kernel, in_specs=[smem, smem, vmem, vmem, vmem] +...  31.5 us
    ppermute x1, waiting for transfers between devices, body(): up = lax.ppermute(bot, 'row', row_down)  19.7 us
    all_to_all x1, blocking collectives, body(): every = lax.all_to_all(mine, ('row', 'col'), 0, 0, tiled=True)  18.1 us
    all_to_all x1, starting transfers between devices, body(): z = lax.all_to_all(z, 'row', 0, 0, tiled=True)  16.6 us
    ppermute x1, waiting for transfers between devices, body(): lcols = lax.ppermute(right, 'col', col_down)  12 us
    all_to_all x1, starting transfers between devices, body(): y = lax.all_to_all(y, 'col', 0, 0, tiled=True)  6.74 us
    pallas_call x1, Pallas kernels, pack(): pl.pallas_call(pack_kernel, grid=(scans,), in_specs=[pl.BlockSpec(memory_...  5.2 us
  transfers between devices with their start and end apart: 12, of which 9 were waited for; matrix products, arithmetic and copies ran while one was open for 5% of the time, Pallas kernels for 0%

profile of v1, /device:TPU:1, one launch (start us, length us, event | category | flops | bytes accessed | tf_op | source)
XLA Modules:
  0.0 215.6 jit_solution(9879460952602132799)
XLA Ops:
  0.6 5.2 %pack.1 = (f32[4,8,136,128]{3,2,1,0:T(8,128)}, f32[4,8,136,128]{3,2,1,0:T(8,128)}, f32[4,136,256]{2,1,0:T(8,128)}, f32[4,136,256]{2,1,0:T(8,128)}) custom-call(s32[2,4]{1,0:T(2,128)} %bitcast.6, f32[4,256,1024]{2,1,0:T(8,128)} %after.1), custom_call_target="tpu_custom_call" | custom-call | tf_op jit(solution)/shard_map/pack/pallas_call | solution.py:45
  5.8 4.4 %collective-permute-start.2 = (f32[4,136,256]{2,1,0:T(8,128)}, f32[4,136,256]{2,1,0:T(8,128)S(1)}, u32[]{:S(2)}, u32[]{:S(2)}) collective-permute-start(f32[4,136,256]{2,1,0:T(8,128)} %get-tuple-element.19), channel_id=1, source_target_pairs={{0,1},{1,2},{2,3},{3,4},{4,5},{5,6},{6,7},{8,9},{9,10},{10,11},{11... | collective-permute-start | bytes 1671176 | tf_op jit(solution)/shard_map/ppermute | solution.py:526
  10.2 1.3 collective-permute-start.3
  11.5 4.0 %collective-permute-start = (f32[4,8,136,128]{3,2,1,0:T(8,128)}, f32[4,8,136,128]{3,2,1,0:T(8,128)S(1)}, u32[]{:S(2)}, u32[]{:S(2)}) collective-permute-start(f32[4,8,136,128]{3,2,1,0:T(8,128)} %get-tuple-element.17), channel_id=1, source_target_pairs={{0,8},{8,16},{16,24},{24,32},{32,40},{40,48},{48,56},{56,64},{64,7... | collective-permute-start | bytes 6684680 | tf_op jit(solution)/shard_map/ppermute | solution.py:524
  15.5 1.9 collective-permute-start.1
  17.9 0.1 min.33
  18.2 0.1 exponential_reduce_fusion.1
  18.4 0.7 exponential_reduce_fusion
  19.1 0.7 divide_select_fusion.2.inv_ref
  19.8 0.7 select_add_fusion.3.rm_ref
  20.5 19.7 %collective-permute-done.up = f32[4,8,136,128]{3,2,1,0:T(8,128)S(1)} collective-permute-done((f32[4,8,136,128]{3,2,1,0:T(8,128)}, f32[4,8,136,128]{3,2,1,0:T(8,128)S(1)}, u32[]{:S(2)}, u32[]{:S(2)}) %collective-permute-start) | collective-permute-done | bytes 2228256 | tf_op jit(solution)/shard_map/ppermute | solution.py:524
  40.2 0.1 fusion.203
  40.3 4.5 %collective-permute-done.1.dn = f32[4,8,136,128]{3,2,1,0:T(8,128)} collective-permute-done((f32[4,8,136,128]{3,2,1,0:T(8,128)}, f32[4,8,136,128]{3,2,1,0:T(8,128)}, u32[]{:S(2)}, u32[]{:S(2)}) %collective-permute-start.1) | collective-permute-done | bytes 2228256 | tf_op jit(solution)/shard_map/ppermute | solution.py:525
  44.8 0.8 fusion.202
  45.6 12.0 %collective-permute-done.2.lcols = f32[4,136,256]{2,1,0:T(8,128)S(1)} collective-permute-done((f32[4,136,256]{2,1,0:T(8,128)}, f32[4,136,256]{2,1,0:T(8,128)S(1)}, u32[]{:S(2)}, u32[]{:S(2)}) %collective-permute-start.2) | collective-permute-done | bytes 557088 | tf_op jit(solution)/shard_map/ppermute | solution.py:526
  57.6 0.1 compare_select_fusion
  57.8 3.5 %collective-permute-start.5 = (f32[4,136,256]{2,1,0:T(8,128)S(1)}, f32[4,136,256]{2,1,0:T(8,128)S(1)}, u32[]{:S(2)}, u32[]{:S(2)}) collective-permute-start(f32[4,136,256]{2,1,0:T(8,128)S(1)} %get-tuple-element.31), channel_id=1, source_target_pairs={{8,0},{16,8},{24,16},{32,24},{40,32},{48,40},{56,48},{64,56},{72,6... | collective-permute-start | bytes 1671176 | tf_op jit(solution)/shard_map/ppermute | solution.py:533
  61.2 2.1 collective-permute-start.4
  63.3 1.1 divide_select_fusion.hc_ref
  64.4 3.4 %select_add_fusion.2.cm_ref = f32[1024,128]{1,0:T(8,128)} fusion(f32[1024]{0:T(1024)S(1)} %get-tuple-element.43, f32[1024]{0:T(1024)S(1)} %get-tuple-element.44, f32[1024]{0:T(1024)S(1)} %get-tuple-element.45, f32[1024]{0:T(1024)S(1)} %get-tuple-element.46, f32[1024]{0:T(1024)S(1)} %get-tuple-element.47, f32[1024]{0:T(1024)S(1)} %get-tuple-element.48, ...), kind=kLoop, calls=%fused_computation.20 | loop fusion | flops 4587520 | bytes 598656 | tf_op jit(solution)/shard_map/add | solution.py:475
  67.8 0.8 collective-permute-done.5.cdn
  68.6 1.2 collective-permute-done.4.cup
  69.8 0.8 copy-done.6
  70.6 31.5 %resample.1 = (f32[4,256,1024]{2,1,0:T(8,128)}, f32[4,8,256]{2,1,0:T(8,128)}, f32[4,8,256]{2,1,0:T(8,128)}, f32[8,4,24,128]{3,2,1,0:T(8,128)}) custom-call(s32[2,4]{1,0:T(2,128)} %bitcast.7, s32[2,4]{1,0:T(2,128)} %bitcast.8, f32[1024,128]{1,0:T(8,128)} %select_add_fusion.2.cm_ref, f32[24,256]{1,0:T(8,128)} %select_add_fusion.3.rm_ref, ...), custom_call_target="tpu_custom_call" | custom-call | tf_op jit(solution)/shard_map/resample/pallas_call | solution.py:205
  102.1 6.7 %all-to-all-start = ((f32[8,4,24,128]{3,2,1,0:T(8,128)}), f32[8,4,24,128]{3,2,1,0:T(8,128)S(1)}, u32[]{:S(2)}, u32[]{:S(2)}) async-start(f32[8,4,24,128]{3,2,1,0:T(8,128)} %get-tuple-element.24), calls=%async_computation | async-start | bytes 786432 | tf_op jit(solution)/shard_map/all_to_all | solution.py:560
  108.9 0.8 divide_select_fusion.1.hr_ref
  109.7 3.4 %collective-permute-start.6 = (f32[4,8,256]{2,1,0:T(8,128)}, f32[4,8,256]{2,1,0:T(8,128)S(1)}, u32[]{:S(2)}, u32[]{:S(2)}) collective-permute-start(f32[4,8,256]{2,1,0:T(8,128)} %get-tuple-element.22), channel_id=1, source_target_pairs={{0,1},{1,2},{2,3},{3,4},{4,5},{5,6},{6,7},{8,9},{9,10},{10,11},{11... | collective-permute-start | bytes 98312 | tf_op jit(solution)/shard_map/ppermute | solution.py:558
  113.1 1.3 collective-permute-start.7
  114.4 3.5 %collective-permute-done.7.rref = f32[4,8,256]{2,1,0:T(8,128)S(1)} collective-permute-done((f32[4,8,256]{2,1,0:T(8,128)}, f32[4,8,256]{2,1,0:T(8,128)S(1)}, u32[]{:S(2)}, u32[]{:S(2)}) %collective-permute-start.7) | collective-permute-done | bytes 32800 | tf_op jit(solution)/shard_map/ppermute | solution.py:559
  118.0 0.6 copy-done.10
  118.5 0.1 copy-done.4
  118.7 3.7 %strips.1 = (f32[16,4,24,128]{3,2,1,0:T(8,128)}, f32[4,10,8,128]{3,2,1,0:T(8,128)}, f32[4,10,8,128]{3,2,1,0:T(8,128)}) custom-call(f32[8,4,24,128]{3,2,1,0:T(8,128)} %copy-done.4, f32[384,24]{1,0:T(8,128)} %divide_select_fusion.1.hr_ref, f32[4,256,1024]{2,1,0:T(8,128)} %get-tuple-element.21.top_ref.bot_ref.diff_ref, ...), custom_call_target="tpu_custom_call" | custom-call | tf_op jit(solution)/shard_map/strips/pallas_call | solution.py:302
  122.4 16.6 %all-to-all-start.1 = ((f32[16,4,24,128]{3,2,1,0:T(8,128)}), f32[16,4,24,128]{3,2,1,0:T(8,128)S(1)}, u32[]{:S(2)}, u32[]{:S(2)}) async-start(f32[16,4,24,128]{3,2,1,0:T(8,128)} %get-tuple-element.27), calls=%async_computation.1 | async-start | bytes 1572864 | tf_op jit(solution)/shard_map/all_to_all | solution.py:564
  139.0 1.1 fusion.8.uc_ref
  140.0 3.5 %collective-permute-start.8 = (f32[4,10,8,128]{3,2,1,0:T(8,128)S(1)}, f32[4,10,8,128]{3,2,1,0:T(8,128)S(1)}, u32[]{:S(2)}, u32[]{:S(2)}) collective-permute-start(f32[4,10,8,128]{3,2,1,0:T(8,128)S(1)} %copy-done.12), channel_id=1, source_target_pairs={{0,8},{8,16},{16,24},{24,32},{32,40},{40,48},{48,56},{56,64},{64,7... | collective-permute-start | bytes 491528 | tf_op jit(solution)/shard_map/ppermute | solution.py:562
  143.6 1.9 collective-permute-start.9
  145.5 0.6 and_convert_fusion.mc_ref
  146.1 3.7 %collective-permute-done.8.upr = f32[4,10,8,128]{3,2,1,0:T(8,128)S(1)} collective-permute-done((f32[4,10,8,128]{3,2,1,0:T(8,128)S(1)}, f32[4,10,8,128]{3,2,1,0:T(8,128)S(1)}, u32[]{:S(2)}, u32[]{:S(2)}) %collective-permute-start.8) | collective-permute-done | bytes 163872 | tf_op jit(solution)/shard_map/ppermute | solution.py:562
  149.8 2.1 collective-permute-done.9.dnr
  152.0 1.5 all-to-all-done.1.z_ref
  153.4 0.9 broadcast_in_dim.667.mr_ref
  154.3 0.7 broadcast_in_dim.666.invr_ref
  155.1 40.6 %final.1 = (f32[4,256,1024]{2,1,0:T(8,128)}, f32[4,256,1024]{2,1,0:T(8,128)}, f32[4,2,128]{2,1,0:T(2,128)}) custom-call(f32[4,256,1024]{2,1,0:T(8,128)} %get-tuple-element.21.top_ref.bot_ref.diff_ref, f32[4,8,256]{2,1,0:T(8,128)} %copy-done.9, f32[4,8,256]{2,1,0:T(8,128)} %copy-done.10, f32[4,10,8,128]{3,2,1,0:T(8,128)} %copy-done.7, ...), custom_call_target="tpu_custom_call" | custom-call | tf_op jit(solution)/shard_map/final/pallas_call | solution.py:421
  195.7 0.8 reduce_sum.38
  196.5 0.1 copy.12
  196.7 18.1 %all_to_all.15 = f32[128,1,8]{2,1,0:T(1,128)S(1)} all-to-all(f32[128,1,8]{2,1,0:T(1,128)S(1)} %broadcast_in_dim.669), channel_id=1, replica_groups=mesh['row'=16,'col'=8] {'row','col'}, dimensions={0} | all-to-all | bytes 8192 | tf_op jit(solution)/shard_map/all_to_all | solution.py:569
  214.8 0.2 reduce_sum.39
  214.9 0.7 sqrt.7
  (66 shorter events, 0.8 us)
Async XLA Ops:
  5.8 51.8 %collective-permute-start.2 = (f32[4,136,256]{2,1,0:T(8,128)}, f32[4,136,256]{2,1,0:T(8,128)S(1)}, u32[]{:S(2)}, u32[]{:S(2)}) collective-permute-start(f32[4,136,256]{2,1,0:T(8,128)} %get-tuple-element.19), channel_id=1, source_target_pairs={{0,1},{1,2},{2,3},{3,4},{4,5},{5,6},{6,7},{8,9},{9,10},{10,11},{11... | collective-permute-start | bytes 1671176 | tf_op jit(solution)/shard_map/ppermute | solution.py:526
  10.2 47.4 %collective-permute-start.3 = (f32[4,136,256]{2,1,0:T(8,128)}, f32[4,136,256]{2,1,0:T(8,128)S(1)}, u32[]{:S(2)}, u32[]{:S(2)}) collective-permute-start(f32[4,136,256]{2,1,0:T(8,128)} %get-tuple-element.20), channel_id=1, source_target_pairs={{1,0},{2,1},{3,2},{4,3},{5,4},{6,5},{7,6},{9,8},{10,9},{11,10},{12... | collective-permute-start | bytes 1671176 | tf_op jit(solution)/shard_map/ppermute | solution.py:527
  11.5 28.6 %collective-permute-start = (f32[4,8,136,128]{3,2,1,0:T(8,128)}, f32[4,8,136,128]{3,2,1,0:T(8,128)S(1)}, u32[]{:S(2)}, u32[]{:S(2)}) collective-permute-start(f32[4,8,136,128]{3,2,1,0:T(8,128)} %get-tuple-element.17), channel_id=1, source_target_pairs={{0,8},{8,16},{16,24},{24,32},{32,40},{40,48},{48,56},{56,64},{64,7... | collective-permute-start | bytes 6684680 | tf_op jit(solution)/shard_map/ppermute | solution.py:524
  15.5 29.3 %collective-permute-start.1 = (f32[4,8,136,128]{3,2,1,0:T(8,128)}, f32[4,8,136,128]{3,2,1,0:T(8,128)}, u32[]{:S(2)}, u32[]{:S(2)}) collective-permute-start(f32[4,8,136,128]{3,2,1,0:T(8,128)} %get-tuple-element.18), channel_id=1, source_target_pairs={{8,0},{16,8},{24,16},{32,24},{40,32},{48,40},{56,48},{64,56},{72,6... | collective-permute-start | bytes 6684680 | tf_op jit(solution)/shard_map/ppermute | solution.py:525
  40.2 29.6 %copy-start.1 = (f32[4,8,136,128]{3,2,1,0:T(8,128)}, f32[4,8,136,128]{3,2,1,0:T(8,128)S(1)}, u32[]{:S(2)}) copy-start(f32[4,8,136,128]{3,2,1,0:T(8,128)S(1)} %collective-permute-done.up) | copy-start | bytes 6684676
  57.6 12.2 %copy-start.2 = (f32[4,136,256]{2,1,0:T(8,128)}, f32[4,136,256]{2,1,0:T(8,128)S(1)}, u32[]{:S(2)}) copy-start(f32[4,136,256]{2,1,0:T(8,128)S(1)} %collective-permute-done.2.lcols) | copy-start | bytes 1671172
  57.6 12.2 %copy-start.3 = (f32[4,136,256]{2,1,0:T(8,128)}, f32[4,136,256]{2,1,0:T(8,128)S(1)}, u32[]{:S(2)}) copy-start(f32[4,136,256]{2,1,0:T(8,128)S(1)} %collective-permute-done.3.rcols) | copy-start | bytes 1671172
  57.8 10.9 %collective-permute-start.5 = (f32[4,136,256]{2,1,0:T(8,128)S(1)}, f32[4,136,256]{2,1,0:T(8,128)S(1)}, u32[]{:S(2)}, u32[]{:S(2)}) collective-permute-start(f32[4,136,256]{2,1,0:T(8,128)S(1)} %get-tuple-element.31), channel_id=1, source_target_pairs={{8,0},{16,8},{24,16},{32,24},{40,32},{48,40},{56,48},{64,56},{72,6... | collective-permute-start | bytes 1671176 | tf_op jit(solution)/shard_map/ppermute | solution.py:533
  61.2 8.6 %collective-permute-start.4 = (f32[4,136,256]{2,1,0:T(8,128)S(1)}, f32[4,136,256]{2,1,0:T(8,128)S(1)}, u32[]{:S(2)}, u32[]{:S(2)}) collective-permute-start(f32[4,136,256]{2,1,0:T(8,128)S(1)} %get-tuple-element.32), channel_id=1, source_target_pairs={{0,8},{8,16},{16,24},{24,32},{32,40},{40,48},{48,56},{56,64},{64,7... | collective-permute-start | bytes 1671176 | tf_op jit(solution)/shard_map/ppermute | solution.py:532
  68.6 1.2 copy-start.5
  69.8 0.8 copy-start.6
  102.1 15.8 %all-to-all-start = ((f32[8,4,24,128]{3,2,1,0:T(8,128)}), f32[8,4,24,128]{3,2,1,0:T(8,128)S(1)}, u32[]{:S(2)}, u32[]{:S(2)}) async-start(f32[8,4,24,128]{3,2,1,0:T(8,128)} %get-tuple-element.24), calls=%async_computation | async-start | bytes 786432 | tf_op jit(solution)/shard_map/all_to_all | solution.py:560
  109.7 4.7 %collective-permute-start.6 = (f32[4,8,256]{2,1,0:T(8,128)}, f32[4,8,256]{2,1,0:T(8,128)S(1)}, u32[]{:S(2)}, u32[]{:S(2)}) collective-permute-start(f32[4,8,256]{2,1,0:T(8,128)} %get-tuple-element.22), channel_id=1, source_target_pairs={{0,1},{1,2},{2,3},{3,4},{4,5},{5,6},{6,7},{8,9},{9,10},{10,11},{11... | collective-permute-start | bytes 98312 | tf_op jit(solution)/shard_map/ppermute | solution.py:558
  113.1 4.9 %collective-permute-start.7 = (f32[4,8,256]{2,1,0:T(8,128)}, f32[4,8,256]{2,1,0:T(8,128)S(1)}, u32[]{:S(2)}, u32[]{:S(2)}) collective-permute-start(f32[4,8,256]{2,1,0:T(8,128)} %get-tuple-element.23), channel_id=1, source_target_pairs={{1,0},{2,1},{3,2},{4,3},{5,4},{6,5},{7,6},{9,8},{10,9},{11,10},{12... | collective-permute-start | bytes 98312 | tf_op jit(solution)/shard_map/ppermute | solution.py:559
  114.4 3.5 %copy-start.9 = (f32[4,8,256]{2,1,0:T(8,128)}, f32[4,8,256]{2,1,0:T(8,128)S(1)}, u32[]{:S(2)}) copy-start(f32[4,8,256]{2,1,0:T(8,128)S(1)} %collective-permute-done.6.lref) | copy-start | bytes 98308
  117.9 0.6 copy-start.10
  117.9 0.8 copy-start.4
  122.4 17.7 %copy-start.12 = (f32[4,10,8,128]{3,2,1,0:T(8,128)S(1)}, f32[4,10,8,128]{3,2,1,0:T(8,128)}, u32[]{:S(2)}) copy-start(f32[4,10,8,128]{3,2,1,0:T(8,128)} %get-tuple-element.25) | copy-start | bytes 491524
  122.4 21.2 %copy-start.11 = (f32[4,10,8,128]{3,2,1,0:T(8,128)S(1)}, f32[4,10,8,128]{3,2,1,0:T(8,128)}, u32[]{:S(2)}) copy-start(f32[4,10,8,128]{3,2,1,0:T(8,128)} %get-tuple-element.26) | copy-start | bytes 491524
  122.4 31.1 %all-to-all-start.1 = ((f32[16,4,24,128]{3,2,1,0:T(8,128)}), f32[16,4,24,128]{3,2,1,0:T(8,128)S(1)}, u32[]{:S(2)}, u32[]{:S(2)}) async-start(f32[16,4,24,128]{3,2,1,0:T(8,128)} %get-tuple-element.27), calls=%async_computation.1 | async-start | bytes 1572864 | tf_op jit(solution)/shard_map/all_to_all | solution.py:564
  140.0 9.8 %collective-permute-start.8 = (f32[4,10,8,128]{3,2,1,0:T(8,128)S(1)}, f32[4,10,8,128]{3,2,1,0:T(8,128)S(1)}, u32[]{:S(2)}, u32[]{:S(2)}) collective-permute-start(f32[4,10,8,128]{3,2,1,0:T(8,128)S(1)} %copy-done.12), channel_id=1, source_target_pairs={{0,8},{8,16},{16,24},{24,32},{32,40},{40,48},{48,56},{56,64},{64,7... | collective-permute-start | bytes 491528 | tf_op jit(solution)/shard_map/ppermute | solution.py:562
  143.6 8.4 %collective-permute-start.9 = (f32[4,10,8,128]{3,2,1,0:T(8,128)S(1)}, f32[4,10,8,128]{3,2,1,0:T(8,128)S(1)}, u32[]{:S(2)}, u32[]{:S(2)}) collective-permute-start(f32[4,10,8,128]{3,2,1,0:T(8,128)S(1)} %copy-done.11), channel_id=1, source_target_pairs={{8,0},{16,8},{24,16},{32,24},{40,32},{48,40},{56,48},{64,56},{72,6... | collective-permute-start | bytes 491528 | tf_op jit(solution)/shard_map/ppermute | solution.py:563
  149.8 5.2 %copy-start.7 = (f32[4,10,8,128]{3,2,1,0:T(8,128)}, f32[4,10,8,128]{3,2,1,0:T(8,128)S(1)}, u32[]{:S(2)}) copy-start(f32[4,10,8,128]{3,2,1,0:T(8,128)S(1)} %collective-permute-done.8.upr) | copy-start | bytes 491524
  152.0 3.1 %copy-start.8 = (f32[4,10,8,128]{3,2,1,0:T(8,128)}, f32[4,10,8,128]{3,2,1,0:T(8,128)S(1)}, u32[]{:S(2)}) copy-start(f32[4,10,8,128]{3,2,1,0:T(8,128)S(1)} %collective-permute-done.9.dnr) | copy-start | bytes 491524
  153.4 1.6 copy-start

commit v2 on v1

v2 whole, which is shorter than its diff:
```python
import math

import jax
import jax.numpy as jnp
from jax import lax
from jax.experimental import pallas as pl
from jax.experimental.pallas import tpu as pltpu
from jax.sharding import PartitionSpec as P

LS = 5
SR = 4
LCUT = 1600
BLOCK = 16
ALPHA = math.sqrt(math.log(2.0) / math.pi)
EPSILON = 1e-06
HIGHEST = lax.Precision.HIGHEST
HALO = 136
EDGE = 8
LANES = 128
TAPS = [math.exp(-math.pi * (k / (ALPHA * LS)) ** 2) for k in range(-SR, SR + 1)]
VMEM_LIMIT = 56 * 1024 * 1024


def lane_iota(rows):
    return lax.broadcasted_iota(jnp.int32, (rows, LANES), 1)


def pack_kernel(offs_ref, x_ref, top_ref, bot_ref, left_ref, right_ref):
    s = pl.program_id(0)
    shift = offs_ref[1, s].astype(jnp.float32)
    rows, cols = x_ref.shape[1], x_ref.shape[2]
    for j in range(cols // LANES):
        sl = slice(j * LANES, (j + 1) * LANES)
        top_ref[0, j] = x_ref[0, 0:HALO, sl]
        bot_ref[0, j] = x_ref[0, rows - HALO : rows, sl]
    top_ref[0, 0, HALO - 1 : HALO, :] = jnp.full((1, LANES), shift, jnp.float32)
    bot_ref[0, 0, 0:1, :] = jnp.full((1, LANES), shift, jnp.float32)
    left_ref[0] = x_ref[0, :, 0:256].T[0:HALO, :]
    right_ref[0] = x_ref[0, :, cols - 256 : cols].T[256 - HALO : 256, :]


def pack(after, offs):
    scans, rows, cols = after.shape
    n_tiles = cols // LANES
    return pl.pallas_call(
        pack_kernel,
        grid=(scans,),
        in_specs=[
            pl.BlockSpec(memory_space=pltpu.SMEM),
            pl.BlockSpec((1, rows, cols), lambda s: (s, 0, 0)),
        ],
        out_specs=[
            pl.BlockSpec((1, n_tiles, HALO, LANES), lambda s: (s, 0, 0, 0)),
            pl.BlockSpec((1, n_tiles, HALO, LANES), lambda s: (s, 0, 0, 0)),
            pl.BlockSpec((1, HALO, rows), lambda s: (s, 0, 0)),
            pl.BlockSpec((1, HALO, rows), lambda s: (s, 0, 0)),
        ],
        out_shape=[
            jax.ShapeDtypeStruct((scans, n_tiles, HALO, LANES), jnp.float32),
            jax.ShapeDtypeStruct((scans, n_tiles, HALO, LANES), jnp.float32),
            jax.ShapeDtypeStruct((scans, HALO, rows), jnp.float32),
            jax.ShapeDtypeStruct((scans, HALO, rows), jnp.float32),
        ],
        name="pack",
    )(offs, after)


def flip_kernel(x_ref, o_ref):
    rows, cols = x_ref.shape[1], x_ref.shape[2]
    for j in range(cols // LANES):
        for h in range(rows // LANES):
            block = x_ref[0, h * LANES : (h + 1) * LANES, j * LANES : (j + 1) * LANES]
            o_ref[0, h, j * LANES : (j + 1) * LANES, :] = block.T


def flip(x):
    scans, rows, cols = x.shape
    halves = rows // LANES
    return pl.pallas_call(
        flip_kernel,
        grid=(scans,),
        in_specs=[pl.BlockSpec((1, rows, cols), lambda s: (s, 0, 0))],
        out_specs=pl.BlockSpec((1, halves, cols, LANES), lambda s: (s, 0, 0, 0)),
        out_shape=jax.ShapeDtypeStruct((scans, halves, cols, LANES), jnp.float32),
        cost_estimate=pl.CostEstimate(
            flops=x.size, bytes_accessed=8 * x.size, transcendentals=0
        ),
        name="flip",
    )(x)


def scalar_taps(fraction):
    t = fraction.astype(jnp.float32) * (1.0 / 256.0)
    t2 = t * t
    t3 = t2 * t
    return (
        0.5 * (2.0 * t2 - t3 - t),
        0.5 * (3.0 * t3 - 5.0 * t2 + 2.0),
        0.5 * (4.0 * t2 - 3.0 * t3 + t),
        0.5 * (t3 - t2),
    )


CB = 64


def resample_kernel(
    offs_ref, fracs_ref, wt_ref, rm_ref, hc_ref,
    after, beforet, up, dn, lcols, rcols, cup, cdn,
    diff_out, edge_l, edge_r, y_ref,
    win, stage, bef, dif, rowsum, sums, part, sem, bsem, osem,
):
    scans, n_tiles = win.shape[0], win.shape[1]
    halves, cols = bef.shape[1], bef.shape[2]
    rows = halves * LANES
    n_out = cols // LANES
    left = 2 * LANES

    def copies(s):
        return [
            (after.at[s, :, pl.ds(j * LANES, LANES)], win.at[s, 2 + j, pl.ds(HALO, rows), :])
            for j in range(n_out)
        ] + [
            (up.at[s], win.at[s, pl.ds(2, n_out), pl.ds(0, HALO), :]),
            (dn.at[s], win.at[s, pl.ds(2, n_out), pl.ds(HALO + rows, HALO), :]),
            (lcols.at[s], stage.at[s, 0, pl.ds(256 - HALO, HALO), :]),
            (rcols.at[s], stage.at[s, 1, pl.ds(0, HALO), :]),
            (cup.at[s], stage.at[s, 2, pl.ds(256 - HALO, HALO), :]),
            (cup.at[s], stage.at[s, 3, pl.ds(0, HALO), :]),
            (cdn.at[s], stage.at[s, 4, pl.ds(256 - HALO, HALO), :]),
            (cdn.at[s], stage.at[s, 5, pl.ds(0, HALO), :]),
        ]

    for s in range(scans):
        for n, (a, b) in enumerate(copies(s)):
            pltpu.make_async_copy(a, b, sem.at[s, n]).start()
        pltpu.make_async_copy(beforet.at[s], bef.at[s], bsem.at[s]).start()
    part[...] = jnp.zeros_like(part)
    sums[...] = jnp.zeros_like(sums)
    n_blocks = cols // BLOCK
    weight = [wt_ref[8 * i : 8 * i + 8, :] for i in range(8)]

    def one_scan(s, carry):
        for n, (a, b) in enumerate(copies(s)):
            pltpu.make_async_copy(a, b, sem.at[s, n]).wait()
        pltpu.make_async_copy(beforet.at[s], bef.at[s], bsem.at[s]).wait()
        dr = offs_ref[0, s]
        dc = offs_ref[1, s]

        def put(slot, first_tile, row0, cut):
            flipped = stage[s, slot].T
            for h in range(2):
                win[s, first_tile + h, row0 : row0 + cut.stop - cut.start, :] = flipped[
                    cut, h * LANES : (h + 1) * LANES
                ]

        def put_side(first_tile, slots):
            put(slots[0], first_tile, HALO, slice(0, rows))

            @pl.when(dr <= 0)
            def _():
                put(slots[1], first_tile, 0, slice(rows - HALO, rows))

            @pl.when(dr >= -1)
            def _():
                put(slots[2], first_tile, HALO + rows, slice(0, HALO))

        @pl.when(dc <= 0)
        def _():
            put_side(0, (0, 2, 4))

        @pl.when(dc >= -1)
        def _():
            put_side(2 + n_out, (1, 3, 5))

        rt = scalar_taps(fracs_ref[0, s])
        ct = scalar_taps(fracs_ref[1, s])
        r0 = HALO + dr - 1
        c0 = left + dc - 1
        k = lax.div(c0, LANES)
        r = c0 - k * LANES

        def row_taps(i, carry):
            outs = []
            for j in range(2):
                for h in range(halves):
                    first = r0 + h * LANES
                    acc = rt[0] * win[s, k + 2 * i + j, pl.ds(first, LANES), :]
                    for a in range(1, 4):
                        acc = acc + rt[a] * win[s, k + 2 * i + j, pl.ds(first + a, LANES), :]
                    outs.append(acc.T)
            for j in range(2):
                for h in range(halves):
                    at = pl.multiple_of((2 * i + j) * LANES, LANES)
                    rowsum[h, pl.ds(at, LANES), :] = outs[j * halves + h]
            return carry

        lax.fori_loop(0, (n_out + 2) // 2, row_taps, 0)

        def col_taps(i, carry):
            q0 = pl.multiple_of(i * CB, CB)
            for h in range(halves):
                acc = ct[0] * rowsum[h, pl.ds(r + q0, CB), :]
                for b in range(1, 4):
                    acc = acc + ct[b] * rowsum[h, pl.ds(r + q0 + b, CB), :]
                dif[s, h, pl.ds(q0, CB), :] = bef[s, h, pl.ds(q0, CB), :] - acc
            return carry

        lax.fori_loop(0, cols // CB, col_taps, 0)
        pltpu.make_async_copy(dif.at[s], diff_out.at[s], osem.at[s]).start()
        for h in range(halves):
            edge_l[s, h] = dif[s, h, 0:EDGE, :]
            edge_r[s, h] = dif[s, h, cols - EDGE : cols, :]

        def block_sums(i, carry):
            for h in range(halves):
                total = []
                for e in range(8):
                    q = pl.multiple_of(i * LANES + e * BLOCK, BLOCK)
                    qa = pl.multiple_of(jnp.maximum(q - 8, 0), 8)
                    qb = pl.multiple_of(jnp.minimum(q + 16, cols - 8), 8)
                    t = weight[0] * dif[s, h, pl.ds(qa, 8), :]
                    t = t + weight[1] * dif[s, h, pl.ds(q, 8), :]
                    t = t + weight[2] * dif[s, h, pl.ds(q + 8, 8), :]
                    t = t + weight[3] * dif[s, h, pl.ds(qb, 8), :]
                    total.append(jnp.sum(t, axis=0, keepdims=True))
                at = pl.multiple_of(i * 8 + 8, 8)
                sums[pl.ds(at, 8), h * LANES : (h + 1) * LANES] = jnp.concatenate(total, axis=0)
            return carry

        lax.fori_loop(0, n_blocks // 8, block_sums, 0)
        for h in range(halves):
            sl = slice(h * LANES, (h + 1) * LANES)
            v = [dif[s, h, 8 * i : 8 * i + 8, :] for i in range(3)]
            w = [dif[s, h, cols - 24 + 8 * i : cols - 16 + 8 * i, :] for i in range(3)]
            rows_at = (
                (7, weight[4] * v[0]),
                (8, weight[5] * v[0] + weight[2] * v[1] + weight[3] * v[2]),
                (7 + n_blocks, weight[0] * w[0] + weight[1] * w[1] + weight[6] * w[2]),
                (8 + n_blocks, weight[7] * w[2]),
            )
            for at, t in rows_at:
                sums[at : at + 1, sl] = jnp.sum(t, axis=0, keepdims=True)
        part[...] += jnp.dot(
            sums[...], rm_ref[s], precision=HIGHEST, preferred_element_type=jnp.float32
        )
        return carry

    lax.fori_loop(0, scans, one_scan, 0)
    y = jnp.dot(hc_ref[...], part[...], precision=HIGHEST, preferred_element_type=jnp.float32)
    ext = hc_ref.shape[0] // y_ref.shape[0]
    for t in range(y_ref.shape[0]):
        y_ref[t] = y[t * ext : (t + 1) * ext, :]
    for s in range(scans):
        pltpu.make_async_copy(dif.at[s], diff_out.at[s], osem.at[s]).wait()


def resample(offs, fracs, wt, rm, hc, ext, after, beforet, up, dn, lcols, rcols, cup, cdn):
    scans, rows, cols = after.shape
    halves = rows // LANES
    n_col = hc.shape[0] // ext
    anywhere = pl.BlockSpec(memory_space=pl.ANY)
    vmem = pl.BlockSpec(memory_space=pltpu.VMEM)
    smem = pl.BlockSpec(memory_space=pltpu.SMEM)
    return pl.pallas_call(
        resample_kernel,
        in_specs=[smem, smem, vmem, vmem, vmem] + [anywhere] * 8,
        out_specs=[anywhere, vmem, vmem, vmem],
        out_shape=[
            jax.ShapeDtypeStruct((scans, halves, cols, LANES), jnp.float32),
            jax.ShapeDtypeStruct((scans, halves, EDGE, LANES), jnp.float32),
            jax.ShapeDtypeStruct((scans, halves, EDGE, LANES), jnp.float32),
            jax.ShapeDtypeStruct((n_col, ext, LANES), jnp.float32),
        ],
        scratch_shapes=[
            pltpu.VMEM((scans, cols // LANES + 4, 2 * HALO + rows, LANES), jnp.float32),
            pltpu.VMEM((scans, 6, 256, rows), jnp.float32),
            pltpu.VMEM((scans, halves, cols, LANES), jnp.float32),
            pltpu.VMEM((scans, halves, cols, LANES), jnp.float32),
            pltpu.VMEM((halves, cols + 2 * LANES, LANES), jnp.float32),
            pltpu.VMEM((hc.shape[1], rows), jnp.float32),
            pltpu.VMEM((hc.shape[1], LANES), jnp.float32),
            pltpu.SemaphoreType.DMA((scans, cols // LANES + 8)),
            pltpu.SemaphoreType.DMA((scans,)),
            pltpu.SemaphoreType.DMA((scans,)),
        ],
        compiler_params=pltpu.CompilerParams(vmem_limit_bytes=VMEM_LIMIT),
        name="resample",
    )(offs, fracs, wt, rm, hc, after, beforet, up, dn, lcols, rcols, cup, cdn)


def long_rows_kernel(y_ref, hr_ref, z_ref):
    n_row, scans, ext, _ = z_ref.shape
    p = y_ref[0]
    for t in range(1, y_ref.shape[0]):
        p = p + y_ref[t]
    p = jnp.concatenate([p, jnp.zeros((LANES - p.shape[0], LANES), jnp.float32)], axis=0).T
    for s in range(scans):
        z = jnp.dot(
            hr_ref[...], p[s * ext : (s + 1) * ext, :],
            precision=HIGHEST, preferred_element_type=jnp.float32,
        )
        for t in range(n_row):
            z_ref[t, s] = z[t * ext : (t + 1) * ext, :]


def long_rows(y, hr, scans):
    ext = hr.shape[1]
    vmem = pl.BlockSpec(memory_space=pltpu.VMEM)
    return pl.pallas_call(
        long_rows_kernel,
        in_specs=[vmem, vmem],
        out_specs=vmem,
        out_shape=jax.ShapeDtypeStruct((hr.shape[0] // ext, scans, ext, LANES), jnp.float32),
        name="long_rows",
    )(y, hr)


PAD = 2 * EDGE


def across_kernel(invc_ref, diff, lstrip, rstrip, ac_out, ftop, fbot, buf, acs, sem, osem):
    scans, halves, cols = diff.shape[0], diff.shape[1], diff.shape[2]
    n_out = cols // LANES
    rows = halves * LANES

    def copies(s):
        return [
            (diff.at[s], buf.at[s, :, pl.ds(PAD, cols), :]),
            (lstrip.at[s], buf.at[s, :, pl.ds(PAD - EDGE, EDGE), :]),
            (rstrip.at[s], buf.at[s, :, pl.ds(PAD + cols, EDGE), :]),
        ]

    for s in range(scans):
        for n, (a, b) in enumerate(copies(s)):
            pltpu.make_async_copy(a, b, sem.at[s, n]).start()
    zero = jnp.zeros((LANES - EDGE, LANES), jnp.float32)

    def filtered(s, h, q, n):
        acc = TAPS[SR] * buf[s, h, pl.ds(q + PAD, n), :]
        for k in range(1, SR + 1):
            acc = acc + TAPS[SR + k] * (
                buf[s, h, pl.ds(q + PAD - k, n), :] + buf[s, h, pl.ds(q + PAD + k, n), :]
            )
        return acc

    def one_scan(s, carry):
        for n, (a, b) in enumerate(copies(s)):
            pltpu.make_async_copy(a, b, sem.at[s, n]).wait()
        for h in range(halves):
            buf[s, h, 0 : PAD - EDGE, :] = zero[0:EDGE]
            buf[s, h, PAD + cols + EDGE :, :] = zero[0:EDGE]
        for h in range(halves):
            sl = slice(h * LANES, (h + 1) * LANES)
            lo = filtered(s, h, -EDGE, EDGE) * invc_ref[0:EDGE, :]
            hi = filtered(s, h, cols, EDGE) * invc_ref[EDGE + cols : 2 * EDGE + cols, :]
            acs[s, 0, sl, :] = jnp.concatenate([zero, lo], axis=0).T
            acs[s, n_out + 1, sl, :] = jnp.concatenate([hi, zero], axis=0).T

        def block(i, carry):
            q0 = pl.multiple_of(i * LANES, LANES)
            inv = invc_ref[pl.ds(q0 + EDGE, LANES), :]
            outs = [(filtered(s, h, q0, LANES) * inv).T for h in range(halves)]
            for h in range(halves):
                acs[s, i + 1, h * LANES : (h + 1) * LANES, :] = outs[h]
            return carry

        lax.fori_loop(0, n_out, block, 0)
        pltpu.make_async_copy(acs.at[s], ac_out.at[s], osem.at[s]).start()
        for j in range(n_out + 2):
            ftop[s, j] = acs[s, j, 0:EDGE, :]
            fbot[s, j] = acs[s, j, rows - EDGE : rows, :]
        return carry

    lax.fori_loop(0, scans, one_scan, 0)
    for s in range(scans):
        pltpu.make_async_copy(acs.at[s], ac_out.at[s], osem.at[s]).wait()


def across(invc, diff, lstrip, rstrip):
    scans, halves, cols, _ = diff.shape
    rows = halves * LANES
    n_wide = cols // LANES + 2
    anywhere = pl.BlockSpec(memory_space=pl.ANY)
    vmem = pl.BlockSpec(memory_space=pltpu.VMEM)
    return pl.pallas_call(
        across_kernel,
        in_specs=[vmem, anywhere, anywhere, anywhere],
        out_specs=[anywhere, vmem, vmem],
        out_shape=[
            jax.ShapeDtypeStruct((scans, n_wide, rows, LANES), jnp.float32),
            jax.ShapeDtypeStruct((scans, n_wide, EDGE, LANES), jnp.float32),
            jax.ShapeDtypeStruct((scans, n_wide, EDGE, LANES), jnp.float32),
        ],
        scratch_shapes=[
            pltpu.VMEM((scans, halves, cols + 2 * PAD, LANES), jnp.float32),
            pltpu.VMEM((scans, n_wide, rows, LANES), jnp.float32),
            pltpu.SemaphoreType.DMA((scans, 3)),
            pltpu.SemaphoreType.DMA((scans,)),
        ],
        compiler_params=pltpu.CompilerParams(vmem_limit_bytes=VMEM_LIMIT),
        cost_estimate=pl.CostEstimate(
            flops=20 * diff.size, bytes_accessed=8 * diff.size, transcendentals=0
        ),
        name="across",
    )(invc, diff, lstrip, rstrip)


def final_kernel(
    z_ref, uc_ref, invr_ref, mc_ref, mr_ref, across_in, upr, dnr,
    band_ref, slope_ref, sum_ref,
    acs, cu, bd, sem,
):
    s = pl.program_id(0)
    scans, n_wide = acs.shape[0], acs.shape[1]
    rows, cols = band_ref.shape[1], band_ref.shape[2]
    n_out = cols // LANES

    def copies(s):
        return [
            (across_in.at[s], acs.at[s, :, pl.ds(PAD, rows), :]),
            (upr.at[s], acs.at[s, :, pl.ds(PAD - EDGE, EDGE), :]),
            (dnr.at[s], acs.at[s, :, pl.ds(PAD + rows, EDGE), :]),
        ]

    @pl.when(s == 0)
    def _():
        for t in range(scans):
            for n, (a, b) in enumerate(copies(t)):
                pltpu.make_async_copy(a, b, sem.at[t, n]).start()

        parts = []
        for t in range(scans):
            w = z_ref[0, t]
            for n in range(1, z_ref.shape[0]):
                w = w + z_ref[n, t]
            parts.append(w)
        w = jnp.concatenate(parts, axis=0)
        total = None
        for _ in range(3):
            piece = w.astype(jnp.bfloat16)
            w = w - piece.astype(jnp.float32)
            term = jnp.dot(piece, uc_ref[...], preferred_element_type=jnp.float32)
            total = term if total is None else total + term
        ext = cu.shape[2]
        for t in range(scans):
            for j in range(n_wide):
                cu[t, j] = total[t * ext : (t + 1) * ext, j * LANES : (j + 1) * LANES]

    for n, (a, b) in enumerate(copies(s)):
        pltpu.make_async_copy(a, b, sem.at[s, n]).wait()
    for j in range(n_wide):
        acs[s, j, 0 : PAD - EDGE, :] = jnp.zeros((PAD - EDGE, LANES), jnp.float32)
        acs[s, j, PAD + rows + EDGE :, :] = jnp.zeros((PAD - EDGE, LANES), jnp.float32)

    sub = lax.broadcasted_iota(jnp.int32, (BLOCK, LANES), 0).astype(jnp.float32)
    f = (2.0 * sub + 1.0) * (1.0 / 32.0)

    def band_rows(e, carry):
        base = pl.multiple_of(e * BLOCK, BLOCK)
        inv = invr_ref[pl.ds(base, BLOCK), :]
        for j in range(n_wide):
            acc = TAPS[SR] * acs[s, j, pl.ds(base + EDGE, BLOCK), :]
            for k in range(1, SR + 1):
                acc = acc + TAPS[SR + k] * (
                    acs[s, j, pl.ds(base + EDGE - k, BLOCK), :]
                    + acs[s, j, pl.ds(base + EDGE + k, BLOCK), :]
                )
            a = cu[s, j, pl.ds(e, 1), :]
            b = cu[s, j, pl.ds(e + 1, 1), :]
            bd[j, pl.ds(base, BLOCK), :] = acc * inv - (a + f * (b - a))
        return carry

    lax.fori_loop(0, rows // BLOCK + 1, band_rows, 0)

    lane = lane_iota(BLOCK)
    first = lane >= 1
    last = lane < LANES - 1

    def slope_rows(c, carry):
        s1, s2 = carry
        base = pl.multiple_of(c * BLOCK, BLOCK)
        here = [bd[j, pl.ds(base + EDGE, BLOCK), :] for j in range(n_wide)]
        fwd = [pltpu.roll(t, LANES - 1, 1) for t in here[1:]]
        bwd = [pltpu.roll(t, 1, 1) for t in here[:-1]]
        mr = mr_ref[pl.ds(base, BLOCK), :]
        for j in range(n_out):
            so = slice(j * LANES, (j + 1) * LANES)
            gc = jnp.where(last, fwd[j], fwd[j + 1]) - jnp.where(first, bwd[j + 1], bwd[j])
            gc = gc * mc_ref[0:1, so]
            gr = (
                bd[j + 1, pl.ds(base + EDGE + 1, BLOCK), :]
                - bd[j + 1, pl.ds(base + EDGE - 1, BLOCK), :]
            ) * mr
            sq = gc * gc + gr * gr
            v = here[j + 1]
            band_ref[0, pl.ds(base, BLOCK), so] = v
            slope_ref[0, pl.ds(base, BLOCK), so] = sq
            s1 = s1 + v * v
            s2 = s2 + sq
        return s1, s2

    zero = jnp.zeros((BLOCK, LANES), jnp.float32)
    s1, s2 = lax.fori_loop(0, rows // BLOCK, slope_rows, (zero, zero))
    sum_ref[0, 0:1, :] = jnp.sum(s1, axis=0, keepdims=True)
    sum_ref[0, 1:2, :] = jnp.sum(s2, axis=0, keepdims=True)


def final(z, uc, invr, mc, mr, ac, upr, dnr):
    scans, n_wide, rows, _ = ac.shape
    cols = mc.shape[1]
    n_row, _, ext, _ = z.shape
    const2 = lambda s: (0, 0)
    one = lambda s: (s, 0, 0)
    anywhere = pl.BlockSpec(memory_space=pl.ANY)
    return pl.pallas_call(
        final_kernel,
        grid=(scans,),
        in_specs=[
            pl.BlockSpec(z.shape, lambda s: (0, 0, 0, 0)),
            pl.BlockSpec(uc.shape, const2),
            pl.BlockSpec(invr.shape, const2),
            pl.BlockSpec(mc.shape, const2),
            pl.BlockSpec(mr.shape, const2),
            anywhere,
            anywhere,
            anywhere,
        ],
        out_specs=[
            pl.BlockSpec((1, rows, cols), one),
            pl.BlockSpec((1, rows, cols), one),
            pl.BlockSpec((1, 2, LANES), one),
        ],
        out_shape=[
            jax.ShapeDtypeStruct((scans, rows, cols), jnp.float32),
            jax.ShapeDtypeStruct((scans, rows, cols), jnp.float32),
            jax.ShapeDtypeStruct((scans, 2, LANES), jnp.float32),
        ],
        scratch_shapes=[
            pltpu.VMEM((scans, n_wide, rows + 2 * PAD, LANES), jnp.float32),
            pltpu.VMEM((scans, n_wide, ext, LANES), jnp.float32),
            pltpu.VMEM((n_wide, rows + 2 * EDGE, LANES), jnp.float32),
            pltpu.SemaphoreType.DMA((scans, 3)),
        ],
        compiler_params=pltpu.CompilerParams(vmem_limit_bytes=VMEM_LIMIT),
        name="final",
    )(z, uc, invr, mc, mr, ac, upr, dnr)


def window_weight(index, count):
    total = jnp.zeros(index.shape, jnp.float32)
    for k in range(-SR, SR + 1):
        inside = (index + k >= 0) & (index + k < count)
        total = total + jnp.where(inside, TAPS[k + SR], 0.0)
    return total


def mean_matrix(start, length, count, width):
    fine = start + lax.broadcasted_iota(jnp.int32, (length, 1), 0)
    blocks = start // BLOCK - 1 + lax.broadcasted_iota(jnp.int32, (1, width), 1)
    valid = lax.broadcasted_iota(jnp.int32, (1, width), 1) < length // BLOCK + 2
    total = jnp.zeros((length, width), jnp.float32)
    for k in range(-SR, SR + 1):
        other = fine + k
        inside = (other >= 0) & (other < count)
        coef = jnp.where(inside, TAPS[k + SR] / (BLOCK * window_weight(other, count)), 0.0)
        total = total + jnp.where((other // BLOCK == blocks) & valid, coef, 0.0)
    return total


def mean_weights(start, length, count):
    b = BLOCK
    cases = (
        (8 * b - 8, 8), (8 * b, 8), (8 * b + 8, 8), (9 * b, 8),
        (0, -1), (0, 0), (length - 8, length // b - 1), (length - 8, length // b),
    )
    base = jnp.array([c[0] for c in cases], jnp.int32)[:, None]
    block = jnp.array([c[1] for c in cases], jnp.int32)[:, None] + start // b
    fine = start + base + jnp.arange(8, dtype=jnp.int32)[None, :]
    total = jnp.zeros(fine.shape, jnp.float32)
    for k in range(-SR, SR + 1):
        other = fine + k
        inside = (other >= 0) & (other < count) & (other // b == block)
        total = total + jnp.where(inside, TAPS[k + SR] / (b * window_weight(other, count)), 0.0)
    return jnp.broadcast_to(total.reshape(64, 1), (64, LANES))


def gauss(distance):
    scaled = (distance * BLOCK).astype(jnp.float32) / (ALPHA * LCUT)
    return jnp.exp(-math.pi * scaled * scaled)


def long_matrix(start_block, per_tile, tiles, src_ext, src_first, ext):
    count = per_tile * tiles
    i = jnp.arange(src_ext, dtype=jnp.int32)
    src = start_block - src_first + i
    src_ok = (i >= src_first - 1) & (i <= src_first + per_tile)
    e = jnp.arange(ext, dtype=jnp.int32)
    tgt = (jnp.arange(tiles, dtype=jnp.int32)[:, None] * per_tile - 1 + e[None, :]).reshape(-1)
    tgt = jnp.clip(tgt, 0, count - 1)
    norm = jnp.sum(gauss(jnp.arange(count, dtype=jnp.int32)[None, :] - tgt[:, None]), axis=1)
    m = gauss(src[None, :] - tgt[:, None]) / norm[:, None]
    return jnp.where(src_ok[None, :], m, 0.0)


def upsample_cols(per_tile, wide):
    q = lax.broadcasted_iota(jnp.int32, (LANES, wide), 1) - LANES
    num = 2 * q + 1 - BLOCK
    low = num // (2 * BLOCK)
    frac = (num - low * (2 * BLOCK)).astype(jnp.float32) / (2.0 * BLOCK)
    e = lax.broadcasted_iota(jnp.int32, (LANES, wide), 0)
    near = (q >= -1) & (q <= per_tile * BLOCK)
    m = jnp.where(e == low + 1, 1.0 - frac, 0.0) + jnp.where(e == low + 2, frac, 0.0)
    return jnp.where(near, m, 0.0).astype(jnp.bfloat16)


def body(before_scan, after_scan, drift_offsets, drift_fractions):
    scans, rows, cols = before_scan.shape
    n_row, n_col = lax.axis_size("row"), lax.axis_size("col")
    row, col = lax.axis_index("row"), lax.axis_index("col")
    offs = drift_offsets.reshape(2, scans)
    fracs = drift_fractions.reshape(2, scans)
    row_down = [(i, i + 1) for i in range(n_row - 1)]
    row_up = [(j, i) for i, j in row_down]
    col_down = [(i, i + 1) for i in range(n_col - 1)]
    col_up = [(j, i) for i, j in col_down]

    top, bot, left, right = pack(after_scan, offs)
    up = lax.ppermute(bot, "row", row_down)
    dn = lax.ppermute(top, "row", row_up)
    lcols = lax.ppermute(right, "col", col_down)
    rcols = lax.ppermute(left, "col", col_up)

    slot = lax.broadcasted_iota(jnp.int32, lcols.shape, 1).astype(jnp.float32)
    for_up = jnp.where(slot < up[:, 0, 0:1, 0:1] + 2.0, rcols, lcols)
    for_dn = jnp.where(slot < dn[:, 0, HALO - 1 : HALO, 0:1] + 2.0, rcols, lcols)
    cup = lax.ppermute(for_dn, "row", row_down)
    cdn = lax.ppermute(for_up, "row", row_up)

    wide = cols + 2 * LANES
    ext_r, ext_c = 24, 72
    wt = mean_weights(col * cols, cols, n_col * cols)
    rm = mean_matrix(row * rows, rows, n_row * rows, ext_r)
    rm = jnp.stack([jnp.pad(rm, ((0, 0), (s * ext_r, LANES - (s + 1) * ext_r))) for s in range(scans)])
    hc = long_matrix(col * (cols // BLOCK), cols // BLOCK, n_col, cols // BLOCK + 16, 8, ext_c)
    hr = long_matrix(row * (rows // BLOCK), rows // BLOCK, n_row, ext_r, 1, ext_r)
    uc = upsample_cols(cols // BLOCK, wide)
    qg = col * cols - EDGE + jnp.arange(cols + 2 * EDGE, dtype=jnp.int32)
    near = (qg >= col * cols - 1) & (qg <= (col + 1) * cols)
    inv = jnp.where(near, 1.0 / jnp.where(near, window_weight(qg, n_col * cols), 1.0), 0.0)
    inv = jnp.broadcast_to(inv[:, None], (cols + 2 * EDGE, LANES))
    pg = row * rows - EDGE + jnp.arange(rows + 2 * EDGE, dtype=jnp.int32)
    nearr = (pg >= row * rows - 1) & (pg <= (row + 1) * rows)
    invr = jnp.where(nearr, 1.0 / jnp.where(nearr, window_weight(pg, n_row * rows), 1.0), 0.0)
    invr = jnp.broadcast_to(invr[:, None], (rows + 2 * EDGE, LANES))
    qi = col * cols + jnp.arange(cols, dtype=jnp.int32)
    mc = ((qi >= 1) & (qi <= n_col * cols - 2)).astype(jnp.float32)[None, :]
    pi = row * rows + jnp.arange(rows, dtype=jnp.int32)
    mr = ((pi >= 1) & (pi <= n_row * rows - 2)).astype(jnp.float32)
    mr = jnp.broadcast_to(mr[:, None], (rows, LANES))

    diff, edge_l, edge_r, y = resample(
        offs, fracs, wt, rm, hc, ext_c, after_scan, flip(before_scan), up, dn, lcols, rcols, cup, cdn
    )
    lstrip = lax.ppermute(edge_r, "col", col_down)
    rstrip = lax.ppermute(edge_l, "col", col_up)
    y = lax.all_to_all(y, "col", 0, 0, tiled=True)
    ac, ftop, fbot = across(inv, diff, lstrip, rstrip)
    y, ac, ftop, fbot = lax.optimization_barrier((y, ac, ftop, fbot))
    z = long_rows(y, hr, scans)
    upr = lax.ppermute(fbot, "row", row_down)
    dnr = lax.ppermute(ftop, "row", row_up)
    z = lax.all_to_all(z, "row", 0, 0, tiled=True)
    band, slope, sums = final(z, uc, invr, mc, mr, ac, upr, dnr)

    mine = jnp.sum(sums, axis=2).T.reshape(1, 2 * scans)
    mine = jnp.broadcast_to(mine[:, None, :], (n_row * n_col, 1, 2 * scans))
    every = lax.all_to_all(mine, ("row", "col"), 0, 0, tiled=True)
    total = jnp.sum(every, axis=(0, 1)).reshape(2, scans)
    cells = n_row * rows * n_col * cols
    return band, slope, jnp.sqrt(total / cells + EPSILON)


def solution(mesh):
    in_specs = (
        P(None, "row", "col"),
        P(None, "row", "col"),
        P(None, None, "row", "col"),
        P(None, None, "row", "col"),
    )
    out_specs = (P(None, "row", "col"), P(None, "row", "col"), P())
    return jax.shard_map(body, mesh=mesh, in_specs=in_specs, out_specs=out_specs, check_vma=False)
```

time: 216 us -> 184 us (0.85)
  Pallas kernels: 81 us -> 53.2 us
  starting transfers between devices: 50.5 us -> 42.8 us
  waiting for transfers between devices: 49 us -> 52.9 us
  other arithmetic: 11.8 us -> 8.38 us
    pallas_call x1, Pallas kernels: 31.5 us -> 15.4 us  [resample(): pl.pallas_call(resample_kernel, in_specs=[smem, smem, vmem, vmem, vmem] +...]
    ppermute x1, waiting for transfers between devices: 12 us -> 25.2 us  [body(): lcols = lax.ppermute(right, 'col', col_down)]
    all_to_all x1, starting transfers between devices: 16.6 us -> 3.51 us  [body(): z = lax.all_to_all(z, 'row', 0, 0, tiled=True)]
    pallas_call x2 -> x4, Pallas kernels: 44.3 us -> 32.6 us  [the longest x1 15.5 us: final(): pl.pallas_call(final_kernel, grid=(scans,), in_specs=[pl.BlockSpec(z.shap...]
    ppermute x1, waiting for transfers between devices: 19.7 us -> 10.9 us  [body(): up = lax.ppermute(bot, 'row', row_down)]
    all_to_all x1, starting transfers between devices: 6.74 us -> 12.9 us  [body(): y = lax.all_to_all(y, 'col', 0, 0, tiled=True)]
    ppermute x1, waiting for transfers between devices: 4.47 us -> 0.01 us  [body(): dn = lax.ppermute(top, 'row', row_up)]
    ppermute x1, waiting for transfers between devices: 0.79 us -> 4.39 us  [body(): cdn = lax.ppermute(for_up, 'row', row_up)]
  transfers between devices with their start and end apart: 12 -> 12, of which waited for: 9 -> 8; matrix products, arithmetic and copies ran while one was open for 5% -> 5% of each run, Pallas kernels for 0% -> 8%
where the time goes in v2:
time: 184 us; the launch traced here: 183 us
  Pallas kernels  53.2 us (29%)
  waiting for transfers between devices  52.9 us (29%)
  starting transfers between devices  42.8 us (23%)
  blocking collectives  18.6 us (10%)
  other arithmetic  8.38 us (5%)
  local copies, waits for them, and re-layouts  5.66 us (3%)
    ppermute x1, waiting for transfers between devices, body(): lcols = lax.ppermute(right, 'col', col_down)  25.2 us
    all_to_all x1, blocking collectives, body(): every = lax.all_to_all(mine, ('row', 'col'), 0, 0, tiled=True)  18.6 us
    pallas_call x1, Pallas kernels, final(): pl.pallas_call(final_kernel, grid=(scans,), in_specs=[pl.BlockSpec(z.shap...  15.5 us
    pallas_call x1, Pallas kernels, resample(): pl.pallas_call(resample_kernel, in_specs=[smem, smem, vmem, vmem, vmem] +...  15.4 us
    all_to_all x1, starting transfers between devices, body(): y = lax.all_to_all(y, 'col', 0, 0, tiled=True)  12.9 us
    ppermute x1, waiting for transfers between devices, body(): up = lax.ppermute(bot, 'row', row_down)  10.9 us
    pallas_call x1, Pallas kernels, across(): pl.pallas_call(across_kernel, in_specs=[vmem, anywhere, anywhere, anywher...  9.08 us
    pallas_call x1, Pallas kernels, flip(): pl.pallas_call(flip_kernel, grid=(scans,), in_specs=[pl.BlockSpec((1, row...  5.24 us
  transfers between devices with their start and end apart: 12, of which 8 were waited for; matrix products, arithmetic and copies ran while one was open for 5% of the time, Pallas kernels for 8%

profile of v2, /device:TPU:1, one launch (start us, length us, event | category | flops | bytes accessed | tf_op | source)
XLA Modules:
  0.0 182.6 jit_solution(8287177611939870308)
XLA Ops:
  0.7 5.2 %pack.1 = (f32[4,8,136,128]{3,2,1,0:T(8,128)}, f32[4,8,136,128]{3,2,1,0:T(8,128)}, f32[4,136,256]{2,1,0:T(8,128)}, f32[4,136,256]{2,1,0:T(8,128)}) custom-call(s32[2,4]{1,0:T(2,128)} %bitcast.12, f32[4,256,1024]{2,1,0:T(8,128)} %after.1), custom_call_target="tpu_custom_call" | custom-call | tf_op jit(solution)/shard_map/pack/pallas_call | solution.py:45
  5.9 3.3 %collective-permute-start.1 = (f32[4,8,136,128]{3,2,1,0:T(8,128)}, f32[4,8,136,128]{3,2,1,0:T(8,128)S(1)}, u32[]{:S(2)}, u32[]{:S(2)}) collective-permute-start(f32[4,8,136,128]{3,2,1,0:T(8,128)} %get-tuple-element.22), channel_id=1, source_target_pairs={{8,0},{16,8},{24,16},{32,24},{40,32},{48,40},{56,48},{64,56},{72,6... | collective-permute-start | bytes 6684680 | tf_op jit(solution)/shard_map/ppermute | solution.py:630
  9.2 3.1 %collective-permute-start = (f32[4,8,136,128]{3,2,1,0:T(8,128)}, f32[4,8,136,128]{3,2,1,0:T(8,128)}, u32[]{:S(2)}, u32[]{:S(2)}) collective-permute-start(f32[4,8,136,128]{3,2,1,0:T(8,128)} %get-tuple-element.21), channel_id=1, source_target_pairs={{0,8},{8,16},{16,24},{24,32},{32,40},{40,48},{48,56},{56,64},{64,7... | collective-permute-start | bytes 6684680 | tf_op jit(solution)/shard_map/ppermute | solution.py:629
  12.3 3.6 %collective-permute-start.2 = (f32[4,136,256]{2,1,0:T(8,128)}, f32[4,136,256]{2,1,0:T(8,128)S(1)}, u32[]{:S(2)}, u32[]{:S(2)}) collective-permute-start(f32[4,136,256]{2,1,0:T(8,128)} %get-tuple-element.23), channel_id=1, source_target_pairs={{0,1},{1,2},{2,3},{3,4},{4,5},{5,6},{6,7},{8,9},{9,10},{10,11},{11... | collective-permute-start | bytes 1671176 | tf_op jit(solution)/shard_map/ppermute | solution.py:631
  15.9 1.3 collective-permute-start.3
  17.9 5.2 %flip.1.beforet = f32[4,2,1024,128]{3,2,1,0:T(8,128)} custom-call(f32[4,256,1024]{2,1,0:T(8,128)} %x_ref.2), custom_call_target="tpu_custom_call" | custom-call | flops 1048576 | bytes 8388608 | tf_op jit(solution)/shard_map/flip/pallas_call | solution.py:79
  23.5 0.7 select_add_fusion.2
  24.2 0.2 pad_bitcast_fusion.3
  24.3 0.8 pad_maximum_fusion.rm_ref
  25.2 0.3 exponential_reduce_fusion.1
  25.4 0.6 exponential_reduce_fusion
  26.1 10.9 %collective-permute-done.up = f32[4,8,136,128]{3,2,1,0:T(8,128)} collective-permute-done((f32[4,8,136,128]{3,2,1,0:T(8,128)}, f32[4,8,136,128]{3,2,1,0:T(8,128)}, u32[]{:S(2)}, u32[]{:S(2)}) %collective-permute-start) | collective-permute-done | bytes 2228256 | tf_op jit(solution)/shard_map/ppermute | solution.py:629
  37.0 0.8 fusion.85
  37.8 0.1 fusion.84
  37.9 25.2 %collective-permute-done.2.lcols = f32[4,136,256]{2,1,0:T(8,128)S(1)} collective-permute-done((f32[4,136,256]{2,1,0:T(8,128)}, f32[4,136,256]{2,1,0:T(8,128)S(1)}, u32[]{:S(2)}, u32[]{:S(2)}) %collective-permute-start.2) | collective-permute-done | bytes 557088 | tf_op jit(solution)/shard_map/ppermute | solution.py:631
  63.2 0.1 compare_select_fusion
  63.3 1.9 %collective-permute-start.4 = (f32[4,136,256]{2,1,0:T(8,128)S(1)}, f32[4,136,256]{2,1,0:T(8,128)S(1)}, u32[]{:S(2)}, u32[]{:S(2)}) collective-permute-start(f32[4,136,256]{2,1,0:T(8,128)S(1)} %get-tuple-element.40), channel_id=1, source_target_pairs={{0,8},{8,16},{16,24},{24,32},{32,40},{40,48},{48,56},{56,64},{64,7... | collective-permute-start | bytes 1671176 | tf_op jit(solution)/shard_map/ppermute | solution.py:637
  65.2 3.0 %collective-permute-start.5 = (f32[4,136,256]{2,1,0:T(8,128)S(1)}, f32[4,136,256]{2,1,0:T(8,128)S(1)}, u32[]{:S(2)}, u32[]{:S(2)}) collective-permute-start(f32[4,136,256]{2,1,0:T(8,128)S(1)} %get-tuple-element.39), channel_id=1, source_target_pairs={{8,0},{16,8},{24,16},{32,24},{40,32},{48,40},{56,48},{64,56},{72,6... | collective-permute-start | bytes 1671176 | tf_op jit(solution)/shard_map/ppermute | solution.py:638
  68.2 0.9 divide_select_fusion.1.hr_ref
  69.1 0.9 divide_select_fusion.hc_ref
  70.1 1.6 collective-permute-done.4.cup
  71.7 4.4 %collective-permute-done.5.cdn = f32[4,136,256]{2,1,0:T(8,128)S(1)} collective-permute-done((f32[4,136,256]{2,1,0:T(8,128)S(1)}, f32[4,136,256]{2,1,0:T(8,128)S(1)}, u32[]{:S(2)}, u32[]{:S(2)}) %collective-permute-start.5) | collective-permute-done | bytes 557088 | tf_op jit(solution)/shard_map/ppermute | solution.py:638
  76.1 0.8 broadcast_in_dim.579.wt_ref
  76.9 15.4 %resample.1 = (f32[4,2,1024,128]{3,2,1,0:T(8,128)}, f32[4,2,8,128]{3,2,1,0:T(8,128)}, f32[4,2,8,128]{3,2,1,0:T(8,128)}, f32[8,72,128]{2,1,0:T(8,128)}) custom-call(s32[2,4]{1,0:T(2,128)} %bitcast.13, s32[2,4]{1,0:T(2,128)} %bitcast.14, f32[64,128]{1,0:T(8,128)} %broadcast_in_dim.579.wt_ref, f32[4,256,128]{2,1,0:T(8,128)} %pad_maximum_fusion.rm_ref, ...), custom_call_target="tpu_custom_call" | custom-call | tf_op jit(solution)/shard_map/resample/pallas_call | solution.py:265
  92.4 12.9 %all-to-all-start = ((f32[8,72,128]{2,1,0:T(8,128)}), f32[8,72,128]{2,1,0:T(8,128)S(1)}, u32[]{:S(2)}, u32[]{:S(2)}) async-start(f32[8,72,128]{2,1,0:T(8,128)} %get-tuple-element.25), calls=%async_computation | async-start | bytes 589824 | tf_op jit(solution)/shard_map/all_to_all | solution.py:667
  105.3 3.4 %collective-permute-start.6 = (f32[4,2,8,128]{3,2,1,0:T(8,128)}, f32[4,2,8,128]{3,2,1,0:T(8,128)S(1)}, u32[]{:S(2)}, u32[]{:S(2)}) collective-permute-start(f32[4,2,8,128]{3,2,1,0:T(8,128)} %get-tuple-element.27), channel_id=1, source_target_pairs={{0,1},{1,2},{2,3},{3,4},{4,5},{5,6},{6,7},{8,9},{9,10},{10,11},{11... | collective-permute-start | bytes 98312 | tf_op jit(solution)/shard_map/ppermute | solution.py:665
  108.7 1.3 collective-permute-start.7
  110.0 3.5 %collective-permute-done.7.rstrip = f32[4,2,8,128]{3,2,1,0:T(8,128)S(1)} collective-permute-done((f32[4,2,8,128]{3,2,1,0:T(8,128)}, f32[4,2,8,128]{3,2,1,0:T(8,128)S(1)}, u32[]{:S(2)}, u32[]{:S(2)}) %collective-permute-start.7) | collective-permute-done | bytes 32800 | tf_op jit(solution)/shard_map/ppermute | solution.py:666
  113.5 1.0 broadcast_in_dim.602.invc_ref
  114.5 9.1 %across.1 = (f32[4,10,256,128]{3,2,1,0:T(8,128)}, f32[4,10,8,128]{3,2,1,0:T(8,128)}, f32[4,10,8,128]{3,2,1,0:T(8,128)}) custom-call(f32[1040,128]{1,0:T(8,128)} %broadcast_in_dim.602.invc_ref, f32[4,2,1024,128]{3,2,1,0:T(8,128)} %get-tuple-element.26.diff, f32[4,2,8,128]{3,2,1,0:T(8,128)} %copy-done.9, f32[4,2,8,128]{3,2,1,0:T(8,128)} %copy-done.10), custom_call_target="tpu_custom_call" | custom-call | flops 20971520 | bytes 8388608 | tf_op jit(solution)/shard_map/across/pallas_call | solution.py:386
  123.7 0.7 copy-done.4
  124.4 2.7 %long_rows.1 = f32[16,4,24,128]{3,2,1,0:T(8,128)} custom-call(f32[8,72,128]{2,1,0:T(8,128)} %copy-done.4, f32[384,24]{1,0:T(8,128)} %divide_select_fusion.1.hr_ref), custom_call_target="tpu_custom_call" | custom-call | tf_op jit(solution)/shard_map/long_rows/pallas_call | solution.py:310
  127.1 3.5 %all-to-all-start.1 = ((f32[16,4,24,128]{3,2,1,0:T(8,128)}), f32[16,4,24,128]{3,2,1,0:T(8,128)S(1)}, u32[]{:S(2)}, u32[]{:S(2)}) async-start(f32[16,4,24,128]{3,2,1,0:T(8,128)} %long_rows.1), calls=%async_computation.1 | async-start | bytes 1572864 | tf_op jit(solution)/shard_map/all_to_all | solution.py:673
  130.7 0.9 fusion.9.uc_ref
  131.6 3.6 %collective-permute-start.8 = (f32[4,10,8,128]{3,2,1,0:T(8,128)S(1)}, f32[4,10,8,128]{3,2,1,0:T(8,128)S(1)}, u32[]{:S(2)}, u32[]{:S(2)}) collective-permute-start(f32[4,10,8,128]{3,2,1,0:T(8,128)S(1)} %copy-done.12), channel_id=1, source_target_pairs={{0,8},{8,16},{16,24},{24,32},{32,40},{40,48},{48,56},{56,64},{64,7... | collective-permute-start | bytes 491528 | tf_op jit(solution)/shard_map/ppermute | solution.py:671
  135.2 1.9 %collective-permute-start.9 = (f32[4,10,8,128]{3,2,1,0:T(8,128)S(1)}, f32[4,10,8,128]{3,2,1,0:T(8,128)S(1)}, u32[]{:S(2)}, u32[]{:S(2)}) collective-permute-start(f32[4,10,8,128]{3,2,1,0:T(8,128)S(1)} %copy-done.11), channel_id=1, source_target_pairs={{8,0},{16,8},{24,16},{32,24},{40,32},{48,40},{56,48},{64,56},{72,6... | collective-permute-start | bytes 491528 | tf_op jit(solution)/shard_map/ppermute | solution.py:672
  137.2 0.6 and_convert_fusion.mc_ref
  137.8 3.6 %collective-permute-done.8.upr = f32[4,10,8,128]{3,2,1,0:T(8,128)S(1)} collective-permute-done((f32[4,10,8,128]{3,2,1,0:T(8,128)S(1)}, f32[4,10,8,128]{3,2,1,0:T(8,128)S(1)}, u32[]{:S(2)}, u32[]{:S(2)}) %collective-permute-start.8) | collective-permute-done | bytes 163872 | tf_op jit(solution)/shard_map/ppermute | solution.py:671
  141.4 2.1 %collective-permute-done.9.dnr = f32[4,10,8,128]{3,2,1,0:T(8,128)S(1)} collective-permute-done((f32[4,10,8,128]{3,2,1,0:T(8,128)S(1)}, f32[4,10,8,128]{3,2,1,0:T(8,128)S(1)}, u32[]{:S(2)}, u32[]{:S(2)}) %collective-permute-start.9) | collective-permute-done | bytes 163872 | tf_op jit(solution)/shard_map/ppermute | solution.py:672
  143.5 1.5 all-to-all-done.1.z_ref
  145.0 0.9 broadcast_in_dim.611.invr_ref
  145.9 0.7 broadcast_in_dim.612.mr_ref
  146.6 15.5 %final.1 = (f32[4,256,1024]{2,1,0:T(8,128)}, f32[4,256,1024]{2,1,0:T(8,128)}, f32[4,2,128]{2,1,0:T(2,128)}) custom-call(f32[16,4,24,128]{3,2,1,0:T(8,128)} %copy-done, bf16[128,1280]{1,0:T(8,128)(2,1)} %fusion.9.uc_ref, f32[272,128]{1,0:T(8,128)} %broadcast_in_dim.611.invr_ref, f32[1,1024]{1,0:T(1,128)} %and_convert_fusion.mc_ref, ...), custom_call_target="tpu_custom_call" | custom-call | tf_op jit(solution)/shard_map/final/pallas_call | solution.py:516
  162.2 0.8 reduce_sum.38
  163.0 0.1 copy.14
  163.2 18.6 %all_to_all.15 = f32[128,1,8]{2,1,0:T(1,128)S(1)} all-to-all(f32[128,1,8]{2,1,0:T(1,128)S(1)} %broadcast_in_dim.614), channel_id=1, replica_groups=mesh['row'=16,'col'=8] {'row','col'}, dimensions={0} | all-to-all | bytes 8192 | tf_op jit(solution)/shard_map/all_to_all | solution.py:678
  181.8 0.2 reduce_sum.39
  181.9 0.7 sqrt.7
  (73 shorter events, 1.2 us)
Async XLA Ops:
  0.6 16.7 %copy-start.14 = (s32[8]{0:T(128)S(1)}, s32[8]{0:T(128)}, u32[]{:S(2)}) copy-start(s32[8]{0:T(128)} %constant.480.clone) | copy-start | bytes 100
  0.6 16.9 %copy-start.13 = (s32[8]{0:T(128)S(1)}, s32[8]{0:T(128)}, u32[]{:S(2)}) copy-start(s32[8]{0:T(128)} %constant.479.clone) | copy-start | bytes 100
  5.9 31.9 %collective-permute-start.1 = (f32[4,8,136,128]{3,2,1,0:T(8,128)}, f32[4,8,136,128]{3,2,1,0:T(8,128)S(1)}, u32[]{:S(2)}, u32[]{:S(2)}) collective-permute-start(f32[4,8,136,128]{3,2,1,0:T(8,128)} %get-tuple-element.22), channel_id=1, source_target_pairs={{8,0},{16,8},{24,16},{32,24},{40,32},{48,40},{56,48},{64,56},{72,6... | collective-permute-start | bytes 6684680 | tf_op jit(solution)/shard_map/ppermute | solution.py:630
  9.2 27.8 %collective-permute-start = (f32[4,8,136,128]{3,2,1,0:T(8,128)}, f32[4,8,136,128]{3,2,1,0:T(8,128)}, u32[]{:S(2)}, u32[]{:S(2)}) collective-permute-start(f32[4,8,136,128]{3,2,1,0:T(8,128)} %get-tuple-element.21), channel_id=1, source_target_pairs={{0,8},{8,16},{16,24},{24,32},{32,40},{40,48},{48,56},{56,64},{64,7... | collective-permute-start | bytes 6684680 | tf_op jit(solution)/shard_map/ppermute | solution.py:629
  12.3 50.8 %collective-permute-start.2 = (f32[4,136,256]{2,1,0:T(8,128)}, f32[4,136,256]{2,1,0:T(8,128)S(1)}, u32[]{:S(2)}, u32[]{:S(2)}) collective-permute-start(f32[4,136,256]{2,1,0:T(8,128)} %get-tuple-element.23), channel_id=1, source_target_pairs={{0,1},{1,2},{2,3},{3,4},{4,5},{5,6},{6,7},{8,9},{9,10},{10,11},{11... | collective-permute-start | bytes 1671176 | tf_op jit(solution)/shard_map/ppermute | solution.py:631
  15.9 47.3 %collective-permute-start.3 = (f32[4,136,256]{2,1,0:T(8,128)}, f32[4,136,256]{2,1,0:T(8,128)S(1)}, u32[]{:S(2)}, u32[]{:S(2)}) collective-permute-start(f32[4,136,256]{2,1,0:T(8,128)} %get-tuple-element.24), channel_id=1, source_target_pairs={{1,0},{2,1},{3,2},{4,3},{5,4},{6,5},{7,6},{9,8},{10,9},{11,10},{12... | collective-permute-start | bytes 1671176 | tf_op jit(solution)/shard_map/ppermute | solution.py:632
  37.8 39.1 %copy-start.1 = (f32[4,8,136,128]{3,2,1,0:T(8,128)}, f32[4,8,136,128]{3,2,1,0:T(8,128)S(1)}, u32[]{:S(2)}) copy-start(f32[4,8,136,128]{3,2,1,0:T(8,128)S(1)} %collective-permute-done.1.dn) | copy-start | bytes 6684676
  63.2 13.7 %copy-start.2 = (f32[4,136,256]{2,1,0:T(8,128)}, f32[4,136,256]{2,1,0:T(8,128)S(1)}, u32[]{:S(2)}) copy-start(f32[4,136,256]{2,1,0:T(8,128)S(1)} %collective-permute-done.2.lcols) | copy-start | bytes 1671172
  63.2 13.7 %copy-start.3 = (f32[4,136,256]{2,1,0:T(8,128)}, f32[4,136,256]{2,1,0:T(8,128)S(1)}, u32[]{:S(2)}) copy-start(f32[4,136,256]{2,1,0:T(8,128)S(1)} %collective-permute-done.3.rcols) | copy-start | bytes 1671172
  63.3 8.4 %collective-permute-start.4 = (f32[4,136,256]{2,1,0:T(8,128)S(1)}, f32[4,136,256]{2,1,0:T(8,128)S(1)}, u32[]{:S(2)}, u32[]{:S(2)}) collective-permute-start(f32[4,136,256]{2,1,0:T(8,128)S(1)} %get-tuple-element.40), channel_id=1, source_target_pairs={{0,8},{8,16},{16,24},{24,32},{32,40},{40,48},{48,56},{56,64},{64,7... | collective-permute-start | bytes 1671176 | tf_op jit(solution)/shard_map/ppermute | solution.py:637
  65.2 10.9 %collective-permute-start.5 = (f32[4,136,256]{2,1,0:T(8,128)S(1)}, f32[4,136,256]{2,1,0:T(8,128)S(1)}, u32[]{:S(2)}, u32[]{:S(2)}) collective-permute-start(f32[4,136,256]{2,1,0:T(8,128)S(1)} %get-tuple-element.39), channel_id=1, source_target_pairs={{8,0},{16,8},{24,16},{32,24},{40,32},{48,40},{56,48},{64,56},{72,6... | collective-permute-start | bytes 1671176 | tf_op jit(solution)/shard_map/ppermute | solution.py:638
  71.7 5.2 %copy-start.5 = (f32[4,136,256]{2,1,0:T(8,128)}, f32[4,136,256]{2,1,0:T(8,128)S(1)}, u32[]{:S(2)}) copy-start(f32[4,136,256]{2,1,0:T(8,128)S(1)} %collective-permute-done.4.cup) | copy-start | bytes 1671172
  76.1 0.8 copy-start.6
  92.4 31.3 %all-to-all-start = ((f32[8,72,128]{2,1,0:T(8,128)}), f32[8,72,128]{2,1,0:T(8,128)S(1)}, u32[]{:S(2)}, u32[]{:S(2)}) async-start(f32[8,72,128]{2,1,0:T(8,128)} %get-tuple-element.25), calls=%async_computation | async-start | bytes 589824 | tf_op jit(solution)/shard_map/all_to_all | solution.py:667
  105.3 4.7 %collective-permute-start.6 = (f32[4,2,8,128]{3,2,1,0:T(8,128)}, f32[4,2,8,128]{3,2,1,0:T(8,128)S(1)}, u32[]{:S(2)}, u32[]{:S(2)}) collective-permute-start(f32[4,2,8,128]{3,2,1,0:T(8,128)} %get-tuple-element.27), channel_id=1, source_target_pairs={{0,1},{1,2},{2,3},{3,4},{4,5},{5,6},{6,7},{8,9},{9,10},{10,11},{11... | collective-permute-start | bytes 98312 | tf_op jit(solution)/shard_map/ppermute | solution.py:665
  108.7 4.9 %collective-permute-start.7 = (f32[4,2,8,128]{3,2,1,0:T(8,128)}, f32[4,2,8,128]{3,2,1,0:T(8,128)S(1)}, u32[]{:S(2)}, u32[]{:S(2)}) collective-permute-start(f32[4,2,8,128]{3,2,1,0:T(8,128)} %get-tuple-element.28), channel_id=1, source_target_pairs={{1,0},{2,1},{3,2},{4,3},{5,4},{6,5},{7,6},{9,8},{10,9},{11,10},{12... | collective-permute-start | bytes 98312 | tf_op jit(solution)/shard_map/ppermute | solution.py:666
  110.0 4.5 %copy-start.9 = (f32[4,2,8,128]{3,2,1,0:T(8,128)}, f32[4,2,8,128]{3,2,1,0:T(8,128)S(1)}, u32[]{:S(2)}) copy-start(f32[4,2,8,128]{3,2,1,0:T(8,128)S(1)} %collective-permute-done.6.lstrip) | copy-start | bytes 98308
  113.5 1.0 copy-start.10
  123.6 8.0 %copy-start.12 = (f32[4,10,8,128]{3,2,1,0:T(8,128)S(1)}, f32[4,10,8,128]{3,2,1,0:T(8,128)}, u32[]{:S(2)}) copy-start(f32[4,10,8,128]{3,2,1,0:T(8,128)} %get-tuple-element.34) | copy-start | bytes 491524
  123.6 11.6 %copy-start.11 = (f32[4,10,8,128]{3,2,1,0:T(8,128)S(1)}, f32[4,10,8,128]{3,2,1,0:T(8,128)}, u32[]{:S(2)}) copy-start(f32[4,10,8,128]{3,2,1,0:T(8,128)} %get-tuple-element.35) | copy-start | bytes 491524
  123.7 0.7 copy-start.4
  127.1 17.9 %all-to-all-start.1 = ((f32[16,4,24,128]{3,2,1,0:T(8,128)}), f32[16,4,24,128]{3,2,1,0:T(8,128)S(1)}, u32[]{:S(2)}, u32[]{:S(2)}) async-start(f32[16,4,24,128]{3,2,1,0:T(8,128)} %long_rows.1), calls=%async_computation.1 | async-start | bytes 1572864 | tf_op jit(solution)/shard_map/all_to_all | solution.py:673
  131.6 9.8 %collective-permute-start.8 = (f32[4,10,8,128]{3,2,1,0:T(8,128)S(1)}, f32[4,10,8,128]{3,2,1,0:T(8,128)S(1)}, u32[]{:S(2)}, u32[]{:S(2)}) collective-permute-start(f32[4,10,8,128]{3,2,1,0:T(8,128)S(1)} %copy-done.12), channel_id=1, source_target_pairs={{0,8},{8,16},{16,24},{24,32},{32,40},{40,48},{48,56},{56,64},{64,7... | collective-permute-start | bytes 491528 | tf_op jit(solution)/shard_map/ppermute | solution.py:671
  135.2 8.3 %collective-permute-start.9 = (f32[4,10,8,128]{3,2,1,0:T(8,128)S(1)}, f32[4,10,8,128]{3,2,1,0:T(8,128)S(1)}, u32[]{:S(2)}, u32[]{:S(2)}) collective-permute-start(f32[4,10,8,128]{3,2,1,0:T(8,128)S(1)} %copy-done.11), channel_id=1, source_target_pairs={{8,0},{16,8},{24,16},{32,24},{40,32},{48,40},{56,48},{64,56},{72,6... | collective-permute-start | bytes 491528 | tf_op jit(solution)/shard_map/ppermute | solution.py:672
  141.4 5.2 %copy-start.7 = (f32[4,10,8,128]{3,2,1,0:T(8,128)}, f32[4,10,8,128]{3,2,1,0:T(8,128)S(1)}, u32[]{:S(2)}) copy-start(f32[4,10,8,128]{3,2,1,0:T(8,128)S(1)} %collective-permute-done.8.upr) | copy-start | bytes 491524
  143.5 3.1 %copy-start.8 = (f32[4,10,8,128]{3,2,1,0:T(8,128)}, f32[4,10,8,128]{3,2,1,0:T(8,128)S(1)}, u32[]{:S(2)}) copy-start(f32[4,10,8,128]{3,2,1,0:T(8,128)S(1)} %collective-permute-done.9.dnr) | copy-start | bytes 491524
  145.0 1.6 copy-start

commit v3 on v2

--- a/solution.py
+++ b/solution.py
@@ -18,51 +18,34 @@
 EDGE = 8
 LANES = 128
 TAPS = [math.exp(-math.pi * (k / (ALPHA * LS)) ** 2) for k in range(-SR, SR + 1)]
-VMEM_LIMIT = 56 * 1024 * 1024
+VMEM_LIMIT = 24 * 1024 * 1024
 
 
 def lane_iota(rows):
     return lax.broadcasted_iota(jnp.int32, (rows, LANES), 1)
 
 
-def pack_kernel(offs_ref, x_ref, top_ref, bot_ref, left_ref, right_ref):
-    s = pl.program_id(0)
-    shift = offs_ref[1, s].astype(jnp.float32)
+def pack_kernel(x_ref, top_ref, bot_ref):
     rows, cols = x_ref.shape[1], x_ref.shape[2]
     for j in range(cols // LANES):
         sl = slice(j * LANES, (j + 1) * LANES)
         top_ref[0, j] = x_ref[0, 0:HALO, sl]
         bot_ref[0, j] = x_ref[0, rows - HALO : rows, sl]
-    top_ref[0, 0, HALO - 1 : HALO, :] = jnp.full((1, LANES), shift, jnp.float32)
-    bot_ref[0, 0, 0:1, :] = jnp.full((1, LANES), shift, jnp.float32)
-    left_ref[0] = x_ref[0, :, 0:256].T[0:HALO, :]
-    right_ref[0] = x_ref[0, :, cols - 256 : cols].T[256 - HALO : 256, :]
-
-
-def pack(after, offs):
+
+
+def pack(after):
     scans, rows, cols = after.shape
     n_tiles = cols // LANES
+    spec = pl.BlockSpec((1, n_tiles, HALO, LANES), lambda s: (s, 0, 0, 0))
+    shape = jax.ShapeDtypeStruct((scans, n_tiles, HALO, LANES), jnp.float32)
     return pl.pallas_call(
         pack_kernel,
         grid=(scans,),
-        in_specs=[
-            pl.BlockSpec(memory_space=pltpu.SMEM),
-            pl.BlockSpec((1, rows, cols), lambda s: (s, 0, 0)),
-        ],
-        out_specs=[
-            pl.BlockSpec((1, n_tiles, HALO, LANES), lambda s: (s, 0, 0, 0)),
-            pl.BlockSpec((1, n_tiles, HALO, LANES), lambda s: (s, 0, 0, 0)),
-            pl.BlockSpec((1, HALO, rows), lambda s: (s, 0, 0)),
-            pl.BlockSpec((1, HALO, rows), lambda s: (s, 0, 0)),
-        ],
-        out_shape=[
-            jax.ShapeDtypeStruct((scans, n_tiles, HALO, LANES), jnp.float32),
-            jax.ShapeDtypeStruct((scans, n_tiles, HALO, LANES), jnp.float32),
-            jax.ShapeDtypeStruct((scans, HALO, rows), jnp.float32),
-            jax.ShapeDtypeStruct((scans, HALO, rows), jnp.float32),
-        ],
+        in_specs=[pl.BlockSpec((1, rows, cols), lambda s: (s, 0, 0))],
+        out_specs=[spec, spec],
+        out_shape=[shape, shape],
         name="pack",
-    )(offs, after)
+    )(after)
 
 
 def flip_kernel(x_ref, o_ref):
@@ -101,113 +84,198 @@
     )
 
 
+def tile_copies(s, groups, after, up, dn, win):
+    rows = after.shape[1]
+    out = []
+    for at, first, n in groups:
+        out += [
+            (up.at[s, pl.ds(first, n)], win.at[s, pl.ds(at, n), pl.ds(0, HALO), :]),
+            (dn.at[s, pl.ds(first, n)], win.at[s, pl.ds(at, n), pl.ds(HALO + rows, HALO), :]),
+        ]
+        out += [
+            (
+                after.at[s, :, pl.ds((first + i) * LANES, LANES)],
+                win.at[s, at + i, pl.ds(HALO, rows), :],
+            )
+            for i in range(n)
+        ]
+    return out
+
+
+def start_copies(copies, sem):
+    for n, (a, b) in enumerate(copies):
+        pltpu.make_async_copy(a, b, sem.at[n]).start()
+
+
+def wait_copies(copies, sem):
+    for n, (a, b) in enumerate(copies):
+        pltpu.make_async_copy(a, b, sem.at[n]).wait()
+
+
+def tapped(win, s, tile, first, taps):
+    acc = taps[0] * win[s, tile, pl.ds(first, LANES), :]
+    for a in range(1, 4):
+        acc = acc + taps[a] * win[s, tile, pl.ds(first + a, LANES), :]
+    return acc.T
+
+
+def edge_rows_kernel(prev_ref, next_ref, after, up, dn, left_out, right_out, win, sem):
+    scans, halves = left_out.shape[0], left_out.shape[1]
+    n_out = after.shape[2] // LANES
+    groups = ((0, 0, 2), (2, n_out - 2, 2))
+    extra = HALO - LANES
+
+    def copies(s):
+        return tile_copies(s, groups, after, up, dn, win)
+
+    for s in range(scans):
+        start_copies(copies(s), sem.at[s])
+
+    def one_scan(s, carry):
+        wait_copies(copies(s), sem.at[s])
+
+        for ref, base in ((prev_ref, 0), (next_ref, 2)):
+            taps = scalar_taps(ref[1, s])
+            first = HALO + ref[0, s] - 1
+            for h in range(halves):
+                a = tapped(win, s, base, first + h * LANES, taps)
+                b = tapped(win, s, base + 1, first + h * LANES, taps)
+                if base == 0:
+                    left_out[s, h, 0:LANES, :] = a
+                    left_out[s, h, LANES:HALO, :] = b[0:extra]
+                else:
+                    right_out[s, h, 0:extra, :] = a[LANES - extra : LANES]
+                    right_out[s, h, extra:HALO, :] = b
+        return carry
+
+    lax.fori_loop(0, scans, one_scan, 0)
+
+
+def edge_rows(prev, after_next, after, up, dn):
+    scans, rows, cols = after.shape
+    halves = rows // LANES
+    anywhere = pl.BlockSpec(memory_space=pl.ANY)
+    vmem = pl.BlockSpec(memory_space=pltpu.VMEM)
+    smem = pl.BlockSpec(memory_space=pltpu.SMEM)
+    shape = jax.ShapeDtypeStruct((scans, halves, HALO, LANES), jnp.float32)
+    return pl.pallas_call(
+        edge_rows_kernel,
+        in_specs=[smem, smem] + [anywhere] * 3,
+        out_specs=[vmem, vmem],
+        out_shape=[shape, shape],
+        scratch_shapes=[
+            pltpu.VMEM((scans, 4, 2 * HALO + rows, LANES), jnp.float32),
+            pltpu.SemaphoreType.DMA((scans, 8)),
+        ],
+        compiler_params=pltpu.CompilerParams(vmem_limit_bytes=VMEM_LIMIT),
+        name="edge_rows",
+    )(prev, after_next, after, up, dn)
+
+
+def own_rows_kernel(mine_ref, after, up, dn, out, win, sem):
+    scans, halves, cols = out.shape[0], out.shape[1], out.shape[2]
+    n_out = cols // LANES
+
+    def copies(s):
+        return tile_copies(s, ((0, 0, n_out),), after, up, dn, win)
+
+    start_copies(copies(0), sem.at[0])
+
+    def one_scan(s, carry):
+        wait_copies(copies(s), sem.at[s])
+
+        @pl.when(s + 1 < scans)
+        def _():
+            start_copies(copies(s + 1), sem.at[s + 1])
+
+        taps = scalar_taps(mine_ref[1, s])
+        first = HALO + mine_ref[0, s] - 1
+
+        def two_tiles(i, carry):
+            done = [
+                tapped(win, s, 2 * i + j, first + h * LANES, taps)
+                for j in range(2)
+                for h in range(halves)
+            ]
+            for j in range(2):
+                at = pl.multiple_of((2 * i + j) * LANES, LANES)
+                for h in range(halves):
+                    out[s, h, pl.ds(at, LANES), :] = done[j * halves + h]
+            return carry
+
+        lax.fori_loop(0, n_out // 2, two_tiles, 0)
+        return carry
+
+    lax.fori_loop(0, scans, one_scan, 0)
+
+
+def own_rows(mine, after, up, dn):
+    scans, rows, cols = after.shape
+    halves = rows // LANES
+    anywhere = pl.BlockSpec(memory_space=pl.ANY)
+    smem = pl.BlockSpec(memory_space=pltpu.SMEM)
+    return pl.pallas_call(
+        own_rows_kernel,
+        in_specs=[smem] + [anywhere] * 3,
+        out_specs=pl.BlockSpec(memory_space=pltpu.VMEM),
+        out_shape=pltpu.VMEM((scans, halves, cols, LANES), jnp.float32),
+        scratch_shapes=[
+            pltpu.VMEM((scans, cols // LANES, 2 * HALO + rows, LANES), jnp.float32),
+            pltpu.SemaphoreType.DMA((scans, 2 + cols // LANES)),
+        ],
+        compiler_params=pltpu.CompilerParams(vmem_limit_bytes=VMEM_LIMIT),
+        cost_estimate=pl.CostEstimate(
+            flops=8 * after.size, bytes_accessed=16 * after.size, transcendentals=0
+        ),
+        name="own_rows",
+    )(mine, after, up, dn)
+
+
 CB = 64
 
 
 def resample_kernel(
     offs_ref, fracs_ref, wt_ref, rm_ref, hc_ref,
-    after, beforet, up, dn, lcols, rcols, cup, cdn,
-    diff_out, edge_l, edge_r, y_ref,
-    win, stage, bef, dif, rowsum, sums, part, sem, bsem, osem,
+    own, lcols, rcols, beforet,
+    dif, edge_l, edge_r, y_ref,
+    win, bef, sums, part, sem,
 ):
-    scans, n_tiles = win.shape[0], win.shape[1]
-    halves, cols = bef.shape[1], bef.shape[2]
-    rows = halves * LANES
-    n_out = cols // LANES
-    left = 2 * LANES
+    scans, halves, cols = bef.shape[0], bef.shape[1], bef.shape[2]
 
     def copies(s):
         return [
-            (after.at[s, :, pl.ds(j * LANES, LANES)], win.at[s, 2 + j, pl.ds(HALO, rows), :])
-            for j in range(n_out)
-        ] + [
-            (up.at[s], win.at[s, pl.ds(2, n_out), pl.ds(0, HALO), :]),
-            (dn.at[s], win.at[s, pl.ds(2, n_out), pl.ds(HALO + rows, HALO), :]),
-            (lcols.at[s], stage.at[s, 0, pl.ds(256 - HALO, HALO), :]),
-            (rcols.at[s], stage.at[s, 1, pl.ds(0, HALO), :]),
-            (cup.at[s], stage.at[s, 2, pl.ds(256 - HALO, HALO), :]),
-            (cup.at[s], stage.at[s, 3, pl.ds(0, HALO), :]),
-            (cdn.at[s], stage.at[s, 4, pl.ds(256 - HALO, HALO), :]),
-            (cdn.at[s], stage.at[s, 5, pl.ds(0, HALO), :]),
+            (lcols.at[s], win.at[s, :, pl.ds(0, HALO), :]),
+            (own.at[s], win.at[s, :, pl.ds(HALO, cols), :]),
+            (rcols.at[s], win.at[s, :, pl.ds(HALO + cols, HALO), :]),
+            (beforet.at[s], bef.at[s]),
         ]
 
-    for s in range(scans):
-        for n, (a, b) in enumerate(copies(s)):
-            pltpu.make_async_copy(a, b, sem.at[s, n]).start()
-        pltpu.make_async_copy(beforet.at[s], bef.at[s], bsem.at[s]).start()
+    start_copies(copies(0), sem.at[0])
     part[...] = jnp.zeros_like(part)
     sums[...] = jnp.zeros_like(sums)
     n_blocks = cols // BLOCK
     weight = [wt_ref[8 * i : 8 * i + 8, :] for i in range(8)]
 
     def one_scan(s, carry):
-        for n, (a, b) in enumerate(copies(s)):
-            pltpu.make_async_copy(a, b, sem.at[s, n]).wait()
-        pltpu.make_async_copy(beforet.at[s], bef.at[s], bsem.at[s]).wait()
-        dr = offs_ref[0, s]
-        dc = offs_ref[1, s]
-
-        def put(slot, first_tile, row0, cut):
-            flipped = stage[s, slot].T
-            for h in range(2):
-                win[s, first_tile + h, row0 : row0 + cut.stop - cut.start, :] = flipped[
-                    cut, h * LANES : (h + 1) * LANES
-                ]
-
-        def put_side(first_tile, slots):
-            put(slots[0], first_tile, HALO, slice(0, rows))
-
-            @pl.when(dr <= 0)
-            def _():
-                put(slots[1], first_tile, 0, slice(rows - HALO, rows))
-
-            @pl.when(dr >= -1)
-            def _():
-                put(slots[2], first_tile, HALO + rows, slice(0, HALO))
-
-        @pl.when(dc <= 0)
+        wait_copies(copies(s), sem.at[s])
+
+        @pl.when(s + 1 < scans)
         def _():
-            put_side(0, (0, 2, 4))
-
-        @pl.when(dc >= -1)
-        def _():
-            put_side(2 + n_out, (1, 3, 5))
-
-        rt = scalar_taps(fracs_ref[0, s])
+            start_copies(copies(s + 1), sem.at[s + 1])
+
         ct = scalar_taps(fracs_ref[1, s])
-        r0 = HALO + dr - 1
-        c0 = left + dc - 1
-        k = lax.div(c0, LANES)
-        r = c0 - k * LANES
-
-        def row_taps(i, carry):
-            outs = []
-            for j in range(2):
-                for h in range(halves):
-                    first = r0 + h * LANES
-                    acc = rt[0] * win[s, k + 2 * i + j, pl.ds(first, LANES), :]
-                    for a in range(1, 4):
-                        acc = acc + rt[a] * win[s, k + 2 * i + j, pl.ds(first + a, LANES), :]
-                    outs.append(acc.T)
-            for j in range(2):
-                for h in range(halves):
-                    at = pl.multiple_of((2 * i + j) * LANES, LANES)
-                    rowsum[h, pl.ds(at, LANES), :] = outs[j * halves + h]
-            return carry
-
-        lax.fori_loop(0, (n_out + 2) // 2, row_taps, 0)
+        first = HALO + offs_ref[1, s] - 1
 
         def col_taps(i, carry):
             q0 = pl.multiple_of(i * CB, CB)
             for h in range(halves):
-                acc = ct[0] * rowsum[h, pl.ds(r + q0, CB), :]
+                acc = ct[0] * win[s, h, pl.ds(first + q0, CB), :]
                 for b in range(1, 4):
-                    acc = acc + ct[b] * rowsum[h, pl.ds(r + q0 + b, CB), :]
+                    acc = acc + ct[b] * win[s, h, pl.ds(first + q0 + b, CB), :]
                 dif[s, h, pl.ds(q0, CB), :] = bef[s, h, pl.ds(q0, CB), :] - acc
             return carry
 
         lax.fori_loop(0, cols // CB, col_taps, 0)
-        pltpu.make_async_copy(dif.at[s], diff_out.at[s], osem.at[s]).start()
         for h in range(halves):
             edge_l[s, h] = dif[s, h, 0:EDGE, :]
             edge_r[s, h] = dif[s, h, cols - EDGE : cols, :]
@@ -251,42 +319,34 @@
     ext = hc_ref.shape[0] // y_ref.shape[0]
     for t in range(y_ref.shape[0]):
         y_ref[t] = y[t * ext : (t + 1) * ext, :]
-    for s in range(scans):
-        pltpu.make_async_copy(dif.at[s], diff_out.at[s], osem.at[s]).wait()
-
-
-def resample(offs, fracs, wt, rm, hc, ext, after, beforet, up, dn, lcols, rcols, cup, cdn):
-    scans, rows, cols = after.shape
-    halves = rows // LANES
+
+
+def resample(offs, fracs, wt, rm, hc, ext, own, lcols, rcols, beforet):
+    scans, halves, cols, _ = own.shape
     n_col = hc.shape[0] // ext
     anywhere = pl.BlockSpec(memory_space=pl.ANY)
     vmem = pl.BlockSpec(memory_space=pltpu.VMEM)
     smem = pl.BlockSpec(memory_space=pltpu.SMEM)
     return pl.pallas_call(
         resample_kernel,
-        in_specs=[smem, smem, vmem, vmem, vmem] + [anywhere] * 8,
-        out_specs=[anywhere, vmem, vmem, vmem],
+        in_specs=[smem, smem, vmem, vmem, vmem] + [anywhere] * 4,
+        out_specs=[vmem, vmem, vmem, vmem],
         out_shape=[
-            jax.ShapeDtypeStruct((scans, halves, cols, LANES), jnp.float32),
+            pltpu.VMEM((scans, halves, cols, LANES), jnp.float32),
             jax.ShapeDtypeStruct((scans, halves, EDGE, LANES), jnp.float32),
             jax.ShapeDtypeStruct((scans, halves, EDGE, LANES), jnp.float32),
             jax.ShapeDtypeStruct((n_col, ext, LANES), jnp.float32),
         ],
         scratch_shapes=[
-            pltpu.VMEM((scans, cols // LANES + 4, 2 * HALO + rows, LANES), jnp.float32),
-            pltpu.VMEM((scans, 6, 256, rows), jnp.float32),
+            pltpu.VMEM((scans, halves, cols + 2 * HALO, LANES), jnp.float32),
             pltpu.VMEM((scans, halves, cols, LANES), jnp.float32),
-            pltpu.VMEM((scans, halves, cols, LANES), jnp.float32),
-            pltpu.VMEM((halves, cols + 2 * LANES, LANES), jnp.float32),
-            pltpu.VMEM((hc.shape[1], rows), jnp.float32),
+            pltpu.VMEM((hc.shape[1], halves * LANES), jnp.float32),
             pltpu.VMEM((hc.shape[1], LANES), jnp.float32),
-            pltpu.SemaphoreType.DMA((scans, cols // LANES + 8)),
-            pltpu.SemaphoreType.DMA((scans,)),
-            pltpu.SemaphoreType.DMA((scans,)),
+            pltpu.SemaphoreType.DMA((scans, 4)),
         ],
         compiler_params=pltpu.CompilerParams(vmem_limit_bytes=VMEM_LIMIT),
         name="resample",
-    )(offs, fracs, wt, rm, hc, after, beforet, up, dn, lcols, rcols, cup, cdn)
+    )(offs, fracs, wt, rm, hc, own, lcols, rcols, beforet)
 
 
 def long_rows_kernel(y_ref, hr_ref, z_ref):
@@ -331,9 +391,11 @@
             (rstrip.at[s], buf.at[s, :, pl.ds(PAD + cols, EDGE), :]),
         ]
 
-    for s in range(scans):
+    def fetch(s):
         for n, (a, b) in enumerate(copies(s)):
             pltpu.make_async_copy(a, b, sem.at[s, n]).start()
+
+    fetch(0)
     zero = jnp.zeros((LANES - EDGE, LANES), jnp.float32)
 
     def filtered(s, h, q, n):
@@ -347,6 +409,11 @@
     def one_scan(s, carry):
         for n, (a, b) in enumerate(copies(s)):
             pltpu.make_async_copy(a, b, sem.at[s, n]).wait()
+
+        @pl.when(s + 1 < scans)
+        def _():
+            fetch(s + 1)
+
         for h in range(halves):
             buf[s, h, 0 : PAD - EDGE, :] = zero[0:EDGE]
             buf[s, h, PAD + cols + EDGE :, :] = zero[0:EDGE]
@@ -386,9 +453,9 @@
     return pl.pallas_call(
         across_kernel,
         in_specs=[vmem, anywhere, anywhere, anywhere],
-        out_specs=[anywhere, vmem, vmem],
+        out_specs=[pl.BlockSpec(memory_space=pltpu.HBM), vmem, vmem],
         out_shape=[
-            jax.ShapeDtypeStruct((scans, n_wide, rows, LANES), jnp.float32),
+            pltpu.HBM((scans, n_wide, rows, LANES), jnp.float32),
             jax.ShapeDtypeStruct((scans, n_wide, EDGE, LANES), jnp.float32),
             jax.ShapeDtypeStruct((scans, n_wide, EDGE, LANES), jnp.float32),
         ],
@@ -423,11 +490,13 @@
             (dnr.at[s], acs.at[s, :, pl.ds(PAD + rows, EDGE), :]),
         ]
 
+    def fetch(s):
+        for n, (a, b) in enumerate(copies(s)):
+            pltpu.make_async_copy(a, b, sem.at[s, n]).start()
+
     @pl.when(s == 0)
     def _():
-        for t in range(scans):
-            for n, (a, b) in enumerate(copies(t)):
-                pltpu.make_async_copy(a, b, sem.at[t, n]).start()
+        fetch(0)
 
         parts = []
         for t in range(scans):
@@ -449,6 +518,11 @@
 
     for n, (a, b) in enumerate(copies(s)):
         pltpu.make_async_copy(a, b, sem.at[s, n]).wait()
+
+    @pl.when(s + 1 < scans)
+    def _():
+        fetch(s + 1)
+
     for j in range(n_wide):
         acs[s, j, 0 : PAD - EDGE, :] = jnp.zeros((PAD - EDGE, LANES), jnp.float32)
         acs[s, j, PAD + rows + EDGE :, :] = jnp.zeros((PAD - EDGE, LANES), jnp.float32)
@@ -522,7 +596,7 @@
             pl.BlockSpec(invr.shape, const2),
             pl.BlockSpec(mc.shape, const2),
             pl.BlockSpec(mr.shape, const2),
-            anywhere,
+            pl.BlockSpec(memory_space=pltpu.HBM),
             anywhere,
             anywhere,
         ],
@@ -614,6 +688,10 @@
     return jnp.where(near, m, 0.0).astype(jnp.bfloat16)
 
 
+def in_hbm(x):
+    return pltpu.with_memory_space_constraint(x, pltpu.HBM)
+
+
 def body(before_scan, after_scan, drift_offsets, drift_fractions):
     scans, rows, cols = before_scan.shape
     n_row, n_col = lax.axis_size("row"), lax.axis_size("col")
@@ -625,18 +703,9 @@
     col_down = [(i, i + 1) for i in range(n_col - 1)]
     col_up = [(j, i) for i, j in col_down]
 
-    top, bot, left, right = pack(after_scan, offs)
+    top, bot = pack(after_scan)
     up = lax.ppermute(bot, "row", row_down)
     dn = lax.ppermute(top, "row", row_up)
-    lcols = lax.ppermute(right, "col", col_down)
-    rcols = lax.ppermute(left, "col", col_up)
-
-    slot = lax.broadcasted_iota(jnp.int32, lcols.shape, 1).astype(jnp.float32)
-    for_up = jnp.where(slot < up[:, 0, 0:1, 0:1] + 2.0, rcols, lcols)
-    for_dn = jnp.where(slot < dn[:, 0, HALO - 1 : HALO, 0:1] + 2.0, rcols, lcols)
-    cup = lax.ppermute(for_dn, "row", row_down)
-    cdn = lax.ppermute(for_up, "row", row_up)
-
     wide = cols + 2 * LANES
     ext_r, ext_c = 24, 72
     wt = mean_weights(col * cols, cols, n_col * cols)
@@ -659,19 +728,30 @@
     mr = ((pi >= 1) & (pi <= n_row * rows - 2)).astype(jnp.float32)
     mr = jnp.broadcast_to(mr[:, None], (rows, LANES))
 
+    mine = jnp.stack([offs[0], fracs[0]])
+    mine, wt, rm, hc, hr, uc, inv, invr, mc, mr = lax.optimization_barrier(
+        (mine, wt, rm, hc, hr, uc, inv, invr, mc, mr)
+    )
+    prev = lax.ppermute(mine, "col", col_down)
+    following = lax.ppermute(mine, "col", col_up)
+    left, right = edge_rows(prev, following, after_scan, up, dn)
+    lcols = lax.ppermute(right, "col", col_down)
+    rcols = lax.ppermute(left, "col", col_up)
+    own = own_rows(mine, after_scan, up, dn)
+    beforet = in_hbm(flip(lax.optimization_barrier((before_scan, left))[0]))
     diff, edge_l, edge_r, y = resample(
-        offs, fracs, wt, rm, hc, ext_c, after_scan, flip(before_scan), up, dn, lcols, rcols, cup, cdn
+        offs, fracs, wt, rm, hc, ext_c, own, lcols, rcols, beforet
     )
     lstrip = lax.ppermute(edge_r, "col", col_down)
     rstrip = lax.ppermute(edge_l, "col", col_up)
+    ac, ftop, fbot = across(inv, diff, lstrip, rstrip)
+    y, ftop, fbot = lax.optimization_barrier((y, ftop, fbot))
     y = lax.all_to_all(y, "col", 0, 0, tiled=True)
-    ac, ftop, fbot = across(inv, diff, lstrip, rstrip)
-    y, ac, ftop, fbot = lax.optimization_barrier((y, ac, ftop, fbot))
-    z = long_rows(y, hr, scans)
     upr = lax.ppermute(fbot, "row", row_down)
     dnr = lax.ppermute(ftop, "row", row_up)
+    z = long_rows(y, hr, scans)
     z = lax.all_to_all(z, "row", 0, 0, tiled=True)
-    band, slope, sums = final(z, uc, invr, mc, mr, ac, upr, dnr)
+    band, slope, sums = final(z, uc, invr, mc, mr, in_hbm(ac), upr, dnr)
 
     mine = jnp.sum(sums, axis=2).T.reshape(1, 2 * scans)
     mine = jnp.broadcast_to(mine[:, None, :], (n_row * n_col, 1, 2 * scans))

time: 184 us -> 165 us (0.90)
  waiting for transfers between devices: 52.9 us -> 26.8 us
  blocking collectives: 18.6 us -> 28 us
  starting transfers between devices: 42.8 us -> 45.9 us
  other arithmetic: 8.38 us -> 5.76 us
  Pallas kernels: 53.2 us -> 51.1 us
    ppermute x1, waiting for transfers between devices: 25.2 us -> 0.1 us  [body(): lcols = lax.ppermute(right, 'col', col_down)]
    all_to_all x1, starting transfers between devices: 3.51 us -> 17.3 us  [body(): z = lax.all_to_all(z, 'row', 0, 0, tiled=True)]
    all_to_all x0 -> x1, blocking collectives: none -> 13.6 us  [body(): y = lax.all_to_all(y, 'col', 0, 0, tiled=True)]
    all_to_all x1 -> x0, starting transfers between devices: 12.9 us -> none  [body(): y = lax.all_to_all(y, 'col', 0, 0, tiled=True)]
    pallas_call x1 -> x3, Pallas kernels: 5.22 us -> 14.7 us  [the longest x1 5.89 us: own_rows(): pl.pallas_call(own_rows_kernel, in_specs=[smem] + [anywhere] * 3, out_spe...]
    pallas_call x1, Pallas kernels: 15.4 us -> 7.61 us  [resample(): pl.pallas_call(resample_kernel, in_specs=[smem, smem, vmem, vmem, vmem] +...]
    ppermute x2, waiting for transfers between devices: 6.02 us -> 0.7 us  [the longest x1 0.7 us: body(): prev = lax.ppermute(mine, 'col', col_down)]
    ppermute x1, waiting for transfers between devices: 0.01 us -> 4.39 us  [body(): dn = lax.ppermute(top, 'row', row_up)]
  transfers between devices with their start and end apart: 12 -> 11, of which waited for: 8 -> 8; matrix products, arithmetic and copies ran while one was open for 5% -> 4% of each run, Pallas kernels for 8% -> 7%
where the time goes in v3:
time: 165 us; the launch traced here: 164 us
  Pallas kernels  51.1 us (31%)
  starting transfers between devices  45.9 us (28%)
  blocking collectives  28 us (17%)
  waiting for transfers between devices  26.8 us (16%)
  other arithmetic  5.76 us (3%)
  local copies, waits for them, and re-layouts  5.45 us (3%)
    all_to_all x1, starting transfers between devices, body(): z = lax.all_to_all(z, 'row', 0, 0, tiled=True)  17.3 us
    all_to_all x1, blocking collectives, body(): every = lax.all_to_all(mine, ('row', 'col'), 0, 0, tiled=True)  14.4 us
    pallas_call x1, Pallas kernels, final(): pl.pallas_call(final_kernel, grid=(scans,), in_specs=[pl.BlockSpec(z.shap...  14.2 us
    all_to_all x1, blocking collectives, body(): y = lax.all_to_all(y, 'col', 0, 0, tiled=True)  13.6 us
    ppermute x1, waiting for transfers between devices, body(): up = lax.ppermute(bot, 'row', row_down)  9.07 us
    pallas_call x1, Pallas kernels, resample(): pl.pallas_call(resample_kernel, in_specs=[smem, smem, vmem, vmem, vmem] +...  7.61 us
    pallas_call x1, Pallas kernels, across(): pl.pallas_call(across_kernel, in_specs=[vmem, anywhere, anywhere, anywher...  6.64 us
    pallas_call x1, Pallas kernels, own_rows(): pl.pallas_call(own_rows_kernel, in_specs=[smem] + [anywhere] * 3, out_spe...  5.89 us
  transfers between devices with their start and end apart: 11, of which 8 were waited for; matrix products, arithmetic and copies ran while one was open for 4% of the time, Pallas kernels for 7%

profile of v3, /device:TPU:1, one launch (start us, length us, event | category | flops | bytes accessed | tf_op | source)
XLA Modules:
  0.0 164.2 jit_solution(5422649363913159707)
XLA Ops:
  0.7 4.8 %pack.1 = (f32[4,8,136,128]{3,2,1,0:T(8,128)}, f32[4,8,136,128]{3,2,1,0:T(8,128)}) custom-call(f32[4,256,1024]{2,1,0:T(8,128)} %after.3), custom_call_target="tpu_custom_call" | custom-call | tf_op jit(solution)/shard_map/pack/pallas_call | solution.py:41
  5.5 4.5 %collective-permute-start = (f32[4,8,136,128]{3,2,1,0:T(8,128)}, f32[4,8,136,128]{3,2,1,0:T(8,128)S(1)}, u32[]{:S(2)}, u32[]{:S(2)}) collective-permute-start(f32[4,8,136,128]{3,2,1,0:T(8,128)} %get-tuple-element.35), channel_id=1, source_target_pairs={{0,8},{8,16},{16,24},{24,32},{32,40},{40,48},{48,56},{56,64},{64,7... | collective-permute-start | bytes 6684680 | tf_op jit(solution)/shard_map/ppermute | solution.py:707
  10.0 1.9 %collective-permute-start.1 = (f32[4,8,136,128]{3,2,1,0:T(8,128)}, f32[4,8,136,128]{3,2,1,0:T(8,128)}, u32[]{:S(2)}, u32[]{:S(2)}) collective-permute-start(f32[4,8,136,128]{3,2,1,0:T(8,128)} %get-tuple-element.36), channel_id=1, source_target_pairs={{8,0},{16,8},{24,16},{32,24},{40,32},{48,40},{56,48},{64,56},{72,6... | collective-permute-start | bytes 6684680 | tf_op jit(solution)/shard_map/ppermute | solution.py:708
  12.3 0.6 and_convert_fusion.mc_ref
  13.5 0.1 min.33
  13.8 0.7 select_add_fusion.2
  14.5 0.2 pad_bitcast_fusion.3
  14.7 0.3 exponential_reduce_fusion.1
  14.9 0.6 exponential_reduce_fusion
  15.6 0.9 divide_select_fusion.1.hr_ref
  16.4 0.9 divide_select_fusion.hc_ref
  17.4 1.0 fusion.9.uc_ref
  18.3 0.7 broadcast_in_dim.579.wt_ref
  19.0 0.1 broadcast_in_dim.612.mr_ref
  19.1 0.1 broadcast_in_dim.611.invr_ref
  19.2 0.2 broadcast_in_dim.605.invc_ref
  19.4 1.3 collective-permute-start.3
  20.7 4.2 %collective-permute-start.2 = (s32[2,4]{1,0:T(2,128)S(1)}, s32[2,4]{1,0:T(2,128)S(1)}, u32[]{:S(2)}, u32[]{:S(2)}) collective-permute-start(s32[2,4]{1,0:T(2,128)S(1)} %pad_add_fusion.mine_ref), channel_id=1, source_target_pairs={{0,1},{1,2},{2,3},{3,4},{4,5},{5,6},{6,7},{8,9},{9,10},{10,11},{11... | collective-permute-start | bytes 104 | tf_op jit(solution)/shard_map/ppermute | solution.py:735
  24.9 0.7 collective-permute-done.2.prev_ref
  25.6 9.1 %collective-permute-done.up = f32[4,8,136,128]{3,2,1,0:T(8,128)S(1)} collective-permute-done((f32[4,8,136,128]{3,2,1,0:T(8,128)}, f32[4,8,136,128]{3,2,1,0:T(8,128)S(1)}, u32[]{:S(2)}, u32[]{:S(2)}) %collective-permute-start) | collective-permute-done | bytes 2228256 | tf_op jit(solution)/shard_map/ppermute | solution.py:707
  34.7 4.4 %collective-permute-done.1.dn = f32[4,8,136,128]{3,2,1,0:T(8,128)} collective-permute-done((f32[4,8,136,128]{3,2,1,0:T(8,128)}, f32[4,8,136,128]{3,2,1,0:T(8,128)}, u32[]{:S(2)}, u32[]{:S(2)}) %collective-permute-start.1) | collective-permute-done | bytes 2228256 | tf_op jit(solution)/shard_map/ppermute | solution.py:708
  39.1 4.0 %edge_rows.1 = (f32[4,2,136,128]{3,2,1,0:T(8,128)}, f32[4,2,136,128]{3,2,1,0:T(8,128)}) custom-call(s32[2,4]{1,0:T(2,128)S(1)} %collective-permute-done.2.prev_ref, s32[2,4]{1,0:T(2,128)S(1)} %collective-permute-done.3.next_ref, f32[4,256,1024]{2,1,0:T(8,128)S(1)} %copy-done, f32[4,8,136,128]{3,2,1,0:T(8,128)S(1)} %collective-permute-done.up, ...), custom_call_target="tpu_custom_call" | custom-call | tf_op jit(solution)/shard_map/edge_rows/pallas_call | solution.py:161
  43.1 4.7 %collective-permute-start.4 = (f32[4,2,136,128]{3,2,1,0:T(8,128)}, f32[4,2,136,128]{3,2,1,0:T(8,128)}, u32[]{:S(2)}, u32[]{:S(2)}) collective-permute-start(f32[4,2,136,128]{3,2,1,0:T(8,128)} %get-tuple-element.37), channel_id=1, source_target_pairs={{0,1},{1,2},{2,3},{3,4},{4,5},{5,6},{6,7},{8,9},{9,10},{10,11},{11... | collective-permute-start | bytes 1671176 | tf_op jit(solution)/shard_map/ppermute | solution.py:738
  47.7 1.3 collective-permute-start.5
  49.0 5.2 %flip.1.beforet = f32[4,2,1024,128]{3,2,1,0:T(8,128)} custom-call(f32[4,256,1024]{2,1,0:T(8,128)} %x_ref.2), custom_call_target="tpu_custom_call" | custom-call | flops 1048576 | bytes 8388608 | tf_op jit(solution)/shard_map/flip/pallas_call | solution.py:62
  54.2 2.2 %copy-done.1 = f32[4,256,1024]{2,1,0:T(8,128)S(1)} copy-done((f32[4,256,1024]{2,1,0:T(8,128)S(1)}, f32[4,256,1024]{2,1,0:T(8,128)}, u32[]{:S(2)}) %copy-start.1) | copy-done | bytes 4194328
  56.4 0.7 copy-done.7
  57.1 5.9 %own_rows.1.own = f32[4,2,1024,128]{3,2,1,0:T(8,128)S(1)} custom-call(s32[2,4]{1,0:T(2,128)S(1)} %copy-done.7, f32[4,256,1024]{2,1,0:T(8,128)S(1)} %copy-done.1, f32[4,8,136,128]{3,2,1,0:T(8,128)S(1)} %collective-permute-done.up, f32[4,8,136,128]{3,2,1,0:T(8,128)} %collective-permute-done.1.dn), custom_call_target="tpu_custom_call" | custom-call | flops 8388608 | bytes 16777216 | tf_op jit(solution)/shard_map/own_rows/pallas_call | solution.py:217
  63.0 0.1 collective-permute-done.4.lcols
  63.1 7.6 %resample.1 = (f32[4,2,1024,128]{3,2,1,0:T(8,128)S(1)}, f32[4,2,8,128]{3,2,1,0:T(8,128)S(1)}, f32[4,2,8,128]{3,2,1,0:T(8,128)S(1)}, f32[8,72,128]{2,1,0:T(8,128)S(1)}) custom-call(s32[2,4]{1,0:T(2,128)S(1)} %bitcast.15, s32[2,4]{1,0:T(2,128)S(1)} %bitcast.16, f32[64,128]{1,0:T(8,128)S(1)} %copy-done.4, f32[4,256,128]{2,1,0:T(8,128)S(1)} %pad_maximum_fusion.rm_ref, ...), custom_call_target="tpu_custom_call" | custom-call | tf_op jit(solution)/shard_map/resample/pallas_call | solution.py:330
  70.8 4.0 %collective-permute-start.6 = (f32[4,2,8,128]{3,2,1,0:T(8,128)S(1)}, f32[4,2,8,128]{3,2,1,0:T(8,128)S(1)}, u32[]{:S(2)}, u32[]{:S(2)}) collective-permute-start(f32[4,2,8,128]{3,2,1,0:T(8,128)S(1)} %get-tuple-element.43), channel_id=1, source_target_pairs={{0,1},{1,2},{2,3},{3,4},{4,5},{5,6},{6,7},{8,9},{9,10},{10,11},{11... | collective-permute-start | bytes 98312 | tf_op jit(solution)/shard_map/ppermute | solution.py:745
  74.8 1.3 collective-permute-start.7
  76.1 3.5 %collective-permute-done.7.rstrip = f32[4,2,8,128]{3,2,1,0:T(8,128)S(1)} collective-permute-done((f32[4,2,8,128]{3,2,1,0:T(8,128)S(1)}, f32[4,2,8,128]{3,2,1,0:T(8,128)S(1)}, u32[]{:S(2)}, u32[]{:S(2)}) %collective-permute-start.7) | collective-permute-done | bytes 32800 | tf_op jit(solution)/shard_map/ppermute | solution.py:746
  79.6 6.6 %across.1 = (f32[4,10,256,128]{3,2,1,0:T(8,128)}, f32[4,10,8,128]{3,2,1,0:T(8,128)S(1)}, f32[4,10,8,128]{3,2,1,0:T(8,128)S(1)}) custom-call(f32[1040,128]{1,0:T(8,128)S(1)} %broadcast_in_dim.605.invc_ref, f32[4,2,1024,128]{3,2,1,0:T(8,128)S(1)} %get-tuple-element.42.diff, f32[4,2,8,128]{3,2,1,0:T(8,128)S(1)} %collective-permute-done.6.lstrip, ...), custom_call_target="tpu_custom_call" | custom-call | flops 20971520 | bytes 8388608 | tf_op jit(solution)/shard_map/across/pallas_call | solution.py:453
  86.3 13.6 %all_to_all.15.y_ref = f32[8,72,128]{2,1,0:T(8,128)} all-to-all(f32[8,72,128]{2,1,0:T(8,128)S(1)} %get-tuple-element.47), channel_id=1, replica_groups=mesh['row'=16,'col'=8] {'col'}, dimensions={0} | all-to-all | bytes 589824 | tf_op jit(solution)/shard_map/all_to_all | solution.py:749
  99.9 2.7 %long_rows.1 = f32[16,4,24,128]{3,2,1,0:T(8,128)} custom-call(f32[8,72,128]{2,1,0:T(8,128)} %all_to_all.15.y_ref, f32[384,24]{1,0:T(8,128)} %divide_select_fusion.1.hr_ref), custom_call_target="tpu_custom_call" | custom-call | tf_op jit(solution)/shard_map/long_rows/pallas_call | solution.py:370
  102.6 17.3 %all-to-all-start.1 = ((f32[16,4,24,128]{3,2,1,0:T(8,128)}), f32[16,4,24,128]{3,2,1,0:T(8,128)S(1)}, u32[]{:S(2)}, u32[]{:S(2)}) async-start(f32[16,4,24,128]{3,2,1,0:T(8,128)} %long_rows.1), calls=%async_computation.1 | async-start | bytes 1572864 | tf_op jit(solution)/shard_map/all_to_all | solution.py:753
  119.9 3.5 %collective-permute-start.8 = (f32[4,10,8,128]{3,2,1,0:T(8,128)S(1)}, f32[4,10,8,128]{3,2,1,0:T(8,128)S(1)}, u32[]{:S(2)}, u32[]{:S(2)}) collective-permute-start(f32[4,10,8,128]{3,2,1,0:T(8,128)S(1)} %get-tuple-element.54), channel_id=1, source_target_pairs={{0,8},{8,16},{16,24},{24,32},{32,40},{40,48},{48,56},{56,64},{64,7... | collective-permute-start | bytes 491528 | tf_op jit(solution)/shard_map/ppermute | solution.py:750
  123.5 1.9 %collective-permute-start.9 = (f32[4,10,8,128]{3,2,1,0:T(8,128)S(1)}, f32[4,10,8,128]{3,2,1,0:T(8,128)S(1)}, u32[]{:S(2)}, u32[]{:S(2)}) collective-permute-start(f32[4,10,8,128]{3,2,1,0:T(8,128)S(1)} %get-tuple-element.55), channel_id=1, source_target_pairs={{8,0},{16,8},{24,16},{32,24},{40,32},{48,40},{56,48},{64,56},{72,6... | collective-permute-start | bytes 491528 | tf_op jit(solution)/shard_map/ppermute | solution.py:751
  125.4 5.4 %collective-permute-done.8.upr = f32[4,10,8,128]{3,2,1,0:T(8,128)S(1)} collective-permute-done((f32[4,10,8,128]{3,2,1,0:T(8,128)S(1)}, f32[4,10,8,128]{3,2,1,0:T(8,128)S(1)}, u32[]{:S(2)}, u32[]{:S(2)}) %collective-permute-start.8) | collective-permute-done | bytes 163872 | tf_op jit(solution)/shard_map/ppermute | solution.py:750
  130.8 2.1 %collective-permute-done.9.dnr = f32[4,10,8,128]{3,2,1,0:T(8,128)S(1)} collective-permute-done((f32[4,10,8,128]{3,2,1,0:T(8,128)S(1)}, f32[4,10,8,128]{3,2,1,0:T(8,128)S(1)}, u32[]{:S(2)}, u32[]{:S(2)}) %collective-permute-start.9) | collective-permute-done | bytes 163872 | tf_op jit(solution)/shard_map/ppermute | solution.py:751
  133.0 1.5 all-to-all-done.1.z_ref
  134.4 14.2 %final.1 = (f32[4,256,1024]{2,1,0:T(8,128)}, f32[4,256,1024]{2,1,0:T(8,128)}, f32[4,2,128]{2,1,0:T(2,128)S(1)}) custom-call(f32[16,4,24,128]{3,2,1,0:T(8,128)S(1)} %all-to-all-done.1.z_ref, bf16[128,1280]{1,0:T(8,128)(2,1)S(1)} %copy-done.2, f32[272,128]{1,0:T(8,128)S(1)} %broadcast_in_dim.611.invr_ref, f32[1,1024]{1,0:T(1,128)S(1)} %copy-done.5, ...), custom_call_target="tpu_custom_call" | custom-call | tf_op jit(solution)/shard_map/final/pallas_call | solution.py:590
  148.6 0.1 reduce_sum.38
  148.7 0.1 copy.14
  149.0 14.4 %all_to_all.16 = f32[128,1,8]{2,1,0:T(1,128)S(1)} all-to-all(f32[128,1,8]{2,1,0:T(1,128)S(1)} %broadcast_in_dim.614), channel_id=1, replica_groups=mesh['row'=16,'col'=8] {'row','col'}, dimensions={0} | all-to-all | bytes 8192 | tf_op jit(solution)/shard_map/all_to_all | solution.py:758
  163.4 0.2 reduce_sum.39
  163.5 0.7 sqrt.7
  (70 shorter events, 1.2 us)
Async XLA Ops:
  0.6 12.3 %copy-start.13 = (s32[8]{0:T(128)S(1)}, s32[8]{0:T(128)}, u32[]{:S(2)}) copy-start(s32[8]{0:T(128)} %constant.477.clone) | copy-start | bytes 100
  0.6 12.6 %copy-start.12 = (s32[8]{0:T(128)S(1)}, s32[8]{0:T(128)}, u32[]{:S(2)}) copy-start(s32[8]{0:T(128)} %constant.478.clone) | copy-start | bytes 100
  0.7 12.9 %copy-start.10 = (s32[2,4,1,1]{1,3,2,0:T(1,128)S(1)}, s32[2,4,1,1]{1,3,2,0:T(1,128)}, u32[]{:S(2)}) copy-start(s32[2,4,1,1]{1,3,2,0:T(1,128)} %param.9) | copy-start | bytes 100
  0.7 12.9 %copy-start.8 = (s32[2,4,1,1]{1,3,2,0:T(1,128)S(1)}, s32[2,4,1,1]{1,3,2,0:T(1,128)}, u32[]{:S(2)}) copy-start(s32[2,4,1,1]{1,3,2,0:T(1,128)} %param.8) | copy-start | bytes 100
  5.5 29.2 %collective-permute-start = (f32[4,8,136,128]{3,2,1,0:T(8,128)}, f32[4,8,136,128]{3,2,1,0:T(8,128)S(1)}, u32[]{:S(2)}, u32[]{:S(2)}) collective-permute-start(f32[4,8,136,128]{3,2,1,0:T(8,128)} %get-tuple-element.35), channel_id=1, source_target_pairs={{0,8},{8,16},{16,24},{24,32},{32,40},{40,48},{48,56},{56,64},{64,7... | collective-permute-start | bytes 6684680 | tf_op jit(solution)/shard_map/ppermute | solution.py:707
  10.0 29.1 %collective-permute-start.1 = (f32[4,8,136,128]{3,2,1,0:T(8,128)}, f32[4,8,136,128]{3,2,1,0:T(8,128)}, u32[]{:S(2)}, u32[]{:S(2)}) collective-permute-start(f32[4,8,136,128]{3,2,1,0:T(8,128)} %get-tuple-element.36), channel_id=1, source_target_pairs={{8,0},{16,8},{24,16},{32,24},{40,32},{48,40},{56,48},{64,56},{72,6... | collective-permute-start | bytes 6684680 | tf_op jit(solution)/shard_map/ppermute | solution.py:708
  13.6 25.5 %copy-start = (f32[4,256,1024]{2,1,0:T(8,128)S(1)}, f32[4,256,1024]{2,1,0:T(8,128)}, u32[]{:S(2)}) copy-start(f32[4,256,1024]{2,1,0:T(8,128)} %after.3) | copy-start | bytes 12582916
  13.7 21.0 %copy-start.6 = (s32[2,4]{1,0:T(2,128)}, s32[2,4]{1,0:T(2,128)S(1)}, u32[]{:S(2)}) copy-start(s32[2,4]{1,0:T(2,128)S(1)} %pad_add_fusion.mine_ref) | copy-start | bytes 100
  19.4 5.5 %collective-permute-start.3 = (s32[2,4]{1,0:T(2,128)S(1)}, s32[2,4]{1,0:T(2,128)S(1)}, u32[]{:S(2)}, u32[]{:S(2)}) collective-permute-start(s32[2,4]{1,0:T(2,128)S(1)} %pad_add_fusion.mine_ref), channel_id=1, source_target_pairs={{1,0},{2,1},{3,2},{4,3},{5,4},{6,5},{7,6},{9,8},{10,9},{11,10},{12... | collective-permute-start | bytes 104 | tf_op jit(solution)/shard_map/ppermute | solution.py:736
  20.7 4.9 %collective-permute-start.2 = (s32[2,4]{1,0:T(2,128)S(1)}, s32[2,4]{1,0:T(2,128)S(1)}, u32[]{:S(2)}, u32[]{:S(2)}) collective-permute-start(s32[2,4]{1,0:T(2,128)S(1)} %pad_add_fusion.mine_ref), channel_id=1, source_target_pairs={{0,1},{1,2},{2,3},{3,4},{4,5},{5,6},{6,7},{8,9},{9,10},{10,11},{11... | collective-permute-start | bytes 104 | tf_op jit(solution)/shard_map/ppermute | solution.py:735
  43.1 20.0 %collective-permute-start.4 = (f32[4,2,136,128]{3,2,1,0:T(8,128)}, f32[4,2,136,128]{3,2,1,0:T(8,128)}, u32[]{:S(2)}, u32[]{:S(2)}) collective-permute-start(f32[4,2,136,128]{3,2,1,0:T(8,128)} %get-tuple-element.37), channel_id=1, source_target_pairs={{0,1},{1,2},{2,3},{3,4},{4,5},{5,6},{6,7},{8,9},{9,10},{10,11},{11... | collective-permute-start | bytes 1671176 | tf_op jit(solution)/shard_map/ppermute | solution.py:738
  47.7 15.4 %collective-permute-start.5 = (f32[4,2,136,128]{3,2,1,0:T(8,128)}, f32[4,2,136,128]{3,2,1,0:T(8,128)}, u32[]{:S(2)}, u32[]{:S(2)}) collective-permute-start(f32[4,2,136,128]{3,2,1,0:T(8,128)} %get-tuple-element.38), channel_id=1, source_target_pairs={{1,0},{2,1},{3,2},{4,3},{5,4},{6,5},{7,6},{9,8},{10,9},{11,10},{12... | collective-permute-start | bytes 1671176 | tf_op jit(solution)/shard_map/ppermute | solution.py:739
  54.2 2.2 %copy-start.1 = (f32[4,256,1024]{2,1,0:T(8,128)S(1)}, f32[4,256,1024]{2,1,0:T(8,128)}, u32[]{:S(2)}) copy-start(f32[4,256,1024]{2,1,0:T(8,128)} %after.3) | copy-start | bytes 12582916
  56.4 0.7 copy-start.7
  57.1 6.0 %copy-start.3 = (f32[576,80]{1,0:T(8,128)S(1)}, f32[576,80]{1,0:T(8,128)}, u32[]{:S(2)}) copy-start(f32[576,80]{1,0:T(8,128)} %divide_select_fusion.hc_ref) | copy-start | bytes 552964
  57.1 6.0 %copy-start.4 = (f32[64,128]{1,0:T(8,128)S(1)}, f32[64,128]{1,0:T(8,128)}, u32[]{:S(2)}) copy-start(f32[64,128]{1,0:T(8,128)} %broadcast_in_dim.579.wt_ref) | copy-start | bytes 98308
  57.1 6.0 %copy-start.9 = (s32[2,4,1,1]{1,3,2,0:T(1,128)S(1)}, s32[2,4,1,1]{1,3,2,0:T(1,128)}, u32[]{:S(2)}) copy-start(s32[2,4,1,1]{1,3,2,0:T(1,128)} %param.8) | copy-start | bytes 100
  57.1 6.0 %copy-start.11 = (s32[2,4,1,1]{1,3,2,0:T(1,128)S(1)}, s32[2,4,1,1]{1,3,2,0:T(1,128)}, u32[]{:S(2)}) copy-start(s32[2,4,1,1]{1,3,2,0:T(1,128)} %param.9) | copy-start | bytes 100
  70.8 5.3 %collective-permute-start.6 = (f32[4,2,8,128]{3,2,1,0:T(8,128)S(1)}, f32[4,2,8,128]{3,2,1,0:T(8,128)S(1)}, u32[]{:S(2)}, u32[]{:S(2)}) collective-permute-start(f32[4,2,8,128]{3,2,1,0:T(8,128)S(1)} %get-tuple-element.43), channel_id=1, source_target_pairs={{0,1},{1,2},{2,3},{3,4},{4,5},{5,6},{6,7},{8,9},{9,10},{10,11},{11... | collective-permute-start | bytes 98312 | tf_op jit(solution)/shard_map/ppermute | solution.py:745
  74.8 4.8 %collective-permute-start.7 = (f32[4,2,8,128]{3,2,1,0:T(8,128)S(1)}, f32[4,2,8,128]{3,2,1,0:T(8,128)S(1)}, u32[]{:S(2)}, u32[]{:S(2)}) collective-permute-start(f32[4,2,8,128]{3,2,1,0:T(8,128)S(1)} %get-tuple-element.44), channel_id=1, source_target_pairs={{1,0},{2,1},{3,2},{4,3},{5,4},{6,5},{7,6},{9,8},{10,9},{11,10},{12... | collective-permute-start | bytes 98312 | tf_op jit(solution)/shard_map/ppermute | solution.py:746
  86.2 48.2 %copy-start.2 = (bf16[128,1280]{1,0:T(8,128)(2,1)S(1)}, bf16[128,1280]{1,0:T(8,128)(2,1)}, u32[]{:S(2)}) copy-start(bf16[128,1280]{1,0:T(8,128)(2,1)} %fusion.9.uc_ref) | copy-start | bytes 983044
  86.2 48.2 %copy-start.5 = (f32[1,1024]{1,0:T(1,128)S(1)}, f32[1,1024]{1,0:T(1,128)}, u32[]{:S(2)}) copy-start(f32[1,1024]{1,0:T(1,128)} %and_convert_fusion.mc_ref) | copy-start | bytes 12292
  102.6 31.8 %all-to-all-start.1 = ((f32[16,4,24,128]{3,2,1,0:T(8,128)}), f32[16,4,24,128]{3,2,1,0:T(8,128)S(1)}, u32[]{:S(2)}, u32[]{:S(2)}) async-start(f32[16,4,24,128]{3,2,1,0:T(8,128)} %long_rows.1), calls=%async_computation.1 | async-start | bytes 1572864 | tf_op jit(solution)/shard_map/all_to_all | solution.py:753
  119.9 10.9 %collective-permute-start.8 = (f32[4,10,8,128]{3,2,1,0:T(8,128)S(1)}, f32[4,10,8,128]{3,2,1,0:T(8,128)S(1)}, u32[]{:S(2)}, u32[]{:S(2)}) collective-permute-start(f32[4,10,8,128]{3,2,1,0:T(8,128)S(1)} %get-tuple-element.54), channel_id=1, source_target_pairs={{0,8},{8,16},{16,24},{24,32},{32,40},{40,48},{48,56},{56,64},{64,7... | collective-permute-start | bytes 491528 | tf_op jit(solution)/shard_map/ppermute | solution.py:750
  123.5 9.5 %collective-permute-start.9 = (f32[4,10,8,128]{3,2,1,0:T(8,128)S(1)}, f32[4,10,8,128]{3,2,1,0:T(8,128)S(1)}, u32[]{:S(2)}, u32[]{:S(2)}) collective-permute-start(f32[4,10,8,128]{3,2,1,0:T(8,128)S(1)} %get-tuple-element.55), channel_id=1, source_target_pairs={{8,0},{16,8},{24,16},{32,24},{40,32},{48,40},{56,48},{64,56},{72,6... | collective-permute-start | bytes 491528 | tf_op jit(solution)/shard_map/ppermute | solution.py:751

commit v4 on v3

--- a/solution.py
+++ b/solution.py
@@ -1,3 +1,4 @@
+import functools
 import math
 
 import jax
@@ -21,29 +22,40 @@
 VMEM_LIMIT = 24 * 1024 * 1024
 
 
-def lane_iota(rows):
-    return lax.broadcasted_iota(jnp.int32, (rows, LANES), 1)
-
-
-def pack_kernel(x_ref, top_ref, bot_ref):
-    rows, cols = x_ref.shape[1], x_ref.shape[2]
-    for j in range(cols // LANES):
-        sl = slice(j * LANES, (j + 1) * LANES)
-        top_ref[0, j] = x_ref[0, 0:HALO, sl]
-        bot_ref[0, j] = x_ref[0, rows - HALO : rows, sl]
+def pack_kernel(x_ref, top, bot, buf, sem):
+    scans, rows, cols = buf.shape
+
+    def fetch(s):
+        return pltpu.make_async_copy(x_ref.at[s], buf.at[s], sem.at[s])
+
+    for s in range(scans):
+        fetch(s).start()
+
+    def one_scan(s, carry):
+        fetch(s).wait()
+        for j in range(cols // LANES):
+            sl = slice(j * LANES, (j + 1) * LANES)
+            top[s, j] = buf[s, 0:HALO, sl]
+            bot[s, j] = buf[s, rows - HALO : rows, sl]
+        return carry
+
+    lax.fori_loop(0, scans, one_scan, 0)
 
 
 def pack(after):
     scans, rows, cols = after.shape
-    n_tiles = cols // LANES
-    spec = pl.BlockSpec((1, n_tiles, HALO, LANES), lambda s: (s, 0, 0, 0))
-    shape = jax.ShapeDtypeStruct((scans, n_tiles, HALO, LANES), jnp.float32)
+    vmem = pl.BlockSpec(memory_space=pltpu.VMEM)
+    strip = pltpu.VMEM((scans, cols // LANES, HALO, LANES), jnp.float32)
     return pl.pallas_call(
         pack_kernel,
-        grid=(scans,),
-        in_specs=[pl.BlockSpec((1, rows, cols), lambda s: (s, 0, 0))],
-        out_specs=[spec, spec],
-        out_shape=[shape, shape],
+        in_specs=[pl.BlockSpec(memory_space=pltpu.HBM)],
+        out_specs=[vmem, vmem],
+        out_shape=[strip, strip],
+        scratch_shapes=[
+            pltpu.VMEM((scans, rows, cols), jnp.float32),
+            pltpu.SemaphoreType.DMA((scans,)),
+        ],
+        compiler_params=pltpu.CompilerParams(vmem_limit_bytes=VMEM_LIMIT),
         name="pack",
     )(after)
 
@@ -237,8 +249,8 @@
 def resample_kernel(
     offs_ref, fracs_ref, wt_ref, rm_ref, hc_ref,
     own, lcols, rcols, beforet,
-    dif, edge_l, edge_r, y_ref,
-    win, bef, sums, part, sem,
+    diff_out, y_ref,
+    win, bef, dif, sums, part, sem, osem,
 ):
     scans, halves, cols = bef.shape[0], bef.shape[1], bef.shape[2]
 
@@ -252,6 +264,10 @@
 
     start_copies(copies(0), sem.at[0])
     part[...] = jnp.zeros_like(part)
+    col = lax.axis_index("col")
+    n_col = y_ref.shape[0]
+    ext = hc_ref.shape[0] // n_col
+    y_ref[:, ext:, :] = jnp.zeros((n_col, y_ref.shape[1] - ext, LANES), jnp.float32)
     sums[...] = jnp.zeros_like(sums)
     n_blocks = cols // BLOCK
     weight = [wt_ref[8 * i : 8 * i + 8, :] for i in range(8)]
@@ -276,9 +292,21 @@
             return carry
 
         lax.fori_loop(0, cols // CB, col_taps, 0)
-        for h in range(halves):
-            edge_l[s, h] = dif[s, h, 0:EDGE, :]
-            edge_r[s, h] = dif[s, h, cols - EDGE : cols, :]
+        pltpu.make_async_copy(dif.at[s], diff_out.at[s], osem.at[s]).start()
+
+        def put_edge(target, first):
+            for h in range(halves):
+                at = pl.multiple_of(ext + (s * halves + h) * EDGE, EDGE)
+                y_ref[target, pl.ds(at, EDGE), :] = dif[s, h, first : first + EDGE, :]
+
+        @pl.when(col > 0)
+        def _():
+            put_edge(col - 1, 0)
+
+        @pl.when(col < n_col - 1)
+        def _():
+            put_edge(col + 1, cols - EDGE)
+
 
         def block_sums(i, carry):
             for h in range(halves):
@@ -316,9 +344,10 @@
 
     lax.fori_loop(0, scans, one_scan, 0)
     y = jnp.dot(hc_ref[...], part[...], precision=HIGHEST, preferred_element_type=jnp.float32)
-    ext = hc_ref.shape[0] // y_ref.shape[0]
-    for t in range(y_ref.shape[0]):
-        y_ref[t] = y[t * ext : (t + 1) * ext, :]
+    for t in range(n_col):
+        y_ref[t, 0:ext, :] = y[t * ext : (t + 1) * ext, :]
+    for s in range(scans):
+        pltpu.make_async_copy(dif.at[s], diff_out.at[s], osem.at[s]).wait()
 
 
 def resample(offs, fracs, wt, rm, hc, ext, own, lcols, rcols, beforet):
@@ -330,30 +359,30 @@
     return pl.pallas_call(
         resample_kernel,
         in_specs=[smem, smem, vmem, vmem, vmem] + [anywhere] * 4,
-        out_specs=[vmem, vmem, vmem, vmem],
+        out_specs=[pl.BlockSpec(memory_space=pltpu.HBM), vmem],
         out_shape=[
-            pltpu.VMEM((scans, halves, cols, LANES), jnp.float32),
-            jax.ShapeDtypeStruct((scans, halves, EDGE, LANES), jnp.float32),
-            jax.ShapeDtypeStruct((scans, halves, EDGE, LANES), jnp.float32),
-            jax.ShapeDtypeStruct((n_col, ext, LANES), jnp.float32),
+            pltpu.HBM((scans, halves, cols, LANES), jnp.float32),
+            jax.ShapeDtypeStruct((n_col, ext + scans * halves * EDGE, LANES), jnp.float32),
         ],
         scratch_shapes=[
             pltpu.VMEM((scans, halves, cols + 2 * HALO, LANES), jnp.float32),
+            pltpu.VMEM((scans, halves, cols, LANES), jnp.float32),
             pltpu.VMEM((scans, halves, cols, LANES), jnp.float32),
             pltpu.VMEM((hc.shape[1], halves * LANES), jnp.float32),
             pltpu.VMEM((hc.shape[1], LANES), jnp.float32),
             pltpu.SemaphoreType.DMA((scans, 4)),
+            pltpu.SemaphoreType.DMA((scans,)),
         ],
         compiler_params=pltpu.CompilerParams(vmem_limit_bytes=VMEM_LIMIT),
         name="resample",
     )(offs, fracs, wt, rm, hc, own, lcols, rcols, beforet)
 
 
-def long_rows_kernel(y_ref, hr_ref, z_ref):
+def long_rows_kernel(ext_c, y_ref, hr_ref, z_ref):
     n_row, scans, ext, _ = z_ref.shape
-    p = y_ref[0]
+    p = y_ref[0, 0:ext_c, :]
     for t in range(1, y_ref.shape[0]):
-        p = p + y_ref[t]
+        p = p + y_ref[t, 0:ext_c, :]
     p = jnp.concatenate([p, jnp.zeros((LANES - p.shape[0], LANES), jnp.float32)], axis=0).T
     for s in range(scans):
         z = jnp.dot(
@@ -364,11 +393,11 @@
             z_ref[t, s] = z[t * ext : (t + 1) * ext, :]
 
 
-def long_rows(y, hr, scans):
+def long_rows(y, hr, scans, ext_c):
     ext = hr.shape[1]
     vmem = pl.BlockSpec(memory_space=pltpu.VMEM)
     return pl.pallas_call(
-        long_rows_kernel,
+        functools.partial(long_rows_kernel, ext_c),
         in_specs=[vmem, vmem],
         out_specs=vmem,
         out_shape=jax.ShapeDtypeStruct((hr.shape[0] // ext, scans, ext, LANES), jnp.float32),
@@ -379,16 +408,28 @@
 PAD = 2 * EDGE
 
 
-def across_kernel(invc_ref, diff, lstrip, rstrip, ac_out, ftop, fbot, buf, acs, sem, osem):
+def across_kernel(invc_ref, diff, y, ac_out, ftop, fbot, buf, acs, sem, osem):
     scans, halves, cols = diff.shape[0], diff.shape[1], diff.shape[2]
     n_out = cols // LANES
     rows = halves * LANES
+    col = lax.axis_index("col")
+    before = jnp.maximum(col - 1, 0)
+    behind = jnp.minimum(col + 1, y.shape[0] - 1)
+
+    def strip_row(s, h):
+        first = y.shape[1] - scans * halves * EDGE
+        return pl.multiple_of(first + (s * halves + h) * EDGE, EDGE)
 
     def copies(s):
         return [
             (diff.at[s], buf.at[s, :, pl.ds(PAD, cols), :]),
-            (lstrip.at[s], buf.at[s, :, pl.ds(PAD - EDGE, EDGE), :]),
-            (rstrip.at[s], buf.at[s, :, pl.ds(PAD + cols, EDGE), :]),
+        ] + [
+            (
+                y.at[source, pl.ds(strip_row(s, h), EDGE), :],
+                buf.at[s, h, pl.ds(first, EDGE), :],
+            )
+            for h in range(halves)
+            for source, first in ((before, PAD - EDGE), (behind, PAD + cols))
         ]
 
     def fetch(s):
@@ -444,7 +485,7 @@
         pltpu.make_async_copy(acs.at[s], ac_out.at[s], osem.at[s]).wait()
 
 
-def across(invc, diff, lstrip, rstrip):
+def across(invc, diff, y):
     scans, halves, cols, _ = diff.shape
     rows = halves * LANES
     n_wide = cols // LANES + 2
@@ -452,7 +493,7 @@
     vmem = pl.BlockSpec(memory_space=pltpu.VMEM)
     return pl.pallas_call(
         across_kernel,
-        in_specs=[vmem, anywhere, anywhere, anywhere],
+        in_specs=[vmem, pl.BlockSpec(memory_space=pltpu.HBM), anywhere],
         out_specs=[pl.BlockSpec(memory_space=pltpu.HBM), vmem, vmem],
         out_shape=[
             pltpu.HBM((scans, n_wide, rows, LANES), jnp.float32),
@@ -462,7 +503,7 @@
         scratch_shapes=[
             pltpu.VMEM((scans, halves, cols + 2 * PAD, LANES), jnp.float32),
             pltpu.VMEM((scans, n_wide, rows, LANES), jnp.float32),
-            pltpu.SemaphoreType.DMA((scans, 3)),
+            pltpu.SemaphoreType.DMA((scans, 5)),
             pltpu.SemaphoreType.DMA((scans,)),
         ],
         compiler_params=pltpu.CompilerParams(vmem_limit_bytes=VMEM_LIMIT),
@@ -470,13 +511,13 @@
             flops=20 * diff.size, bytes_accessed=8 * diff.size, transcendentals=0
         ),
         name="across",
-    )(invc, diff, lstrip, rstrip)
+    )(invc, diff, y)
 
 
 def final_kernel(
     z_ref, uc_ref, invr_ref, mc_ref, mr_ref, across_in, upr, dnr,
     band_ref, slope_ref, sum_ref,
-    acs, cu, bd, sem,
+    acs, cu, bd, bt, sem,
 ):
     s = pl.program_id(0)
     scans, n_wide = acs.shape[0], acs.shape[1]
@@ -547,35 +588,47 @@
 
     lax.fori_loop(0, rows // BLOCK + 1, band_rows, 0)
 
-    lane = lane_iota(BLOCK)
-    first = lane >= 1
-    last = lane < LANES - 1
-
-    def slope_rows(c, carry):
+    halves = rows // LANES
+
+    def turn(i, carry):
+        done = [
+            bd[2 * i + n, EDGE + h * LANES : EDGE + (h + 1) * LANES, :].T
+            for n in range(2)
+            for h in range(halves)
+        ]
+        for n in range(2):
+            at = pl.multiple_of((2 * i + n) * LANES, LANES)
+            for h in range(halves):
+                bt[h, pl.ds(at, LANES), :] = done[n * halves + h]
+        return carry
+
+    lax.fori_loop(0, n_wide // 2, turn, 0)
+
+    def slope_tile(j, carry):
         s1, s2 = carry
-        base = pl.multiple_of(c * BLOCK, BLOCK)
-        here = [bd[j, pl.ds(base + EDGE, BLOCK), :] for j in range(n_wide)]
-        fwd = [pltpu.roll(t, LANES - 1, 1) for t in here[1:]]
-        bwd = [pltpu.roll(t, 1, 1) for t in here[:-1]]
-        mr = mr_ref[pl.ds(base, BLOCK), :]
-        for j in range(n_out):
-            so = slice(j * LANES, (j + 1) * LANES)
-            gc = jnp.where(last, fwd[j], fwd[j + 1]) - jnp.where(first, bwd[j + 1], bwd[j])
-            gc = gc * mc_ref[0:1, so]
+        lanes = pl.ds(pl.multiple_of(j * LANES, LANES), LANES)
+        at = pl.multiple_of((j + 1) * LANES, LANES)
+        squares = []
+        for h in range(halves):
+            g = bt[h, pl.ds(at + 1, LANES), :] - bt[h, pl.ds(at - 1, LANES), :]
+            squares.append((g * g).T)
+        for h in range(halves):
+            first = h * LANES
+            here = slice(first, first + LANES)
             gr = (
-                bd[j + 1, pl.ds(base + EDGE + 1, BLOCK), :]
-                - bd[j + 1, pl.ds(base + EDGE - 1, BLOCK), :]
-            ) * mr
-            sq = gc * gc + gr * gr
-            v = here[j + 1]
-            band_ref[0, pl.ds(base, BLOCK), so] = v
-            slope_ref[0, pl.ds(base, BLOCK), so] = sq
-            s1 = s1 + v * v
-            s2 = s2 + sq
+                bd[j + 1, first + EDGE + 1 : first + EDGE + 1 + LANES, :]
+                - bd[j + 1, first + EDGE - 1 : first + EDGE - 1 + LANES, :]
+            ) * mr_ref[here, :]
+            sq = squares[h] * mc_ref[0:1, lanes] + gr * gr
+            v = bd[j + 1, first + EDGE : first + EDGE + LANES, :]
+            band_ref[0, here, lanes] = v
+            slope_ref[0, here, lanes] = sq
+            s1 = s1 + jnp.sum((v * v).reshape(BLOCK, 8, LANES), axis=0)
+            s2 = s2 + jnp.sum(sq.reshape(BLOCK, 8, LANES), axis=0)
         return s1, s2
 
-    zero = jnp.zeros((BLOCK, LANES), jnp.float32)
-    s1, s2 = lax.fori_loop(0, rows // BLOCK, slope_rows, (zero, zero))
+    zero = jnp.zeros((8, LANES), jnp.float32)
+    s1, s2 = lax.fori_loop(0, n_out, slope_tile, (zero, zero))
     sum_ref[0, 0:1, :] = jnp.sum(s1, axis=0, keepdims=True)
     sum_ref[0, 1:2, :] = jnp.sum(s2, axis=0, keepdims=True)
 
@@ -614,6 +667,7 @@
             pltpu.VMEM((scans, n_wide, rows + 2 * PAD, LANES), jnp.float32),
             pltpu.VMEM((scans, n_wide, ext, LANES), jnp.float32),
             pltpu.VMEM((n_wide, rows + 2 * EDGE, LANES), jnp.float32),
+            pltpu.VMEM((rows // LANES, n_wide * LANES, LANES), jnp.float32),
             pltpu.SemaphoreType.DMA((scans, 3)),
         ],
         compiler_params=pltpu.CompilerParams(vmem_limit_bytes=VMEM_LIMIT),
@@ -703,7 +757,7 @@
     col_down = [(i, i + 1) for i in range(n_col - 1)]
     col_up = [(j, i) for i, j in col_down]
 
-    top, bot = pack(after_scan)
+    top, bot = pack(in_hbm(after_scan))
     up = lax.ppermute(bot, "row", row_down)
     dn = lax.ppermute(top, "row", row_up)
     wide = cols + 2 * LANES
@@ -739,17 +793,12 @@
     rcols = lax.ppermute(left, "col", col_up)
     own = own_rows(mine, after_scan, up, dn)
     beforet = in_hbm(flip(lax.optimization_barrier((before_scan, left))[0]))
-    diff, edge_l, edge_r, y = resample(
-        offs, fracs, wt, rm, hc, ext_c, own, lcols, rcols, beforet
-    )
-    lstrip = lax.ppermute(edge_r, "col", col_down)
-    rstrip = lax.ppermute(edge_l, "col", col_up)
-    ac, ftop, fbot = across(inv, diff, lstrip, rstrip)
-    y, ftop, fbot = lax.optimization_barrier((y, ftop, fbot))
+    diff, y = resample(offs, fracs, wt, rm, hc, ext_c, own, lcols, rcols, beforet)
     y = lax.all_to_all(y, "col", 0, 0, tiled=True)
+    z = long_rows(y, hr, scans, ext_c)
+    ac, ftop, fbot = across(inv, in_hbm(diff), y)
     upr = lax.ppermute(fbot, "row", row_down)
     dnr = lax.ppermute(ftop, "row", row_up)
-    z = long_rows(y, hr, scans)
     z = lax.all_to_all(z, "row", 0, 0, tiled=True)
     band, slope, sums = final(z, uc, invr, mc, mr, in_hbm(ac), upr, dnr)
 

time: 165 us -> 158 us (0.958)
  waiting for transfers between devices: 26.8 us -> 19 us
  blocking collectives: 28 us -> 34.1 us
  starting transfers between devices: 45.9 us -> 39.9 us
    ppermute x2 -> x0, starting transfers between devices: 5.29 us -> none  [the longest x1 3.99 us: body(): lstrip = lax.ppermute(edge_r, 'col', col_down)]
    ppermute x1, waiting for transfers between devices: 5.43 us -> 0.31 us  [body(): upr = lax.ppermute(fbot, 'row', row_down)]
    all_to_all x1, blocking collectives: 14.4 us -> 18.7 us  [body(): every = lax.all_to_all(mine, ('row', 'col'), 0, 0, tiled=True)]
    ppermute x2 -> x0, waiting for transfers between devices: 3.53 us -> none  [the longest x1 3.53 us: body(): rstrip = lax.ppermute(edge_l, 'col', col_up)]
    ppermute x1, waiting for transfers between devices: 2.12 us -> 4.4 us  [body(): dnr = lax.ppermute(ftop, 'row', row_up)]
    all_to_all x1, blocking collectives: 13.6 us -> 15.4 us  [body(): y = lax.all_to_all(y, 'col', 0, 0, tiled=True)]
  transfers between devices with their start and end apart: 11 -> 9, of which waited for: 8 -> 6; matrix products, arithmetic and copies ran while one was open for 4% -> 5% of each run, Pallas kernels for 7% -> 12%
where the time goes in v4:
time: 158 us; the launch traced here: 157 us
  Pallas kernels  51.9 us (33%)
  starting transfers between devices  39.9 us (25%)
  blocking collectives  34.1 us (22%)
  waiting for transfers between devices  19 us (12%)
  other arithmetic  5.76 us (4%)
  local copies, waits for them, and re-layouts  5.43 us (3%)
    all_to_all x1, blocking collectives, body(): every = lax.all_to_all(mine, ('row', 'col'), 0, 0, tiled=True)  18.7 us
    all_to_all x1, starting transfers between devices, body(): z = lax.all_to_all(z, 'row', 0, 0, tiled=True)  16.6 us
    all_to_all x1, blocking collectives, body(): y = lax.all_to_all(y, 'col', 0, 0, tiled=True)  15.4 us
    pallas_call x1, Pallas kernels, final(): pl.pallas_call(final_kernel, grid=(scans,), in_specs=[pl.BlockSpec(z.shap...  13.7 us
    ppermute x1, waiting for transfers between devices, body(): up = lax.ppermute(bot, 'row', row_down)  9.09 us
    pallas_call x1, Pallas kernels, across(): pl.pallas_call(across_kernel, in_specs=[vmem, pl.BlockSpec(memory_space=p...  8.11 us
    pallas_call x1, Pallas kernels, resample(): pl.pallas_call(resample_kernel, in_specs=[smem, smem, vmem, vmem, vmem] +...  7.73 us
    pallas_call x1, Pallas kernels, own_rows(): pl.pallas_call(own_rows_kernel, in_specs=[smem] + [anywhere] * 3, out_spe...  5.89 us
  transfers between devices with their start and end apart: 9, of which 6 were waited for; matrix products, arithmetic and copies ran while one was open for 5% of the time, Pallas kernels for 12%

profile of v4, /device:TPU:1, one launch (start us, length us, event | category | flops | bytes accessed | tf_op | source)
XLA Modules:
  0.0 157.3 jit_solution(6501047658783907504)
XLA Ops:
  0.7 4.4 %pack.1 = (f32[4,8,136,128]{3,2,1,0:T(8,128)}, f32[4,8,136,128]{3,2,1,0:T(8,128)}) custom-call(f32[4,256,1024]{2,1,0:T(8,128)} %after.3), custom_call_target="tpu_custom_call" | custom-call | tf_op jit(solution)/shard_map/pack/pallas_call | solution.py:49
  5.1 4.5 %collective-permute-start = (f32[4,8,136,128]{3,2,1,0:T(8,128)}, f32[4,8,136,128]{3,2,1,0:T(8,128)S(1)}, u32[]{:S(2)}, u32[]{:S(2)}) collective-permute-start(f32[4,8,136,128]{3,2,1,0:T(8,128)} %get-tuple-element.30), channel_id=1, source_target_pairs={{0,8},{8,16},{16,24},{24,32},{32,40},{40,48},{48,56},{56,64},{64,7... | collective-permute-start | bytes 6684680 | tf_op jit(solution)/shard_map/ppermute | solution.py:761
  9.6 1.9 %collective-permute-start.1 = (f32[4,8,136,128]{3,2,1,0:T(8,128)}, f32[4,8,136,128]{3,2,1,0:T(8,128)}, u32[]{:S(2)}, u32[]{:S(2)}) collective-permute-start(f32[4,8,136,128]{3,2,1,0:T(8,128)} %get-tuple-element.31), channel_id=1, source_target_pairs={{8,0},{16,8},{24,16},{32,24},{40,32},{48,40},{56,48},{64,56},{72,6... | collective-permute-start | bytes 6684680 | tf_op jit(solution)/shard_map/ppermute | solution.py:762
  11.9 0.6 and_convert_fusion.mc_ref
  12.6 0.1 min.30
  12.8 0.1 add.2905
  12.9 0.1 eq.202
  13.1 0.1 min.33
  13.4 0.7 select_add_fusion.2
  14.1 0.2 pad_bitcast_fusion.3
  14.3 0.3 exponential_reduce_fusion.1
  14.5 0.6 exponential_reduce_fusion
  15.2 0.8 divide_select_fusion.1.hr_ref
  16.0 0.9 divide_select_fusion.hc_ref
  17.0 1.0 fusion.9.uc_ref
  17.9 0.7 broadcast_in_dim.579.wt_ref
  18.6 0.1 broadcast_in_dim.612.mr_ref
  18.7 0.1 broadcast_in_dim.611.invr_ref
  18.8 0.2 broadcast_in_dim.605.invc_ref
  19.0 1.3 collective-permute-start.3
  20.3 4.2 %collective-permute-start.2 = (s32[2,4]{1,0:T(2,128)S(1)}, s32[2,4]{1,0:T(2,128)S(1)}, u32[]{:S(2)}, u32[]{:S(2)}) collective-permute-start(s32[2,4]{1,0:T(2,128)S(1)} %pad_add_fusion.mine_ref), channel_id=1, source_target_pairs={{0,1},{1,2},{2,3},{3,4},{4,5},{5,6},{6,7},{8,9},{9,10},{10,11},{11... | collective-permute-start | bytes 104 | tf_op jit(solution)/shard_map/ppermute | solution.py:789
  24.5 0.7 collective-permute-done.2.prev_ref
  25.2 9.1 %collective-permute-done.up = f32[4,8,136,128]{3,2,1,0:T(8,128)S(1)} collective-permute-done((f32[4,8,136,128]{3,2,1,0:T(8,128)}, f32[4,8,136,128]{3,2,1,0:T(8,128)S(1)}, u32[]{:S(2)}, u32[]{:S(2)}) %collective-permute-start) | collective-permute-done | bytes 2228256 | tf_op jit(solution)/shard_map/ppermute | solution.py:761
  34.3 4.4 %collective-permute-done.1.dn = f32[4,8,136,128]{3,2,1,0:T(8,128)} collective-permute-done((f32[4,8,136,128]{3,2,1,0:T(8,128)}, f32[4,8,136,128]{3,2,1,0:T(8,128)}, u32[]{:S(2)}, u32[]{:S(2)}) %collective-permute-start.1) | collective-permute-done | bytes 2228256 | tf_op jit(solution)/shard_map/ppermute | solution.py:762
  38.7 4.0 %edge_rows.1 = (f32[4,2,136,128]{3,2,1,0:T(8,128)}, f32[4,2,136,128]{3,2,1,0:T(8,128)}) custom-call(s32[2,4]{1,0:T(2,128)S(1)} %collective-permute-done.2.prev_ref, s32[2,4]{1,0:T(2,128)S(1)} %collective-permute-done.3.next_ref, f32[4,256,1024]{2,1,0:T(8,128)S(1)} %copy-done, f32[4,8,136,128]{3,2,1,0:T(8,128)S(1)} %collective-permute-done.up, ...), custom_call_target="tpu_custom_call" | custom-call | tf_op jit(solution)/shard_map/edge_rows/pallas_call | solution.py:173
  42.6 4.7 %collective-permute-start.4 = (f32[4,2,136,128]{3,2,1,0:T(8,128)}, f32[4,2,136,128]{3,2,1,0:T(8,128)}, u32[]{:S(2)}, u32[]{:S(2)}) collective-permute-start(f32[4,2,136,128]{3,2,1,0:T(8,128)} %get-tuple-element.32), channel_id=1, source_target_pairs={{0,1},{1,2},{2,3},{3,4},{4,5},{5,6},{6,7},{8,9},{9,10},{10,11},{11... | collective-permute-start | bytes 1671176 | tf_op jit(solution)/shard_map/ppermute | solution.py:792
  47.3 1.3 collective-permute-start.5
  48.6 5.2 %flip.1.beforet = f32[4,2,1024,128]{3,2,1,0:T(8,128)} custom-call(f32[4,256,1024]{2,1,0:T(8,128)} %x_ref.2), custom_call_target="tpu_custom_call" | custom-call | flops 1048576 | bytes 8388608 | tf_op jit(solution)/shard_map/flip/pallas_call | solution.py:74
  53.8 2.2 %copy-done.1 = f32[4,256,1024]{2,1,0:T(8,128)S(1)} copy-done((f32[4,256,1024]{2,1,0:T(8,128)S(1)}, f32[4,256,1024]{2,1,0:T(8,128)}, u32[]{:S(2)}) %copy-start.1) | copy-done | bytes 4194328
  56.0 0.7 copy-done.8
  56.7 5.9 %own_rows.1.own = f32[4,2,1024,128]{3,2,1,0:T(8,128)S(1)} custom-call(s32[2,4]{1,0:T(2,128)S(1)} %copy-done.8, f32[4,256,1024]{2,1,0:T(8,128)S(1)} %copy-done.1, f32[4,8,136,128]{3,2,1,0:T(8,128)S(1)} %collective-permute-done.up, f32[4,8,136,128]{3,2,1,0:T(8,128)} %collective-permute-done.1.dn), custom_call_target="tpu_custom_call" | custom-call | flops 8388608 | bytes 16777216 | tf_op jit(solution)/shard_map/own_rows/pallas_call | solution.py:229
  62.6 0.1 collective-permute-done.4.lcols
  62.7 7.7 %resample.1 = (f32[4,2,1024,128]{3,2,1,0:T(8,128)}, f32[8,136,128]{2,1,0:T(8,128)S(1)}) custom-call(s32[2,4]{1,0:T(2,128)S(1)} %bitcast.15, s32[2,4]{1,0:T(2,128)S(1)} %bitcast.16, f32[64,128]{1,0:T(8,128)S(1)} %copy-done.5, f32[4,256,128]{2,1,0:T(8,128)S(1)} %pad_maximum_fusion.rm_ref, f32[576,80]{1,0:T(8,128)S(1)} %copy-done.4, ...), custom_call_target="tpu_custom_call" | custom-call | tf_op jit(solution)/shard_map/resample/pallas_call | solution.py:359
  70.5 15.4 %all_to_all.15.y_ref.y = f32[8,136,128]{2,1,0:T(8,128)} all-to-all(f32[8,136,128]{2,1,0:T(8,128)S(1)} %get-tuple-element.35), channel_id=1, replica_groups=mesh['row'=16,'col'=8] {'col'}, dimensions={0} | all-to-all | bytes 1114112 | tf_op jit(solution)/shard_map/all_to_all | solution.py:797
  85.9 2.9 %long_rows.1 = f32[16,4,24,128]{3,2,1,0:T(8,128)} custom-call(f32[8,136,128]{2,1,0:T(8,128)} %all_to_all.15.y_ref.y, f32[384,24]{1,0:T(8,128)} %divide_select_fusion.1.hr_ref), custom_call_target="tpu_custom_call" | custom-call | tf_op jit(solution)/shard_map/long_rows/pallas_call | solution.py:399
  88.8 16.6 %all-to-all-start.1 = ((f32[16,4,24,128]{3,2,1,0:T(8,128)}), f32[16,4,24,128]{3,2,1,0:T(8,128)S(1)}, u32[]{:S(2)}, u32[]{:S(2)}) async-start(f32[16,4,24,128]{3,2,1,0:T(8,128)} %long_rows.1), calls=%async_computation.1 | async-start | bytes 1572864 | tf_op jit(solution)/shard_map/all_to_all | solution.py:802
  105.4 8.1 %across.1 = (f32[4,10,256,128]{3,2,1,0:T(8,128)}, f32[4,10,8,128]{3,2,1,0:T(8,128)S(1)}, f32[4,10,8,128]{3,2,1,0:T(8,128)S(1)}) custom-call(f32[1040,128]{1,0:T(8,128)S(1)} %broadcast_in_dim.605.invc_ref, f32[4,2,1024,128]{3,2,1,0:T(8,128)} %get-tuple-element.42.diff, f32[8,136,128]{2,1,0:T(8,128)S(1)} %copy-done.2), custom_call_target="tpu_custom_call" | custom-call | flops 20971520 | bytes 8388608 | tf_op jit(solution)/shard_map/across/pallas_call | solution.py:494
  113.5 3.5 %collective-permute-start.6 = (f32[4,10,8,128]{3,2,1,0:T(8,128)S(1)}, f32[4,10,8,128]{3,2,1,0:T(8,128)S(1)}, u32[]{:S(2)}, u32[]{:S(2)}) collective-permute-start(f32[4,10,8,128]{3,2,1,0:T(8,128)S(1)} %get-tuple-element.44), channel_id=1, source_target_pairs={{0,8},{8,16},{16,24},{24,32},{32,40},{40,48},{48,56},{56,64},{64,7... | collective-permute-start | bytes 491528 | tf_op jit(solution)/shard_map/ppermute | solution.py:800
  117.1 1.9 %collective-permute-start.7 = (f32[4,10,8,128]{3,2,1,0:T(8,128)S(1)}, f32[4,10,8,128]{3,2,1,0:T(8,128)S(1)}, u32[]{:S(2)}, u32[]{:S(2)}) collective-permute-start(f32[4,10,8,128]{3,2,1,0:T(8,128)S(1)} %get-tuple-element.45), channel_id=1, source_target_pairs={{8,0},{16,8},{24,16},{32,24},{40,32},{48,40},{56,48},{64,56},{72,6... | collective-permute-start | bytes 491528 | tf_op jit(solution)/shard_map/ppermute | solution.py:801
  119.0 0.3 collective-permute-done.6.upr
  119.3 4.4 %collective-permute-done.7.dnr = f32[4,10,8,128]{3,2,1,0:T(8,128)S(1)} collective-permute-done((f32[4,10,8,128]{3,2,1,0:T(8,128)S(1)}, f32[4,10,8,128]{3,2,1,0:T(8,128)S(1)}, u32[]{:S(2)}, u32[]{:S(2)}) %collective-permute-start.7) | collective-permute-done | bytes 163872 | tf_op jit(solution)/shard_map/ppermute | solution.py:801
  123.7 13.7 %final.1 = (f32[4,256,1024]{2,1,0:T(8,128)}, f32[4,256,1024]{2,1,0:T(8,128)}, f32[4,2,128]{2,1,0:T(2,128)S(1)}) custom-call(f32[16,4,24,128]{3,2,1,0:T(8,128)S(1)} %all-to-all-done.1.z_ref, bf16[128,1280]{1,0:T(8,128)(2,1)S(1)} %copy-done.3, f32[272,128]{1,0:T(8,128)S(1)} %broadcast_in_dim.611.invr_ref, f32[1,1024]{1,0:T(1,128)S(1)} %copy-done.6, ...), custom_call_target="tpu_custom_call" | custom-call | tf_op jit(solution)/shard_map/final/pallas_call | solution.py:643
  137.4 0.1 reduce_sum.38
  137.5 0.1 copy.14
  137.6 0.1 broadcast_in_dim.613
  137.7 18.7 %all_to_all.16 = f32[128,1,8]{2,1,0:T(1,128)S(1)} all-to-all(f32[128,1,8]{2,1,0:T(1,128)S(1)} %broadcast_in_dim.614), channel_id=1, replica_groups=mesh['row'=16,'col'=8] {'row','col'}, dimensions={0} | all-to-all | bytes 8192 | tf_op jit(solution)/shard_map/all_to_all | solution.py:807
  156.4 0.2 reduce_sum.39
  156.6 0.7 sqrt.7
  (68 shorter events, 0.8 us)
Async XLA Ops:
  0.6 11.9 %copy-start.14 = (s32[8]{0:T(128)S(1)}, s32[8]{0:T(128)}, u32[]{:S(2)}) copy-start(s32[8]{0:T(128)} %constant.477.clone) | copy-start | bytes 100
  0.6 12.2 %copy-start.13 = (s32[8]{0:T(128)S(1)}, s32[8]{0:T(128)}, u32[]{:S(2)}) copy-start(s32[8]{0:T(128)} %constant.478.clone) | copy-start | bytes 100
  0.7 12.5 %copy-start.11 = (s32[2,4,1,1]{1,3,2,0:T(1,128)S(1)}, s32[2,4,1,1]{1,3,2,0:T(1,128)}, u32[]{:S(2)}) copy-start(s32[2,4,1,1]{1,3,2,0:T(1,128)} %param.9) | copy-start | bytes 100
  0.7 12.5 %copy-start.9 = (s32[2,4,1,1]{1,3,2,0:T(1,128)S(1)}, s32[2,4,1,1]{1,3,2,0:T(1,128)}, u32[]{:S(2)}) copy-start(s32[2,4,1,1]{1,3,2,0:T(1,128)} %param.8) | copy-start | bytes 100
  5.1 29.2 %collective-permute-start = (f32[4,8,136,128]{3,2,1,0:T(8,128)}, f32[4,8,136,128]{3,2,1,0:T(8,128)S(1)}, u32[]{:S(2)}, u32[]{:S(2)}) collective-permute-start(f32[4,8,136,128]{3,2,1,0:T(8,128)} %get-tuple-element.30), channel_id=1, source_target_pairs={{0,8},{8,16},{16,24},{24,32},{32,40},{40,48},{48,56},{56,64},{64,7... | collective-permute-start | bytes 6684680 | tf_op jit(solution)/shard_map/ppermute | solution.py:761
  9.6 29.1 %collective-permute-start.1 = (f32[4,8,136,128]{3,2,1,0:T(8,128)}, f32[4,8,136,128]{3,2,1,0:T(8,128)}, u32[]{:S(2)}, u32[]{:S(2)}) collective-permute-start(f32[4,8,136,128]{3,2,1,0:T(8,128)} %get-tuple-element.31), channel_id=1, source_target_pairs={{8,0},{16,8},{24,16},{32,24},{40,32},{48,40},{56,48},{64,56},{72,6... | collective-permute-start | bytes 6684680 | tf_op jit(solution)/shard_map/ppermute | solution.py:762
  13.2 25.5 %copy-start = (f32[4,256,1024]{2,1,0:T(8,128)S(1)}, f32[4,256,1024]{2,1,0:T(8,128)}, u32[]{:S(2)}) copy-start(f32[4,256,1024]{2,1,0:T(8,128)} %after.3) | copy-start | bytes 12582916
  13.3 21.0 %copy-start.7 = (s32[2,4]{1,0:T(2,128)}, s32[2,4]{1,0:T(2,128)S(1)}, u32[]{:S(2)}) copy-start(s32[2,4]{1,0:T(2,128)S(1)} %pad_add_fusion.mine_ref) | copy-start | bytes 100
  19.0 5.5 %collective-permute-start.3 = (s32[2,4]{1,0:T(2,128)S(1)}, s32[2,4]{1,0:T(2,128)S(1)}, u32[]{:S(2)}, u32[]{:S(2)}) collective-permute-start(s32[2,4]{1,0:T(2,128)S(1)} %pad_add_fusion.mine_ref), channel_id=1, source_target_pairs={{1,0},{2,1},{3,2},{4,3},{5,4},{6,5},{7,6},{9,8},{10,9},{11,10},{12... | collective-permute-start | bytes 104 | tf_op jit(solution)/shard_map/ppermute | solution.py:790
  20.3 4.9 %collective-permute-start.2 = (s32[2,4]{1,0:T(2,128)S(1)}, s32[2,4]{1,0:T(2,128)S(1)}, u32[]{:S(2)}, u32[]{:S(2)}) collective-permute-start(s32[2,4]{1,0:T(2,128)S(1)} %pad_add_fusion.mine_ref), channel_id=1, source_target_pairs={{0,1},{1,2},{2,3},{3,4},{4,5},{5,6},{6,7},{8,9},{9,10},{10,11},{11... | collective-permute-start | bytes 104 | tf_op jit(solution)/shard_map/ppermute | solution.py:789
  42.6 20.1 %collective-permute-start.4 = (f32[4,2,136,128]{3,2,1,0:T(8,128)}, f32[4,2,136,128]{3,2,1,0:T(8,128)}, u32[]{:S(2)}, u32[]{:S(2)}) collective-permute-start(f32[4,2,136,128]{3,2,1,0:T(8,128)} %get-tuple-element.32), channel_id=1, source_target_pairs={{0,1},{1,2},{2,3},{3,4},{4,5},{5,6},{6,7},{8,9},{9,10},{10,11},{11... | collective-permute-start | bytes 1671176 | tf_op jit(solution)/shard_map/ppermute | solution.py:792
  47.3 15.4 %collective-permute-start.5 = (f32[4,2,136,128]{3,2,1,0:T(8,128)}, f32[4,2,136,128]{3,2,1,0:T(8,128)}, u32[]{:S(2)}, u32[]{:S(2)}) collective-permute-start(f32[4,2,136,128]{3,2,1,0:T(8,128)} %get-tuple-element.33), channel_id=1, source_target_pairs={{1,0},{2,1},{3,2},{4,3},{5,4},{6,5},{7,6},{9,8},{10,9},{11,10},{12... | collective-permute-start | bytes 1671176 | tf_op jit(solution)/shard_map/ppermute | solution.py:793
  53.8 2.2 %copy-start.1 = (f32[4,256,1024]{2,1,0:T(8,128)S(1)}, f32[4,256,1024]{2,1,0:T(8,128)}, u32[]{:S(2)}) copy-start(f32[4,256,1024]{2,1,0:T(8,128)} %after.3) | copy-start | bytes 12582916
  56.0 0.7 copy-start.8
  56.7 6.0 %copy-start.4 = (f32[576,80]{1,0:T(8,128)S(1)}, f32[576,80]{1,0:T(8,128)}, u32[]{:S(2)}) copy-start(f32[576,80]{1,0:T(8,128)} %divide_select_fusion.hc_ref) | copy-start | bytes 552964
  56.7 6.0 %copy-start.5 = (f32[64,128]{1,0:T(8,128)S(1)}, f32[64,128]{1,0:T(8,128)}, u32[]{:S(2)}) copy-start(f32[64,128]{1,0:T(8,128)} %broadcast_in_dim.579.wt_ref) | copy-start | bytes 98308
  56.7 6.0 %copy-start.10 = (s32[2,4,1,1]{1,3,2,0:T(1,128)S(1)}, s32[2,4,1,1]{1,3,2,0:T(1,128)}, u32[]{:S(2)}) copy-start(s32[2,4,1,1]{1,3,2,0:T(1,128)} %param.8) | copy-start | bytes 100
  56.7 6.0 %copy-start.12 = (s32[2,4,1,1]{1,3,2,0:T(1,128)S(1)}, s32[2,4,1,1]{1,3,2,0:T(1,128)}, u32[]{:S(2)}) copy-start(s32[2,4,1,1]{1,3,2,0:T(1,128)} %param.9) | copy-start | bytes 100
  85.9 19.5 %copy-start.2 = (f32[8,136,128]{2,1,0:T(8,128)S(1)}, f32[8,136,128]{2,1,0:T(8,128)}, u32[]{:S(2)}) copy-start(f32[8,136,128]{2,1,0:T(8,128)} %all_to_all.15.y_ref.y) | copy-start | bytes 1671172
  88.8 35.0 %all-to-all-start.1 = ((f32[16,4,24,128]{3,2,1,0:T(8,128)}), f32[16,4,24,128]{3,2,1,0:T(8,128)S(1)}, u32[]{:S(2)}, u32[]{:S(2)}) async-start(f32[16,4,24,128]{3,2,1,0:T(8,128)} %long_rows.1), calls=%async_computation.1 | async-start | bytes 1572864 | tf_op jit(solution)/shard_map/all_to_all | solution.py:802
  105.4 18.3 %copy-start.3 = (bf16[128,1280]{1,0:T(8,128)(2,1)S(1)}, bf16[128,1280]{1,0:T(8,128)(2,1)}, u32[]{:S(2)}) copy-start(bf16[128,1280]{1,0:T(8,128)(2,1)} %fusion.9.uc_ref) | copy-start | bytes 983044
  105.4 18.3 %copy-start.6 = (f32[1,1024]{1,0:T(1,128)S(1)}, f32[1,1024]{1,0:T(1,128)}, u32[]{:S(2)}) copy-start(f32[1,1024]{1,0:T(1,128)} %and_convert_fusion.mc_ref) | copy-start | bytes 12292
  113.5 5.8 %collective-permute-start.6 = (f32[4,10,8,128]{3,2,1,0:T(8,128)S(1)}, f32[4,10,8,128]{3,2,1,0:T(8,128)S(1)}, u32[]{:S(2)}, u32[]{:S(2)}) collective-permute-start(f32[4,10,8,128]{3,2,1,0:T(8,128)S(1)} %get-tuple-element.44), channel_id=1, source_target_pairs={{0,8},{8,16},{16,24},{24,32},{32,40},{40,48},{48,56},{56,64},{64,7... | collective-permute-start | bytes 491528 | tf_op jit(solution)/shard_map/ppermute | solution.py:800
  117.1 6.6 %collective-permute-start.7 = (f32[4,10,8,128]{3,2,1,0:T(8,128)S(1)}, f32[4,10,8,128]{3,2,1,0:T(8,128)S(1)}, u32[]{:S(2)}, u32[]{:S(2)}) collective-permute-start(f32[4,10,8,128]{3,2,1,0:T(8,128)S(1)} %get-tuple-element.45), channel_id=1, source_target_pairs={{8,0},{16,8},{24,16},{32,24},{40,32},{48,40},{56,48},{64,56},{72,6... | collective-permute-start | bytes 491528 | tf_op jit(solution)/shard_map/ppermute | solution.py:801

commit v5 on v4

--- a/solution.py
+++ b/solution.py
@@ -262,7 +262,8 @@
             (beforet.at[s], bef.at[s]),
         ]
 
-    start_copies(copies(0), sem.at[0])
+    for s in range(scans):
+        start_copies(copies(s), sem.at[s])
     part[...] = jnp.zeros_like(part)
     col = lax.axis_index("col")
     n_col = y_ref.shape[0]
@@ -274,10 +275,6 @@
 
     def one_scan(s, carry):
         wait_copies(copies(s), sem.at[s])
-
-        @pl.when(s + 1 < scans)
-        def _():
-            start_copies(copies(s + 1), sem.at[s + 1])
 
         ct = scalar_taps(fracs_ref[1, s])
         first = HALO + offs_ref[1, s] - 1
@@ -436,7 +433,8 @@
         for n, (a, b) in enumerate(copies(s)):
             pltpu.make_async_copy(a, b, sem.at[s, n]).start()
 
-    fetch(0)
+    for s in range(scans):
+        fetch(s)
     zero = jnp.zeros((LANES - EDGE, LANES), jnp.float32)
 
     def filtered(s, h, q, n):
@@ -450,10 +448,6 @@
     def one_scan(s, carry):
         for n, (a, b) in enumerate(copies(s)):
             pltpu.make_async_copy(a, b, sem.at[s, n]).wait()
-
-        @pl.when(s + 1 < scans)
-        def _():
-            fetch(s + 1)
 
         for h in range(halves):
             buf[s, h, 0 : PAD - EDGE, :] = zero[0:EDGE]
@@ -537,7 +531,9 @@
 
     @pl.when(s == 0)
     def _():
-        fetch(0)
+        for t in range(scans):
+            fetch(t)
+
 
         parts = []
         for t in range(scans):
@@ -559,10 +555,6 @@
 
     for n, (a, b) in enumerate(copies(s)):
         pltpu.make_async_copy(a, b, sem.at[s, n]).wait()
-
-    @pl.when(s + 1 < scans)
-    def _():
-        fetch(s + 1)
 
     for j in range(n_wide):
         acs[s, j, 0 : PAD - EDGE, :] = jnp.zeros((PAD - EDGE, LANES), jnp.float32)

time: 158 us -> 156 us (0.987)
  Pallas kernels: 51.9 us -> 50.2 us
where the time goes in v5:
time: 156 us
  Pallas kernels  50.2 us (32%)
  starting transfers between devices  40 us (26%)
  blocking collectives  34.1 us (22%)
  waiting for transfers between devices  19 us (12%)
  other arithmetic  5.76 us (4%)
  local copies, waits for them, and re-layouts  5.43 us (3%)
    all_to_all x1, blocking collectives, body(): every = lax.all_to_all(mine, ('row', 'col'), 0, 0, tiled=True)  18.7 us
    all_to_all x1, starting transfers between devices, body(): z = lax.all_to_all(z, 'row', 0, 0, tiled=True)  16.7 us
    all_to_all x1, blocking collectives, body(): y = lax.all_to_all(y, 'col', 0, 0, tiled=True)  15.4 us
    pallas_call x1, Pallas kernels, final(): pl.pallas_call(final_kernel, grid=(scans,), in_specs=[pl.BlockSpec(z.shap...  13.6 us
    ppermute x1, waiting for transfers between devices, body(): up = lax.ppermute(bot, 'row', row_down)  9.09 us
    pallas_call x1, Pallas kernels, across(): pl.pallas_call(across_kernel, in_specs=[vmem, pl.BlockSpec(memory_space=p...  7.67 us
    pallas_call x1, Pallas kernels, resample(): pl.pallas_call(resample_kernel, in_specs=[smem, smem, vmem, vmem, vmem] +...  6.56 us
    pallas_call x1, Pallas kernels, own_rows(): pl.pallas_call(own_rows_kernel, in_specs=[smem] + [anywhere] * 3, out_spe...  5.89 us
  transfers between devices with their start and end apart: 9, of which 6 were waited for; matrix products, arithmetic and copies ran while one was open for 5% of the time, Pallas kernels for 12%

profile of v5, /device:TPU:1, one launch (start us, length us, event | category | flops | bytes accessed | tf_op | source)
XLA Modules:
  0.0 155.7 jit_solution(17582859842349563451)
XLA Ops:
  0.7 4.4 %pack.1 = (f32[4,8,136,128]{3,2,1,0:T(8,128)}, f32[4,8,136,128]{3,2,1,0:T(8,128)}) custom-call(f32[4,256,1024]{2,1,0:T(8,128)} %after.3), custom_call_target="tpu_custom_call" | custom-call | tf_op jit(solution)/shard_map/pack/pallas_call | solution.py:49
  5.1 4.5 %collective-permute-start = (f32[4,8,136,128]{3,2,1,0:T(8,128)}, f32[4,8,136,128]{3,2,1,0:T(8,128)S(1)}, u32[]{:S(2)}, u32[]{:S(2)}) collective-permute-start(f32[4,8,136,128]{3,2,1,0:T(8,128)} %get-tuple-element.30), channel_id=1, source_target_pairs={{0,8},{8,16},{16,24},{24,32},{32,40},{40,48},{48,56},{56,64},{64,7... | collective-permute-start | bytes 6684680 | tf_op jit(solution)/shard_map/ppermute | solution.py:753
  9.6 1.9 %collective-permute-start.1 = (f32[4,8,136,128]{3,2,1,0:T(8,128)}, f32[4,8,136,128]{3,2,1,0:T(8,128)}, u32[]{:S(2)}, u32[]{:S(2)}) collective-permute-start(f32[4,8,136,128]{3,2,1,0:T(8,128)} %get-tuple-element.31), channel_id=1, source_target_pairs={{8,0},{16,8},{24,16},{32,24},{40,32},{48,40},{56,48},{64,56},{72,6... | collective-permute-start | bytes 6684680 | tf_op jit(solution)/shard_map/ppermute | solution.py:754
  11.9 0.6 and_convert_fusion.mc_ref
  12.6 0.1 min.30
  12.8 0.1 add.2905
  12.9 0.1 eq.202
  13.1 0.1 min.33
  13.4 0.7 select_add_fusion.2
  14.1 0.2 pad_bitcast_fusion.3
  14.3 0.3 exponential_reduce_fusion.1
  14.5 0.6 exponential_reduce_fusion
  15.2 0.8 divide_select_fusion.1.hr_ref
  16.0 0.9 divide_select_fusion.hc_ref
  17.0 1.0 fusion.9.uc_ref
  17.9 0.7 broadcast_in_dim.579.wt_ref
  18.6 0.1 broadcast_in_dim.612.mr_ref
  18.7 0.1 broadcast_in_dim.611.invr_ref
  18.8 0.2 broadcast_in_dim.605.invc_ref
  19.0 1.3 collective-permute-start.3
  20.3 4.2 %collective-permute-start.2 = (s32[2,4]{1,0:T(2,128)S(1)}, s32[2,4]{1,0:T(2,128)S(1)}, u32[]{:S(2)}, u32[]{:S(2)}) collective-permute-start(s32[2,4]{1,0:T(2,128)S(1)} %pad_add_fusion.mine_ref), channel_id=1, source_target_pairs={{0,1},{1,2},{2,3},{3,4},{4,5},{5,6},{6,7},{8,9},{9,10},{10,11},{11... | collective-permute-start | bytes 104 | tf_op jit(solution)/shard_map/ppermute | solution.py:781
  24.5 0.7 collective-permute-done.2.prev_ref
  25.2 9.1 %collective-permute-done.up = f32[4,8,136,128]{3,2,1,0:T(8,128)S(1)} collective-permute-done((f32[4,8,136,128]{3,2,1,0:T(8,128)}, f32[4,8,136,128]{3,2,1,0:T(8,128)S(1)}, u32[]{:S(2)}, u32[]{:S(2)}) %collective-permute-start) | collective-permute-done | bytes 2228256 | tf_op jit(solution)/shard_map/ppermute | solution.py:753
  34.3 4.4 %collective-permute-done.1.dn = f32[4,8,136,128]{3,2,1,0:T(8,128)} collective-permute-done((f32[4,8,136,128]{3,2,1,0:T(8,128)}, f32[4,8,136,128]{3,2,1,0:T(8,128)}, u32[]{:S(2)}, u32[]{:S(2)}) %collective-permute-start.1) | collective-permute-done | bytes 2228256 | tf_op jit(solution)/shard_map/ppermute | solution.py:754
  38.7 4.0 %edge_rows.1 = (f32[4,2,136,128]{3,2,1,0:T(8,128)}, f32[4,2,136,128]{3,2,1,0:T(8,128)}) custom-call(s32[2,4]{1,0:T(2,128)S(1)} %collective-permute-done.2.prev_ref, s32[2,4]{1,0:T(2,128)S(1)} %collective-permute-done.3.next_ref, f32[4,256,1024]{2,1,0:T(8,128)S(1)} %copy-done, f32[4,8,136,128]{3,2,1,0:T(8,128)S(1)} %collective-permute-done.up, ...), custom_call_target="tpu_custom_call" | custom-call | tf_op jit(solution)/shard_map/edge_rows/pallas_call | solution.py:173
  42.6 4.7 %collective-permute-start.4 = (f32[4,2,136,128]{3,2,1,0:T(8,128)}, f32[4,2,136,128]{3,2,1,0:T(8,128)}, u32[]{:S(2)}, u32[]{:S(2)}) collective-permute-start(f32[4,2,136,128]{3,2,1,0:T(8,128)} %get-tuple-element.32), channel_id=1, source_target_pairs={{0,1},{1,2},{2,3},{3,4},{4,5},{5,6},{6,7},{8,9},{9,10},{10,11},{11... | collective-permute-start | bytes 1671176 | tf_op jit(solution)/shard_map/ppermute | solution.py:784
  47.3 1.3 collective-permute-start.5
  48.6 5.2 %flip.1.beforet = f32[4,2,1024,128]{3,2,1,0:T(8,128)} custom-call(f32[4,256,1024]{2,1,0:T(8,128)} %x_ref.2), custom_call_target="tpu_custom_call" | custom-call | flops 1048576 | bytes 8388608 | tf_op jit(solution)/shard_map/flip/pallas_call | solution.py:74
  53.8 2.2 %copy-done.1 = f32[4,256,1024]{2,1,0:T(8,128)S(1)} copy-done((f32[4,256,1024]{2,1,0:T(8,128)S(1)}, f32[4,256,1024]{2,1,0:T(8,128)}, u32[]{:S(2)}) %copy-start.1) | copy-done | bytes 4194328
  56.0 0.7 copy-done.8
  56.7 5.9 %own_rows.1.own = f32[4,2,1024,128]{3,2,1,0:T(8,128)S(1)} custom-call(s32[2,4]{1,0:T(2,128)S(1)} %copy-done.8, f32[4,256,1024]{2,1,0:T(8,128)S(1)} %copy-done.1, f32[4,8,136,128]{3,2,1,0:T(8,128)S(1)} %collective-permute-done.up, f32[4,8,136,128]{3,2,1,0:T(8,128)} %collective-permute-done.1.dn), custom_call_target="tpu_custom_call" | custom-call | flops 8388608 | bytes 16777216 | tf_op jit(solution)/shard_map/own_rows/pallas_call | solution.py:229
  62.6 0.1 collective-permute-done.4.lcols
  62.7 6.6 %resample.1 = (f32[4,2,1024,128]{3,2,1,0:T(8,128)}, f32[8,136,128]{2,1,0:T(8,128)S(1)}) custom-call(s32[2,4]{1,0:T(2,128)S(1)} %bitcast.15, s32[2,4]{1,0:T(2,128)S(1)} %bitcast.16, f32[64,128]{1,0:T(8,128)S(1)} %copy-done.5, f32[4,256,128]{2,1,0:T(8,128)S(1)} %pad_maximum_fusion.rm_ref, f32[576,80]{1,0:T(8,128)S(1)} %copy-done.4, ...), custom_call_target="tpu_custom_call" | custom-call | tf_op jit(solution)/shard_map/resample/pallas_call | solution.py:356
  69.3 15.4 %all_to_all.15.y_ref.y = f32[8,136,128]{2,1,0:T(8,128)} all-to-all(f32[8,136,128]{2,1,0:T(8,128)S(1)} %get-tuple-element.35), channel_id=1, replica_groups=mesh['row'=16,'col'=8] {'col'}, dimensions={0} | all-to-all | bytes 1114112 | tf_op jit(solution)/shard_map/all_to_all | solution.py:789
  84.7 2.9 %long_rows.1 = f32[16,4,24,128]{3,2,1,0:T(8,128)} custom-call(f32[8,136,128]{2,1,0:T(8,128)} %all_to_all.15.y_ref.y, f32[384,24]{1,0:T(8,128)} %divide_select_fusion.1.hr_ref), custom_call_target="tpu_custom_call" | custom-call | tf_op jit(solution)/shard_map/long_rows/pallas_call | solution.py:396
  87.6 16.7 %all-to-all-start.1 = ((f32[16,4,24,128]{3,2,1,0:T(8,128)}), f32[16,4,24,128]{3,2,1,0:T(8,128)S(1)}, u32[]{:S(2)}, u32[]{:S(2)}) async-start(f32[16,4,24,128]{3,2,1,0:T(8,128)} %long_rows.1), calls=%async_computation.1 | async-start | bytes 1572864 | tf_op jit(solution)/shard_map/all_to_all | solution.py:794
  104.3 7.7 %across.1 = (f32[4,10,256,128]{3,2,1,0:T(8,128)}, f32[4,10,8,128]{3,2,1,0:T(8,128)S(1)}, f32[4,10,8,128]{3,2,1,0:T(8,128)S(1)}) custom-call(f32[1040,128]{1,0:T(8,128)S(1)} %broadcast_in_dim.605.invc_ref, f32[4,2,1024,128]{3,2,1,0:T(8,128)} %get-tuple-element.42.diff, f32[8,136,128]{2,1,0:T(8,128)S(1)} %copy-done.2), custom_call_target="tpu_custom_call" | custom-call | flops 20971520 | bytes 8388608 | tf_op jit(solution)/shard_map/across/pallas_call | solution.py:488
  112.0 3.5 %collective-permute-start.6 = (f32[4,10,8,128]{3,2,1,0:T(8,128)S(1)}, f32[4,10,8,128]{3,2,1,0:T(8,128)S(1)}, u32[]{:S(2)}, u32[]{:S(2)}) collective-permute-start(f32[4,10,8,128]{3,2,1,0:T(8,128)S(1)} %get-tuple-element.44), channel_id=1, source_target_pairs={{0,8},{8,16},{16,24},{24,32},{32,40},{40,48},{48,56},{56,64},{64,7... | collective-permute-start | bytes 491528 | tf_op jit(solution)/shard_map/ppermute | solution.py:792
  115.6 1.9 %collective-permute-start.7 = (f32[4,10,8,128]{3,2,1,0:T(8,128)S(1)}, f32[4,10,8,128]{3,2,1,0:T(8,128)S(1)}, u32[]{:S(2)}, u32[]{:S(2)}) collective-permute-start(f32[4,10,8,128]{3,2,1,0:T(8,128)S(1)} %get-tuple-element.45), channel_id=1, source_target_pairs={{8,0},{16,8},{24,16},{32,24},{40,32},{48,40},{56,48},{64,56},{72,6... | collective-permute-start | bytes 491528 | tf_op jit(solution)/shard_map/ppermute | solution.py:793
  117.5 0.3 collective-permute-done.6.upr
  117.8 4.4 %collective-permute-done.7.dnr = f32[4,10,8,128]{3,2,1,0:T(8,128)S(1)} collective-permute-done((f32[4,10,8,128]{3,2,1,0:T(8,128)S(1)}, f32[4,10,8,128]{3,2,1,0:T(8,128)S(1)}, u32[]{:S(2)}, u32[]{:S(2)}) %collective-permute-start.7) | collective-permute-done | bytes 163872 | tf_op jit(solution)/shard_map/ppermute | solution.py:793
  122.2 13.6 %final.1 = (f32[4,256,1024]{2,1,0:T(8,128)}, f32[4,256,1024]{2,1,0:T(8,128)}, f32[4,2,128]{2,1,0:T(2,128)S(1)}) custom-call(f32[16,4,24,128]{3,2,1,0:T(8,128)S(1)} %all-to-all-done.1.z_ref, bf16[128,1280]{1,0:T(8,128)(2,1)S(1)} %copy-done.3, f32[272,128]{1,0:T(8,128)S(1)} %broadcast_in_dim.611.invr_ref, f32[1,1024]{1,0:T(1,128)S(1)} %copy-done.6, ...), custom_call_target="tpu_custom_call" | custom-call | tf_op jit(solution)/shard_map/final/pallas_call | solution.py:635
  135.8 0.1 reduce_sum.38
  135.9 0.1 copy.14
  136.0 0.1 broadcast_in_dim.613
  136.1 18.7 %all_to_all.16 = f32[128,1,8]{2,1,0:T(1,128)S(1)} all-to-all(f32[128,1,8]{2,1,0:T(1,128)S(1)} %broadcast_in_dim.614), channel_id=1, replica_groups=mesh['row'=16,'col'=8] {'row','col'}, dimensions={0} | all-to-all | bytes 8192 | tf_op jit(solution)/shard_map/all_to_all | solution.py:799
  154.9 0.2 reduce_sum.39
  155.0 0.7 sqrt.7
  (68 shorter events, 0.8 us)
Async XLA Ops:
  0.6 11.9 %copy-start.14 = (s32[8]{0:T(128)S(1)}, s32[8]{0:T(128)}, u32[]{:S(2)}) copy-start(s32[8]{0:T(128)} %constant.477.clone) | copy-start | bytes 100
  0.6 12.2 %copy-start.13 = (s32[8]{0:T(128)S(1)}, s32[8]{0:T(128)}, u32[]{:S(2)}) copy-start(s32[8]{0:T(128)} %constant.478.clone) | copy-start | bytes 100
  0.7 12.5 %copy-start.11 = (s32[2,4,1,1]{1,3,2,0:T(1,128)S(1)}, s32[2,4,1,1]{1,3,2,0:T(1,128)}, u32[]{:S(2)}) copy-start(s32[2,4,1,1]{1,3,2,0:T(1,128)} %param.9) | copy-start | bytes 100
  0.7 12.5 %copy-start.9 = (s32[2,4,1,1]{1,3,2,0:T(1,128)S(1)}, s32[2,4,1,1]{1,3,2,0:T(1,128)}, u32[]{:S(2)}) copy-start(s32[2,4,1,1]{1,3,2,0:T(1,128)} %param.8) | copy-start | bytes 100
  5.1 29.2 %collective-permute-start = (f32[4,8,136,128]{3,2,1,0:T(8,128)}, f32[4,8,136,128]{3,2,1,0:T(8,128)S(1)}, u32[]{:S(2)}, u32[]{:S(2)}) collective-permute-start(f32[4,8,136,128]{3,2,1,0:T(8,128)} %get-tuple-element.30), channel_id=1, source_target_pairs={{0,8},{8,16},{16,24},{24,32},{32,40},{40,48},{48,56},{56,64},{64,7... | collective-permute-start | bytes 6684680 | tf_op jit(solution)/shard_map/ppermute | solution.py:753
  9.6 29.1 %collective-permute-start.1 = (f32[4,8,136,128]{3,2,1,0:T(8,128)}, f32[4,8,136,128]{3,2,1,0:T(8,128)}, u32[]{:S(2)}, u32[]{:S(2)}) collective-permute-start(f32[4,8,136,128]{3,2,1,0:T(8,128)} %get-tuple-element.31), channel_id=1, source_target_pairs={{8,0},{16,8},{24,16},{32,24},{40,32},{48,40},{56,48},{64,56},{72,6... | collective-permute-start | bytes 6684680 | tf_op jit(solution)/shard_map/ppermute | solution.py:754
  13.2 25.5 %copy-start = (f32[4,256,1024]{2,1,0:T(8,128)S(1)}, f32[4,256,1024]{2,1,0:T(8,128)}, u32[]{:S(2)}) copy-start(f32[4,256,1024]{2,1,0:T(8,128)} %after.3) | copy-start | bytes 12582916
  13.3 21.0 %copy-start.7 = (s32[2,4]{1,0:T(2,128)}, s32[2,4]{1,0:T(2,128)S(1)}, u32[]{:S(2)}) copy-start(s32[2,4]{1,0:T(2,128)S(1)} %pad_add_fusion.mine_ref) | copy-start | bytes 100
  19.0 5.5 %collective-permute-start.3 = (s32[2,4]{1,0:T(2,128)S(1)}, s32[2,4]{1,0:T(2,128)S(1)}, u32[]{:S(2)}, u32[]{:S(2)}) collective-permute-start(s32[2,4]{1,0:T(2,128)S(1)} %pad_add_fusion.mine_ref), channel_id=1, source_target_pairs={{1,0},{2,1},{3,2},{4,3},{5,4},{6,5},{7,6},{9,8},{10,9},{11,10},{12... | collective-permute-start | bytes 104 | tf_op jit(solution)/shard_map/ppermute | solution.py:782
  20.3 4.9 %collective-permute-start.2 = (s32[2,4]{1,0:T(2,128)S(1)}, s32[2,4]{1,0:T(2,128)S(1)}, u32[]{:S(2)}, u32[]{:S(2)}) collective-permute-start(s32[2,4]{1,0:T(2,128)S(1)} %pad_add_fusion.mine_ref), channel_id=1, source_target_pairs={{0,1},{1,2},{2,3},{3,4},{4,5},{5,6},{6,7},{8,9},{9,10},{10,11},{11... | collective-permute-start | bytes 104 | tf_op jit(solution)/shard_map/ppermute | solution.py:781
  42.6 20.1 %collective-permute-start.4 = (f32[4,2,136,128]{3,2,1,0:T(8,128)}, f32[4,2,136,128]{3,2,1,0:T(8,128)}, u32[]{:S(2)}, u32[]{:S(2)}) collective-permute-start(f32[4,2,136,128]{3,2,1,0:T(8,128)} %get-tuple-element.32), channel_id=1, source_target_pairs={{0,1},{1,2},{2,3},{3,4},{4,5},{5,6},{6,7},{8,9},{9,10},{10,11},{11... | collective-permute-start | bytes 1671176 | tf_op jit(solution)/shard_map/ppermute | solution.py:784
  47.3 15.4 %collective-permute-start.5 = (f32[4,2,136,128]{3,2,1,0:T(8,128)}, f32[4,2,136,128]{3,2,1,0:T(8,128)}, u32[]{:S(2)}, u32[]{:S(2)}) collective-permute-start(f32[4,2,136,128]{3,2,1,0:T(8,128)} %get-tuple-element.33), channel_id=1, source_target_pairs={{1,0},{2,1},{3,2},{4,3},{5,4},{6,5},{7,6},{9,8},{10,9},{11,10},{12... | collective-permute-start | bytes 1671176 | tf_op jit(solution)/shard_map/ppermute | solution.py:785
  53.8 2.2 %copy-start.1 = (f32[4,256,1024]{2,1,0:T(8,128)S(1)}, f32[4,256,1024]{2,1,0:T(8,128)}, u32[]{:S(2)}) copy-start(f32[4,256,1024]{2,1,0:T(8,128)} %after.3) | copy-start | bytes 12582916
  56.0 0.7 copy-start.8
  56.7 6.0 %copy-start.4 = (f32[576,80]{1,0:T(8,128)S(1)}, f32[576,80]{1,0:T(8,128)}, u32[]{:S(2)}) copy-start(f32[576,80]{1,0:T(8,128)} %divide_select_fusion.hc_ref) | copy-start | bytes 552964
  56.7 6.0 %copy-start.5 = (f32[64,128]{1,0:T(8,128)S(1)}, f32[64,128]{1,0:T(8,128)}, u32[]{:S(2)}) copy-start(f32[64,128]{1,0:T(8,128)} %broadcast_in_dim.579.wt_ref) | copy-start | bytes 98308
  56.7 6.0 %copy-start.10 = (s32[2,4,1,1]{1,3,2,0:T(1,128)S(1)}, s32[2,4,1,1]{1,3,2,0:T(1,128)}, u32[]{:S(2)}) copy-start(s32[2,4,1,1]{1,3,2,0:T(1,128)} %param.8) | copy-start | bytes 100
  56.7 6.0 %copy-start.12 = (s32[2,4,1,1]{1,3,2,0:T(1,128)S(1)}, s32[2,4,1,1]{1,3,2,0:T(1,128)}, u32[]{:S(2)}) copy-start(s32[2,4,1,1]{1,3,2,0:T(1,128)} %param.9) | copy-start | bytes 100
  84.7 19.6 %copy-start.2 = (f32[8,136,128]{2,1,0:T(8,128)S(1)}, f32[8,136,128]{2,1,0:T(8,128)}, u32[]{:S(2)}) copy-start(f32[8,136,128]{2,1,0:T(8,128)} %all_to_all.15.y_ref.y) | copy-start | bytes 1671172
  87.6 34.6 %all-to-all-start.1 = ((f32[16,4,24,128]{3,2,1,0:T(8,128)}), f32[16,4,24,128]{3,2,1,0:T(8,128)S(1)}, u32[]{:S(2)}, u32[]{:S(2)}) async-start(f32[16,4,24,128]{3,2,1,0:T(8,128)} %long_rows.1), calls=%async_computation.1 | async-start | bytes 1572864 | tf_op jit(solution)/shard_map/all_to_all | solution.py:794
  104.3 17.9 %copy-start.3 = (bf16[128,1280]{1,0:T(8,128)(2,1)S(1)}, bf16[128,1280]{1,0:T(8,128)(2,1)}, u32[]{:S(2)}) copy-start(bf16[128,1280]{1,0:T(8,128)(2,1)} %fusion.9.uc_ref) | copy-start | bytes 983044
  104.3 17.9 %copy-start.6 = (f32[1,1024]{1,0:T(1,128)S(1)}, f32[1,1024]{1,0:T(1,128)}, u32[]{:S(2)}) copy-start(f32[1,1024]{1,0:T(1,128)} %and_convert_fusion.mc_ref) | copy-start | bytes 12292
  112.0 5.8 %collective-permute-start.6 = (f32[4,10,8,128]{3,2,1,0:T(8,128)S(1)}, f32[4,10,8,128]{3,2,1,0:T(8,128)S(1)}, u32[]{:S(2)}, u32[]{:S(2)}) collective-permute-start(f32[4,10,8,128]{3,2,1,0:T(8,128)S(1)} %get-tuple-element.44), channel_id=1, source_target_pairs={{0,8},{8,16},{16,24},{24,32},{32,40},{40,48},{48,56},{56,64},{64,7... | collective-permute-start | bytes 491528 | tf_op jit(solution)/shard_map/ppermute | solution.py:792
  115.6 6.6 %collective-permute-start.7 = (f32[4,10,8,128]{3,2,1,0:T(8,128)S(1)}, f32[4,10,8,128]{3,2,1,0:T(8,128)S(1)}, u32[]{:S(2)}, u32[]{:S(2)}) collective-permute-start(f32[4,10,8,128]{3,2,1,0:T(8,128)S(1)} %get-tuple-element.45), channel_id=1, source_target_pairs={{8,0},{16,8},{24,16},{32,24},{40,32},{48,40},{56,48},{64,56},{72,6... | collective-permute-start | bytes 491528 | tf_op jit(solution)/shard_map/ppermute | solution.py:793
